TPU v7x, 32 devices: a whole 2x2x4 slice. The times are simulated.
32 devices in a mesh: seq: 8 (over y, x, core), exp: 4 (over z).
Axes of the slice: x: 2, y: 2, z: 4, core: 2. Of those that a mesh axis runs over, the one named last changes fastest.
Arguments:
- queries: bfloat16 [1024, 2048], P('seq', 'exp'), may hold values from -10 to 10
- key_rows: bfloat16 [1024, 2048], P('seq', 'exp'), may hold values from -10 to 10
- value_rows: bfloat16 [1024, 2048], P('seq', 'exp'), may hold values from -6 to 6
- residual: bfloat16 [1024, 2048], P('seq'), may hold values from -20 to 20
- out_weight: bfloat16 [2048, 2048], P('exp'), may hold values from -1 to 1
- norm_gain: float32 [2048], replicated, may hold values from 0.5 to 1.5
- gate_weight: bfloat16 [16, 2048, 1408], P('seq', None, 'exp'), may hold values from -0.125 to 0.125
- up_weight: bfloat16 [16, 2048, 1408], P('seq', None, 'exp'), may hold values from -0.125 to 0.125
- down_weight: bfloat16 [16, 1408, 2048], P('seq', 'exp'), may hold values from -0.15625 to 0.15625
- routes: int32 [1024, 6], P('seq'), may hold values from 0 to 15, all different within a row; in each aligned block of 128 rows (0 to 127, 128 to 255, ...) at most 96 rows name the same one
- route_gates: float32 [1024, 6], P('seq'), may hold values from 0.2 to 1
- block_picks: int32 [2, 3], replicated, may hold values from 0 to 1, as said below
Outputs:
- layer_out: bfloat16 [1024, 2048], P(('seq', 'exp'))
Inputs may be any that keep to these rules, and one draw needn't show every extreme that they name: `block_picks`: row b names block b first, then blocks at or before b, repeats allowed. `routes`: in each aligned block of 128 rows no expert is named by more than 96 rows, a bound that some block reaches.
All inputs are finite; a program needn't handle non-finite values.
Results may differ from a plain program's by a relative error of at most 0.015.
Values may be sent and summed in bfloat16 or wider, within the bound.
No kernel may reach another device: no remote copies, remote signals or barrier semaphores. Data moves between devices by JAX's collectives and lax.ppermute only.
A program may use at most 64 MiB of HBM per device.

v0:
```python
import jax
import jax.numpy as jnp
from jax import lax
from jax.sharding import PartitionSpec as P

HD = 128
TOPK = 6
BLK = 512


def rms_scale(hidden, norm_gain):
    mean_square = jnp.mean(hidden * hidden, axis=-1, keepdims=True)
    return hidden * lax.rsqrt(mean_square + 1e-06) * norm_gain


def expert_block(arrived, gate_weight, up_weight, down_weight):
    gate_part = jnp.einsum(
        "semd,edf->semf", arrived, gate_weight, preferred_element_type=jnp.float32
    )
    up_part = jnp.einsum("semd,edf->semf", arrived, up_weight, preferred_element_type=jnp.float32)
    inner_act = (jax.nn.silu(gate_part) * up_part).astype(jnp.bfloat16)
    return jnp.einsum(
        "semf,efd->semd", inner_act, down_weight, preferred_element_type=jnp.float32
    ).astype(jnp.bfloat16)


def per_device(
    queries,
    key_rows,
    value_rows,
    residual,
    out_weight,
    norm_gain,
    gate_weight,
    up_weight,
    down_weight,
    routes,
    route_gates,
    block_picks,
):
    seq_count = lax.axis_size("seq")
    exp_count = lax.axis_size("exp")
    seq_index = lax.axis_index("seq")
    exp_index = lax.axis_index("exp")
    tok_rows = queries.shape[0]
    head_count = queries.shape[1] // HD
    nblocks = block_picks.shape[0]
    model_width = residual.shape[1]
    positions = seq_index * tok_rows + jnp.arange(tok_rows, dtype=jnp.int32)
    block_ids = jnp.arange(nblocks, dtype=jnp.int32)
    chosen = jnp.any(block_picks[:, :, None] == block_ids[None, None, :], axis=1).astype(
        jnp.float32
    )
    query_onehot = ((positions // BLK)[:, None] == block_ids[None, :]).astype(jnp.float32)
    query_allowed = jnp.dot(query_onehot, chosen)
    split_queries = queries.reshape(tok_rows, head_count, HD)
    score_scale = HD ** (-0.5)
    run_max = jnp.full((tok_rows, head_count), -1e30, jnp.float32)
    key_piece = lax.all_gather(key_rows, "seq", axis=0, tiled=True)
    value_piece = lax.all_gather(value_rows, "seq", axis=0, tiled=True)
    piece_rows = key_piece.shape[0]
    key_pos = jnp.arange(piece_rows, dtype=jnp.int32)
    key_onehot = ((key_pos // BLK)[:, None] == block_ids[None, :]).astype(jnp.float32)
    allowed = (
        (jnp.dot(query_allowed, key_onehot.T) > 0.5) & (key_pos[None, :] <= positions[:, None])
    )[:, None, :]
    scores = (
        jnp.einsum(
            "qhd,khd->qhk",
            split_queries,
            key_piece.reshape(piece_rows, head_count, HD),
            preferred_element_type=jnp.float32,
        )
        * score_scale
    )
    piece_max = jnp.max(jnp.where(allowed, scores, -1e30), axis=2)
    new_max = jnp.maximum(run_max, piece_max)
    expo = jnp.where(allowed, jnp.exp(scores - new_max[:, :, None]), 0.0)
    new_total = jnp.sum(expo, axis=2)
    mixed_values = jnp.einsum(
        "qhk,khd->qhd",
        expo.astype(jnp.bfloat16),
        value_piece.reshape(piece_rows, head_count, HD),
        preferred_element_type=jnp.float32,
    )
    attended = (
        (mixed_values / new_total[:, :, None])
        .astype(jnp.bfloat16)
        .reshape(tok_rows, head_count * HD)
    )
    proj_part = jnp.dot(attended, out_weight, preferred_element_type=jnp.float32)
    share_rows = tok_rows // exp_count
    projected = lax.psum_scatter(
        proj_part.astype(jnp.bfloat16), "exp", scatter_dimension=0, tiled=True
    ).astype(jnp.float32)
    own_residual = lax.dynamic_slice_in_dim(residual, exp_index * share_rows, share_rows, 0).astype(
        jnp.float32
    )
    own_hidden = own_residual + projected
    own_normed = rms_scale(own_hidden, norm_gain).astype(jnp.bfloat16)
    normed = lax.all_gather(own_normed, "exp", axis=0, tiled=True)
    local_experts = gate_weight.shape[0]
    expert_count = local_experts * seq_count
    slot_most = exp_count * max(1, 2 * tok_rows * TOPK // (expert_count * exp_count))
    slot_total = expert_count * slot_most
    pair_count = tok_rows * TOPK
    flat_routes = routes.reshape(pair_count)
    route_onehot = (
        flat_routes[:, None] == jnp.arange(expert_count, dtype=jnp.int32)[None, :]
    ).astype(jnp.int32)
    slot_rank = jnp.sum((jnp.cumsum(route_onehot, axis=0) - 1) * route_onehot, axis=1)
    slot_ids = flat_routes * slot_most + slot_rank
    sources = (
        jnp.full((slot_total,), pair_count, jnp.int32)
        .at[slot_ids]
        .set(jnp.arange(pair_count, dtype=jnp.int32))
    )
    live_slot = sources < pair_count
    token_ids = jnp.minimum(sources, pair_count - 1) // TOPK
    outgoing = jnp.where(live_slot[:, None], normed[token_ids], jnp.zeros((), jnp.bfloat16))
    outgoing = outgoing.reshape(seq_count, local_experts, slot_most, model_width)
    returned = lax.all_to_all(
        expert_block(
            lax.all_to_all(outgoing, "seq", split_axis=0, concat_axis=0, tiled=True),
            gate_weight,
            up_weight,
            down_weight,
        ),
        "seq",
        split_axis=0,
        concat_axis=0,
        tiled=True,
    )
    back_rows = returned.reshape(slot_total, model_width)[slot_ids].astype(jnp.float32)
    weighted = back_rows.reshape(tok_rows, TOPK, model_width) * route_gates[:, :, None]
    mixture_part = jnp.sum(weighted, axis=1)
    own_mixture = lax.psum_scatter(
        mixture_part.astype(jnp.bfloat16), "exp", scatter_dimension=0, tiled=True
    ).astype(jnp.float32)
    return (own_hidden + own_mixture).astype(jnp.bfloat16)


def solution(mesh):
    placed = (
        P("seq", "exp"),
        P("seq", "exp"),
        P("seq", "exp"),
        P("seq", None),
        P("exp", None),
        P(),
        P("seq", None, "exp"),
        P("seq", None, "exp"),
        P("seq", "exp", None),
        P("seq", None),
        P("seq", None),
        P(),
    )
    return jax.shard_map(
        per_device, mesh=mesh, in_specs=placed, out_specs=P(("seq", "exp"), None), check_vma=False
    )
```

profile of v0, /device:TPU:0, one launch (start us, length us, event | category | flops | bytes accessed | tf_op | source)
XLA Modules:
  0.0 345.7 jit_solution(12460206369254408509)
XLA Ops:
  6.5 0.0 copy-start
  6.5 0.0 all-gather.3.cloned.1.call-start
  6.5 1.8 copy.47
  8.4 0.0 all-gather.3.cloned.1.call-update
  8.4 0.0 all-gather.5.cloned.1.call-start
  8.4 0.7 all-gather.5.cloned.1.call-update
  9.1 0.0 reduce-scatter.3.cloned.1.call-start
  9.2 0.8 fusion.49
  10.0 0.6 fusion.27
  10.5 0.3 copy.46
  10.8 0.8 copy.53
  11.6 0.1 eq.77
  11.8 1.7 reduce-window.6
  13.5 22.0 %all-gather.3.cloned.1.call-done = bf16[1024,512]{0,1:T(8,128)(2,1)} async-done(((bf16[128,512]{0,1:T(8,128)(2,1)}), bf16[1024,512]{0,1:T(8,128)(2,1)}) %all-gather.3.cloned.1.call-update) | async-done | bytes 1048592 | tf_op jit(solution)/shard_map/all_gather | solution.py:59
  35.4 1.9 fusion.11
  37.3 0.0 copy-start.2
  37.3 1.3 copy-done.2
  38.7 0.5 fusion.22
  39.1 21.6 %all-gather.5.cloned.1.call-done = bf16[1024,512]{1,0:T(8,128)(2,1)} async-done(((bf16[128,512]{1,0:T(8,128)(2,1)}), bf16[1024,512]{1,0:T(8,128)(2,1)}) %all-gather.5.cloned.1.call-update) | async-done | bytes 1048592 | tf_op jit(solution)/shard_map/all_gather | solution.py:60
  60.7 2.3 copy.50
  63.0 0.0 copy-start.4
  63.0 2.7 fusion.26
  65.8 0.0 copy-start.6
  65.8 0.0 copy-start.7
  65.8 0.0 copy-done.4
  65.8 1.3 convolution_convert_fusion
  67.1 0.0 reduce-scatter.3.cloned.1.call-update
  67.1 0.2 slice_reduce_fusion
  67.3 0.1 eq.73
  67.5 0.0 copy-done.6
  67.5 0.1 copy.52
  67.6 0.1 mul.75
  67.8 0.1 fusion.40
  67.9 3.4 scatter_custom_fusion
  71.3 0.1 broadcast_in_dim.60
  71.4 17.6 %reduce-scatter.3.cloned.1.call-done = bf16[32,2048]{1,0:T(8,128)(2,1)} async-done(((bf16[128,2048]{1,0:T(8,128)(2,1)}), bf16[32,2048]{1,0:T(8,128)(2,1)}) %reduce-scatter.3.cloned.1.call-update) | async-done | bytes 131088 | tf_op jit(solution)/shard_map/reduce_scatter | solution.py:93
  89.1 1.1 multiply_reduce_fusion.1
  90.2 0.0 copy-done.7
  90.2 1.1 multiply_convert_fusion
  91.3 15.4 %all_gather.11 = bf16[128,2048]{1,0:T(8,128)(2,1)S(1)} all-gather(bf16[32,2048]{1,0:T(8,128)(2,1)S(1)} %multiply_convert_fusion), channel_id=1, replica_groups=mesh['seq'=8,'exp'=4] {'exp'}, dimensions={0}, use_global_device_ids=true | all-gather | bytes 655360 | tf_op jit(solution)/shard_map/all_gather | solution.py:101
  106.6 7.1 %gather_fusion = bf16[1536,2048]{1,0:T(8,128)(2,1)} fusion(bf16[128,2048]{1,0:T(8,128)(2,1)S(1)} %all_gather.11, s32[2048]{0:T(1024)S(1)} %pad_clamp_fusion), kind=kCustom, calls=%fused_computation | custom fusion | bytes 12589056 | tf_op jit(solution)/shard_map/gather | solution.py:120
  113.7 3.3 broadcast_select_fusion
  117.0 0.0 copy-start.9
  117.0 75.3 %all_to_all.10 = bf16[8,2,96,2048]{3,2,1,0:T(8,128)(2,1)S(1)} all-to-all(bf16[8,2,96,2048]{3,2,1,0:T(8,128)(2,1)S(1)} %broadcast_select_fusion), channel_id=1, replica_groups=mesh['seq'=8,'exp'=4] {'seq'}, dimensions={0} | all-to-all | bytes 12582912 | tf_op jit(solution)/shard_map/all_to_all | solution.py:124
  192.4 0.0 copy-start.3
  192.4 2.7 copy-done.3
  195.0 0.0 copy-done.9
  195.0 4.8 %fusion.2 = f32[2,8,96,352]{3,2,1,0:T(8,128)} fusion(bf16[8,2,96,2048]{3,2,1,0:T(8,128)(2,1)S(1)} %all_to_all.10, bf16[2,2048,352]{1,2,0:T(8,128)(2,1)S(1)} %copy-done.9), kind=kOutput, calls=%fused_computation.8 | convolution fusion | flops 2214592512 | bytes 11337728 | tf_op jit(solution)/shard_map/semd,edf->semf/dot_general | solution.py:17
  199.9 0.0 copy-done
  199.9 11.2 %convert_bitcast_fusion = bf16[8,2,96,2048]{3,2,0,1:T(8,128)(2,1)} fusion(bf16[2,352,2048]{2,1,0:T(8,128)(2,1)S(1)} %copy-done, f32[2,8,96,352]{3,2,1,0:T(8,128)} %fusion.2, bf16[2,2048,352]{1,2,0:T(8,128)(2,1)} %param.19, bf16[8,2,96,2048]{3,2,1,0:T(8,128)(2,1)} %copy-done.3), kind=kOutput, calls=%fused_computation.4 | convolution fusion | flops 4435574784 | bytes 20512768 | tf_op jit(solution)/shard_map/semf,efd->semd/dot_general | solution.py:22
  211.1 6.6 %copy.58 = bf16[8,2,96,2048]{3,2,1,0:T(8,128)(2,1)} copy(bf16[8,2,96,2048]{3,2,0,1:T(8,128)(2,1)} %convert_bitcast_fusion) | data formatting | bytes 12582912 | tf_op jit(solution)/shard_map/convert_element_type | solution.py:24
  217.7 4.9 %all-to-all-start.1 = ((bf16[8,2,96,2048]{3,2,1,0:T(8,128)(2,1)}), bf16[8,2,96,2048]{3,2,1,0:T(8,128)(2,1)}, u32[]{:S(2)}, u32[]{:S(2)}) async-start(bf16[8,2,96,2048]{3,2,1,0:T(8,128)(2,1)} %copy.58), calls=%async_computation.2 | async-start | bytes 12582912 | tf_op jit(solution)/shard_map/all_to_all | solution.py:122
  222.6 0.3 reduce-scatter.5.cloned.1.call-start
  222.8 0.0 copy-done.8
  222.8 0.1 copy.59
  223.0 71.2 %all-to-all-done.1 = bf16[8,2,96,2048]{3,2,1,0:T(8,128)(2,1)} async-done(((bf16[8,2,96,2048]{3,2,1,0:T(8,128)(2,1)}), bf16[8,2,96,2048]{3,2,1,0:T(8,128)(2,1)}, u32[]{:S(2)}, u32[]{:S(2)}) %all-to-all-start.1) | async-done | bytes 6291488 | tf_op jit(solution)/shard_map/all_to_all | solution.py:122
  294.1 10.7 %gather_fusion.1 = bf16[768,2048]{1,0:T(8,128)(2,1)} fusion(bf16[1536,2048]{1,0:T(8,128)(2,1)} %bitcast.16, s32[1024]{0:T(1024)S(1)} %pad_clamp_fusion.1), kind=kCustom, calls=%fused_computation.1 | custom fusion | bytes 6294528 | tf_op jit(solution)/shard_map/gather | solution.py:134
  304.8 6.7 %reshape.131 = f32[128,6,2048]{2,1,0:T(8,128)} reshape(bf16[768,2048]{1,0:T(8,128)(2,1)} %gather_fusion.1) | data formatting | bytes 9437184 | tf_op jit(solution)/shard_map/convert_element_type | solution.py:134
  311.5 7.4 %multiply_reduce_fusion = bf16[128,2048]{1,0:T(8,128)(2,1)} fusion(f32[128,6,2048]{2,1,0:T(8,128)} %reshape.131, f32[128,6]{1,0:T(8,128)S(1)} %copy.59), kind=kLoop, calls=%fused_computation.3 | loop fusion | flops 2883584 | bytes 6818816 | tf_op jit(solution)/shard_map/reduce_sum | solution.py:136
  319.0 0.0 reduce-scatter.5.cloned.1.call-update
  319.0 18.5 %reduce-scatter.5.cloned.1.call-done = bf16[32,2048]{1,0:T(8,128)(2,1)} async-done(((bf16[128,2048]{1,0:T(8,128)(2,1)}), bf16[32,2048]{1,0:T(8,128)(2,1)}) %reduce-scatter.5.cloned.1.call-update) | async-done | bytes 131088 | tf_op jit(solution)/shard_map/reduce_scatter | solution.py:137
  337.5 0.0 copy-done.5
  337.5 1.7 add_convert_fusion
  339.2 0.0 copy-done.1
  (16 shorter events, 0.1 us)
Async XLA Ops:
  6.5 193.3 %copy-start = (bf16[2,352,2048]{2,1,0:T(8,128)(2,1)S(1)}, bf16[2,352,2048]{2,1,0:T(8,128)(2,1)}, u32[]{:S(2)}) copy-start(bf16[2,352,2048]{2,1,0:T(8,128)(2,1)} %param.20) | copy-start | bytes 8650756
  6.5 28.9 %all-gather.3.cloned.1.call-start = ((), (), s32[]{:S(2)}) async-start(), calls=%async_computation.4 | async-start | bytes 1179648 | tf_op jit(solution)/shard_map/all_gather | solution.py:59
  8.4 52.4 %all-gather.5.cloned.1.call-start = ((), (), s32[]{:S(2)}) async-start(), calls=%async_computation.5 | async-start | bytes 1179648 | tf_op jit(solution)/shard_map/all_gather | solution.py:60
  9.1 79.9 %reduce-scatter.3.cloned.1.call-start = ((), (), s32[]{:S(2)}) async-start(), calls=%async_computation.6 | async-start | bytes 655360 | tf_op jit(solution)/shard_map/reduce_scatter | solution.py:93
  37.3 1.4 copy-start.2
  63.0 2.8 copy-start.4
  65.8 1.7 copy-start.6
  65.8 24.4 %copy-start.7 = (f32[2048]{0:T(1024)S(1)}, f32[2048]{0:T(1024)}, u32[]{:S(2)}) copy-start(f32[2048]{0:T(1024)} %param.17) | copy-start | bytes 24580
  117.0 78.0 %copy-start.9 = (bf16[2,2048,352]{1,2,0:T(8,128)(2,1)S(1)}, bf16[2,2048,352]{1,2,0:T(8,128)(2,1)}, u32[]{:S(2)}) copy-start(bf16[2,2048,352]{1,2,0:T(8,128)(2,1)} %param.18) | copy-start | bytes 8650756
  192.4 2.7 copy-start.3
  217.7 5.2 %copy-start.8 = (f32[128,6]{0,1:T(8,128)S(1)}, f32[128,6]{0,1:T(8,128)}, u32[]{:S(2)}) copy-start(f32[128,6]{0,1:T(8,128)} %param.22) | copy-start | bytes 9220
  217.7 76.4 %all-to-all-start.1 = ((bf16[8,2,96,2048]{3,2,1,0:T(8,128)(2,1)}), bf16[8,2,96,2048]{3,2,1,0:T(8,128)(2,1)}, u32[]{:S(2)}, u32[]{:S(2)}) async-start(bf16[8,2,96,2048]{3,2,1,0:T(8,128)(2,1)} %copy.58), calls=%async_computation.2 | async-start | bytes 12582912 | tf_op jit(solution)/shard_map/all_to_all | solution.py:122
  222.6 115.0 %reduce-scatter.5.cloned.1.call-start = ((), (), s32[]{:S(2)}) async-start(), calls=%async_computation.7 | async-start | bytes 655360 | tf_op jit(solution)/shard_map/reduce_scatter | solution.py:137
  304.8 34.4 %copy-start.1 = (bf16[2,352,2048]{2,1,0:T(8,128)(2,1)S(1)}, bf16[2,352,2048]{2,1,0:T(8,128)(2,1)}, u32[]{:S(2)}) copy-start(bf16[2,352,2048]{2,1,0:T(8,128)(2,1)} %param.20) | copy-start | bytes 8650756
  311.5 26.0 %copy-start.5 = (bf16[32,2048]{1,0:T(8,128)(2,1)S(1)}, bf16[32,2048]{1,0:T(8,128)(2,1)}, u32[]{:S(2)}) copy-start(bf16[32,2048]{1,0:T(8,128)(2,1)} %reduce-scatter.3.cloned.1.call-done) | copy-start | bytes 393220
Sparse Core Ops, SparseCore 0:
  9.2 26.1 all-gather.2
  37.3 23.3 all-gather.4
  67.2 21.8 reduce-scatter.2
  319.1 18.3 reduce-scatter.4
where the time goes:
time: 346 us
  waiting for transfers between devices  152 us (44%)
  blocking collectives  90.7 us (26%)
  local copies, waits for them, and re-layouts  44.6 us (13%)
  matrix products  22.5 us (7%)
  other arithmetic  17.8 us (5%)
  between operations  13.3 us (4%)
  starting transfers between devices  5.21 us (2%)
    all_to_all x1, blocking collectives, per_device(): lax.all_to_all(outgoing, 'seq', split_axis=0, concat_axis=0, tiled=True)  75.3 us
    all_to_all x1, waiting for transfers between devices, per_device(): lax.all_to_all(expert_block(lax.all_to_all(outgoing, 'seq', split_axis=0,...  71.2 us
    all_gather x1, waiting for transfers between devices, per_device(): key_piece = lax.all_gather(key_rows, 'seq', axis=0, tiled=True)  22 us
    all_gather x1, waiting for transfers between devices, per_device(): value_piece = lax.all_gather(value_rows, 'seq', axis=0, tiled=True)  21.6 us
    reduce_scatter x1, waiting for transfers between devices, per_device(): lax.psum_scatter(mixture_part.astype(jnp.bfloat16), 'exp', scatter_dimens...  18.5 us
    reduce_scatter x1, waiting for transfers between devices, per_device(): lax.psum_scatter(proj_part.astype(jnp.bfloat16), 'exp', scatter_dimension...  17.6 us
    all_gather x1, blocking collectives, per_device(): normed = lax.all_gather(own_normed, 'exp', axis=0, tiled=True)  15.4 us
    dot_general x1, matrix products, expert_block(): jnp.einsum('semf,efd->semd', inner_act, down_weight, preferred_element_ty...  11.2 us
  transfers between devices with their start and end apart: 5, of which 5 were waited for; matrix products, arithmetic and copies ran while one was open for 3% of the time, Pallas kernels for 0%

commit v1 on v0

v1 whole, which is shorter than its diff:
```python
import functools

import jax
import jax.numpy as jnp
from jax import lax
from jax.experimental import pallas as pl
from jax.experimental.pallas import tpu as pltpu
from jax.sharding import PartitionSpec as P


HD = 128
BLK = 512
LANES = 128
MIB = 1 << 20
VMEM = pltpu.MemorySpace.VMEM
SMEM = pltpu.MemorySpace.SMEM
HBM = pltpu.MemorySpace.HBM


def call(kernel, out_shape, in_spaces, limit, scratch=()):
    specs = [pl.BlockSpec(memory_space=s) for s in in_spaces]
    return pl.pallas_call(
        kernel,
        out_shape=out_shape,
        in_specs=specs,
        out_specs=jax.tree.map(lambda _: pl.BlockSpec(memory_space=VMEM), out_shape),
        scratch_shapes=list(scratch),
        compiler_params=pltpu.CompilerParams(vmem_limit_bytes=limit * MIB),
    )


def xor_swap(count, mask):
    return [(i, i ^ mask) for i in range(count)]


def load_kernel(seq_count, exp_count, expert_count, picks_ref, routes_ref, gates_ref, *refs):
    copied = (len(refs) - 4) // 2
    sources, targets = refs[:copied], refs[copied : 2 * copied]
    key_out, gates_out, turned, sems = refs[2 * copied :]
    seq_index, exp_index = lax.axis_index("seq"), lax.axis_index("exp")
    top, rows = routes_ref.shape
    share = rows // exp_count
    here = pl.ds(pl.multiple_of(exp_index * share, share), share)
    copies = []
    for i in range(copied):
        source = sources[i].at[here] if i == 0 else sources[i]
        copies.append(pltpu.make_async_copy(source, targets[i], sems.at[i]))
        copies[-1].start()

    block = seq_index * rows // BLK
    lane = lax.broadcasted_iota(jnp.int32, (1, rows), 1)
    for mask in range(seq_count):
        group = seq_index ^ mask
        key_block = group * rows // BLK
        seen = picks_ref[block, 0] == key_block
        for j in range(1, picks_ref.shape[1]):
            seen = seen | (picks_ref[block, j] == key_block)
        key_out[:, mask * rows : (mask + 1) * rows] = lane + jnp.where(seen, group * rows, 1 << 30)

    width = gates_out.shape[1]
    line = lax.broadcasted_iota(jnp.int32, (width, rows), 0)
    expert = jnp.where(line < expert_count, line, line - expert_count)
    value = jnp.zeros((width, rows), jnp.float32)
    for k in range(top):
        hit = expert == routes_ref[k : k + 1, :]
        value = value + jnp.where(hit, gates_ref[k : k + 1, :], 0.0)
    high = value.astype(jnp.bfloat16).astype(jnp.float32)
    turned[...] = jnp.where(line < expert_count, high, value - high).T
    gates_out[...] = turned[here, :].astype(jnp.bfloat16)
    for copy in copies:
        copy.wait()


def attention_kernel(count, key_ref, own_ref, *refs):
    pieces, (own_out, partner_out) = refs[:count], refs[count:]
    seq_index = lax.axis_index("seq")
    rows, width = own_ref.shape
    key_pos = key_ref[...]
    line = lax.broadcasted_iota(jnp.int32, (rows, 1), 0)
    query_pos = jnp.concatenate(
        [line + seq_index * rows, line + (seq_index ^ 1) * rows], axis=0
    )
    allowed = key_pos <= query_pos
    for first in range(0, width, HD):
        q = jnp.concatenate(
            [
                own_ref[:, first : first + HD],
                pieces[1][:, 2 * width + first : 2 * width + first + HD],
            ],
            axis=0,
        )
        k = jnp.concatenate([p[:, first : first + HD] for p in pieces], axis=0)
        v = jnp.concatenate(
            [p[:, width + first : width + first + HD] for p in pieces], axis=0
        )
        scores = lax.dot_general(
            q, k, (((1,), (1,)), ((), ())), preferred_element_type=jnp.float32
        ) * (HD ** -0.5)
        scores = jnp.where(allowed, scores, -1e30)
        peak = jnp.max(scores, axis=1, keepdims=True)
        expo = jnp.where(allowed, jnp.exp(scores - peak), 0.0)
        total = jnp.sum(expo, axis=1, keepdims=True)
        mixed = jnp.dot(expo.astype(jnp.bfloat16), v, preferred_element_type=jnp.float32) / total
        mixed = mixed.astype(jnp.bfloat16)
        own_out[:, first : first + HD] = mixed[:rows]
        partner_out[:, first : first + HD] = mixed[rows:]


def project_kernel(exp_count, mine_ref, other_ref, weight_ref, own_out, *outs):
    rows, width = mine_ref.shape
    share = rows // exp_count
    exp_index = lax.axis_index("exp")
    half = lax.axis_index("seq") & 1

    def turned(ref):
        parts = []
        for r in range(exp_count):
            first = pl.multiple_of((exp_index ^ r) * share, share)
            parts.append(ref[pl.ds(first, share), :])
        return jnp.concatenate(parts, axis=0)

    first = pl.multiple_of(half * width, width)
    last = pl.multiple_of((1 - half) * width, width)
    result = jnp.dot(
        turned(mine_ref), weight_ref[pl.ds(first, width), :], preferred_element_type=jnp.float32
    ) + jnp.dot(
        turned(other_ref), weight_ref[pl.ds(last, width), :], preferred_element_type=jnp.float32
    )
    own_out[...] = result[:share]
    for r in range(1, exp_count):
        outs[r - 1][...] = result[r * share : (r + 1) * share].astype(jnp.bfloat16)


def norm_kernel(exp_count, own_ref, *refs):
    received = refs[: exp_count - 1]
    residual_ref, gain_ref, gates_ref, hidden_out, rows_out = refs[exp_count - 1 :]
    width = own_ref.shape[1]
    projected = own_ref[...]
    for r in received:
        projected = projected + r[...].astype(jnp.float32)
    hidden = residual_ref[...].astype(jnp.float32) + projected
    mean_square = jnp.mean(hidden * hidden, axis=-1, keepdims=True)
    hidden_out[...] = hidden
    rows_out[:, :width] = (hidden * lax.rsqrt(mean_square + 1e-06) * gain_ref[...]).astype(
        jnp.bfloat16
    )
    rows_out[:, width:] = gates_ref[...]


def expert_kernel(expert_count, local, arrays, *refs):
    pieces = refs[:arrays]
    gate_ref, up_ref, down_ref = refs[arrays : arrays + 3]
    outs = refs[arrays + 3 :]
    rows = pieces[0].shape[1]
    inner_width, width = down_ref.shape
    hidden_units = inner_width // local
    places = [(p, i) for p in pieces for i in range(p.shape[0])]
    tokens = jnp.concatenate([p[i, :, :width] for p, i in places], axis=0)
    gates = jnp.concatenate([p[i, :, width:] for p, i in places], axis=0)
    gates = gates.astype(jnp.float32)
    line = lax.broadcasted_iota(jnp.int32, (1, gates.shape[1]), 1)
    column = lax.broadcasted_iota(jnp.int32, (1, inner_width), 1)
    scale = jnp.zeros((gates.shape[0], inner_width), jnp.float32)
    for e in range(local):
        expert = lax.axis_index("seq") * local + e
        chosen = (line == expert) | (line == expert + expert_count)
        value = jnp.sum(jnp.where(chosen, gates, 0.0), axis=1, keepdims=True)
        here = (column >= e * hidden_units) & (column < (e + 1) * hidden_units)
        scale = jnp.where(here, value, scale)
    turn = (((1,), (1,)), ((), ()))
    gate = lax.dot_general(tokens, gate_ref[...], turn, preferred_element_type=jnp.float32)
    up = lax.dot_general(tokens, up_ref[...], turn, preferred_element_type=jnp.float32)
    inner = (gate / (1.0 + jnp.exp(-gate)) * up * scale).astype(jnp.bfloat16)
    result = jnp.dot(inner, down_ref[...], preferred_element_type=jnp.float32)
    at = 0
    for out in outs:
        for i in range(out.shape[0]):
            out[i] = result[at : at + rows].astype(jnp.bfloat16)
            at += rows


def join_kernel(a_ref, b_ref, out_ref):
    out_ref[: a_ref.shape[0]] = a_ref[...]
    out_ref[a_ref.shape[0] :] = b_ref[...]


def join(a, b):
    shape = jax.ShapeDtypeStruct((a.shape[0] + b.shape[0],) + a.shape[1:], a.dtype)
    return call(join_kernel, shape, [VMEM] * 2, 8)(a, b)


def plus_kernel(a_ref, b_ref, *outs):
    at = 0
    for out in outs:
        part = slice(at, at + out.shape[0])
        at += out.shape[0]
        out[...] = (a_ref[part].astype(jnp.float32) + b_ref[part].astype(jnp.float32)).astype(
            out.dtype
        )


def plus(a, b, parts=1):
    shape = jax.ShapeDtypeStruct((a.shape[0] // parts,) + a.shape[1:], a.dtype)
    return call(plus_kernel, (shape,) * parts, [VMEM] * 2, 8)(a, b)


def per_device(
    queries,
    key_rows,
    value_rows,
    residual,
    out_weight,
    norm_gain,
    gate_weight,
    up_weight,
    down_weight,
    routes,
    route_gates,
    block_picks,
):
    seq_count = lax.axis_size("seq")
    exp_count = lax.axis_size("exp")
    seq_index = lax.axis_index("seq")
    tok_rows, head_width = queries.shape
    width = residual.shape[1]
    share = tok_rows // exp_count
    local, _, hidden_units = gate_weight.shape
    expert_count = local * seq_count
    half_width = head_width // 2
    core = seq_index & 1
    bf16, f32 = jnp.bfloat16, jnp.float32

    def seq_send(a, mask):
        return lax.ppermute(a, "seq", xor_swap(seq_count, mask))

    def exp_send(a, by):
        return lax.ppermute(a, "exp", xor_swap(exp_count, by))

    def half_of(a, which):
        return lax.dynamic_slice_in_dim(a, which * half_width, half_width, 1)

    kv_same = jnp.concatenate([half_of(key_rows, core), half_of(value_rows, core)], axis=1)
    other = [half_of(a, 1 - core) for a in (key_rows, value_rows, queries)]
    kv_other = jnp.concatenate(other[:2], axis=1)
    pieces = [kv_same] + [None] * (seq_count - 1)
    for mask in range(seq_count - 1, 1, -1):
        pieces[mask] = seq_send(kv_other if mask & 1 else kv_same, mask)
    pieces[1] = seq_send(jnp.concatenate(other, axis=1), 1)

    gate_columns = -(-2 * expert_count // LANES) * LANES
    loaded = [
        residual,
        norm_gain[None, :],
        out_weight,
        gate_weight.transpose(0, 2, 1).reshape(local * hidden_units, width),
        up_weight.transpose(0, 2, 1).reshape(local * hidden_units, width),
        down_weight.reshape(local * hidden_units, width),
    ]
    shapes = [jax.ShapeDtypeStruct(a.shape, a.dtype) for a in loaded]
    shapes[0] = jax.ShapeDtypeStruct((share, width), residual.dtype)
    shapes.append(jax.ShapeDtypeStruct((1, seq_count * tok_rows), jnp.int32))
    shapes.append(jax.ShapeDtypeStruct((share, gate_columns), bf16))
    residual_rows, gain, out_proj, gate_t, up_t, down, key_pos, gates = call(
        functools.partial(load_kernel, seq_count, exp_count, expert_count),
        tuple(shapes),
        [SMEM, VMEM, VMEM] + [HBM] * len(loaded),
        24,
        [
            pltpu.VMEM((tok_rows, gate_columns), f32),
            pltpu.SemaphoreType.DMA((len(loaded),)),
        ],
    )(block_picks, routes.T, route_gates.T, *[pltpu.with_memory_space_constraint(a, HBM) for a in loaded])

    half_shape = jax.ShapeDtypeStruct((tok_rows, half_width), bf16)
    attended, partner_attended = call(
        functools.partial(attention_kernel, seq_count),
        (half_shape, half_shape),
        [VMEM] * (2 + seq_count),
        32,
    )(key_pos, half_of(queries, core), *pieces)
    other_attended = seq_send(partner_attended, 1)

    projected = call(
        functools.partial(project_kernel, exp_count),
        (jax.ShapeDtypeStruct((share, width), f32),)
        + (jax.ShapeDtypeStruct((share, width), bf16),) * (exp_count - 1),
        [VMEM] * 3,
        16,
    )(attended, other_attended, out_proj)
    received = [exp_send(projected[r], r) for r in range(1, exp_count)]

    hidden, own_rows = call(
        functools.partial(norm_kernel, exp_count),
        (
            jax.ShapeDtypeStruct((share, width), f32),
            jax.ShapeDtypeStruct((share, width + gate_columns), bf16),
        ),
        [VMEM] * (exp_count + 3),
        8,
    )(projected[0], *received, residual_rows, gain, gates)

    far = [1 << b for b in range(1, (seq_count - 1).bit_length())]
    turned = far[len(far) // 2 :] + far[: len(far) // 2]

    def lane_send(a, step):
        pairs = [(i, i ^ (turned[step] if i & 1 else far[step])) for i in range(seq_count)]
        return lax.ppermute(a, "seq", pairs)

    def lane_exp_send(a, even, odd):
        pairs = [
            (i * exp_count + j, i * exp_count + (j ^ (odd if i & 1 else even)))
            for i in range(seq_count)
            for j in range(exp_count)
        ]
        return lax.ppermute(a, ("seq", "exp"), pairs)

    def mlp(arrays):
        outs = call(
            functools.partial(expert_kernel, expert_count, local, len(arrays)),
            tuple(jax.ShapeDtypeStruct(a.shape[:2] + (width,), bf16) for a in arrays),
            [VMEM] * (len(arrays) + 3),
            32,
        )(*arrays, gate_t, up_t, down)
        return list(outs)

    if exp_count == 4:
        groups = [(0, 0), (1, 2), (3, 3)]
    else:
        groups = [(r, r) for r in range(exp_count)]
    own_rows = own_rows[None]
    bases = []
    for even, odd in groups:
        base = own_rows
        if even != odd:
            base = join(own_rows, seq_send(own_rows, 1))
        bases.append(lane_exp_send(base, even, odd) if even or odd else base)
    mixture = 0.0
    for at, (even, odd) in enumerate(groups):
        whole = bases[at]
        for step in range(len(far)):
            arrived = lane_send(whole, step)
            if step + 1 < len(far):
                whole = join(whole, arrived)
        mine = [whole, arrived]
        other = [seq_send(a, 1) for a in mine]
        if even != odd:
            sums = mlp(other)
            parts = [seq_send(sums[i], 1) for i in (1, 0)][::-1]
            sums = mlp(mine)
        else:
            sums = mlp(other + mine)
            parts = [seq_send(sums[i], 1) for i in (1, 0)][::-1]
            sums = sums[2:]
        (sent,) = plus(sums[1], parts[1])
        (kept,) = plus(sums[0], parts[0])
        for step in reversed(range(len(far))):
            arrived = lane_send(sent, step)
            if step:
                kept, sent = plus(kept, arrived, 2)
            else:
                (kept,) = plus(kept, arrived)
        if even or odd:
            kept = lane_exp_send(kept, even, odd)
        mixture = mixture + kept[0].astype(f32)
        if even != odd:
            mixture = mixture + seq_send(kept[1], 1).astype(f32)
    return (hidden + mixture).astype(bf16)


def solution(mesh):
    placed = (
        P("seq", "exp"),
        P("seq", "exp"),
        P("seq", "exp"),
        P("seq", None),
        P("exp", None),
        P(),
        P("seq", None, "exp"),
        P("seq", None, "exp"),
        P("seq", "exp", None),
        P("seq", None),
        P("seq", None),
        P(),
    )

    return jax.shard_map(
        per_device, mesh=mesh, in_specs=placed, out_specs=P(("seq", "exp"), None), check_vma=False
    )
```

time: 346 us -> 124 us (0.36)
  waiting for transfers between devices: 152 us -> 60.2 us
  blocking collectives: 90.7 us -> 0 us
  local copies, waits for them, and re-layouts: 44.6 us -> 3.9 us
  starting transfers between devices: 5.21 us -> 40.3 us
  matrix products: 22.5 us -> 0 us
  Pallas kernels: 0 us -> 18.7 us
  other arithmetic: 17.8 us -> 0.77 us
  between operations: 13.3 us -> 0.32 us
    all_to_all x1 -> x0, blocking collectives: 75.3 us -> none  [per_device(): lax.all_to_all(outgoing, 'seq', split_axis=0, concat_axis=0, tiled=True)]
    all_to_all x1 -> x0, waiting for transfers between devices: 71.2 us -> none  [per_device(): lax.all_to_all(expert_block(lax.all_to_all(outgoing, 'seq', split_axis=0,...]
    ppermute x0 -> x41, waiting for transfers between devices: none -> 60.2 us  [the longest x12 27.8 us: lane_send(): return lax.ppermute(a, 'seq', pairs)]
    all_gather x2 -> x0, waiting for transfers between devices: 43.6 us -> none  [the longest x1 22 us: per_device(): key_piece = lax.all_gather(key_rows, 'seq', axis=0, tiled=True)]
    ppermute x0 -> x41, starting transfers between devices: none -> 40.3 us  [the longest x12 12.8 us: lane_send(): return lax.ppermute(a, 'seq', pairs)]
    reduce_scatter x2 -> x0, waiting for transfers between devices: 36.2 us -> none  [the longest x1 18.5 us: per_device(): lax.psum_scatter(mixture_part.astype(jnp.bfloat16), 'exp', scatter_dimens...]
    dot_general x6 -> x0, matrix products: 22.5 us -> none  [the longest x1 11.2 us: expert_block(): jnp.einsum('semf,efd->semd', inner_act, down_weight, preferred_element_ty...]
    pallas_call x0 -> x24, Pallas kernels: none -> 18.7 us  [the longest x4 10.8 us: mlp(): call(functools.partial(expert_kernel, expert_count, local, len(arrays)),...]
  transfers between devices with their start and end apart: 5 -> 41, of which waited for: 5 -> 16; matrix products, arithmetic and copies ran while one was open for 3% -> 1% of each run, Pallas kernels for 0% -> 11%
where the time goes in v1:
time: 124 us
  waiting for transfers between devices  60.2 us (49%)
  starting transfers between devices  40.3 us (32%)
  Pallas kernels  18.7 us (15%)
  local copies, waits for them, and re-layouts  3.9 us (3%)
    ppermute x12, waiting for transfers between devices, lane_send(): return lax.ppermute(a, 'seq', pairs)  27.8 us
    ppermute x4, waiting for transfers between devices, lane_exp_send(): return lax.ppermute(a, ('seq', 'exp'), pairs)  17.1 us
    ppermute x12, starting transfers between devices, lane_send(): return lax.ppermute(a, 'seq', pairs)  12.8 us
    ppermute x22, starting transfers between devices, seq_send(): return lax.ppermute(a, 'seq', xor_swap(seq_count, mask))  12.6 us
    pallas_call x4, Pallas kernels, mlp(): call(functools.partial(expert_kernel, expert_count, local, len(arrays)),...  10.8 us
    ppermute x4, starting transfers between devices, lane_exp_send(): return lax.ppermute(a, ('seq', 'exp'), pairs)  10.5 us
    ppermute x3, waiting for transfers between devices, exp_send(): return lax.ppermute(a, 'exp', xor_swap(exp_count, by))  10.1 us
    ppermute x22, waiting for transfers between devices, seq_send(): return lax.ppermute(a, 'seq', xor_swap(seq_count, mask))  5.29 us
  transfers between devices with their start and end apart: 41, of which 16 were waited for; matrix products, arithmetic and copies ran while one was open for 1% of the time, Pallas kernels for 11%

profile of v1, /device:TPU:0, one launch (start us, length us, event | category | flops | bytes accessed | tf_op | source)
XLA Modules:
  0.0 124.2 jit_solution(12010693820666195963)
XLA Ops:
  0.0 1.0 constant_dynamic-slice_fusion.1
  1.0 3.0 %collective-permute-start.1 = (bf16[128,512]{1,0:T(8,128)(2,1)S(1)}, bf16[128,512]{1,0:T(8,128)(2,1)S(1)}, u32[]{:S(2)}, u32[]{:S(2)}) collective-permute-start(bf16[128,512]{1,0:T(8,128)(2,1)S(1)} %pad_maximum_fusion.1.refs_0_), channel_id=1, source_target_pairs={{0,8},{4,12},{8,0},{12,4},{16,24},{20,28},{24,16},{28,20},{1,9},{5... | collective-permute-start | bytes 393224 | tf_op jit(solution)/shard_map/ppermute | solution.py:234
  4.0 0.1 collective-permute-start.2
  4.1 0.9 constant_dynamic-slice_fusion
  5.0 0.2 collective-permute-start
  5.2 2.0 %collective-permute-start.3 = (bf16[128,512]{1,0:T(8,128)(2,1)S(1)}, bf16[128,512]{1,0:T(8,128)(2,1)S(1)}, u32[]{:S(2)}, u32[]{:S(2)}) collective-permute-start(bf16[128,512]{1,0:T(8,128)(2,1)S(1)} %pad_maximum_fusion.1.refs_0_), channel_id=1, source_target_pairs={{0,16},{4,20},{8,24},{12,28},{16,0},{20,4},{24,8},{28,12},{1,17},{... | collective-permute-start | bytes 393224 | tf_op jit(solution)/shard_map/ppermute | solution.py:234
  7.2 0.7 collective-permute-done.1.refs_2_
  7.9 3.4 %collective-permute-start.5 = (bf16[128,512]{1,0:T(8,128)(2,1)S(1)}, bf16[128,512]{1,0:T(8,128)(2,1)S(1)}, u32[]{:S(2)}, u32[]{:S(2)}) collective-permute-start(bf16[128,512]{1,0:T(8,128)(2,1)S(1)} %pad_maximum_fusion.1.refs_0_), channel_id=1, source_target_pairs={{0,24},{4,28},{8,16},{12,20},{16,8},{20,12},{24,0},{28,4},{1,25},{... | collective-permute-start | bytes 393224 | tf_op jit(solution)/shard_map/ppermute | solution.py:234
  11.3 1.6 %collective-permute-start.6 = (bf16[128,512]{1,0:T(8,128)(2,1)S(1)}, bf16[128,512]{1,0:T(8,128)(2,1)S(1)}, u32[]{:S(2)}, u32[]{:S(2)}) collective-permute-start(bf16[128,512]{1,0:T(8,128)(2,1)S(1)} %pad_maximum_fusion.2), channel_id=1, source_target_pairs={{0,28},{4,24},{8,20},{12,16},{16,12},{20,8},{24,4},{28,0},{1,29},{... | collective-permute-start | bytes 393224 | tf_op jit(solution)/shard_map/ppermute | solution.py:234
  12.9 0.7 copy-done
  13.6 0.7 copy-done.1
  14.3 0.7 copy-done.2
  15.0 4.9 %shard_map.118 = (bf16[32,2048]{1,0:T(8,128)(2,1)S(1)}, f32[1,2048]{1,0:T(1,128)S(1)}, bf16[512,2048]{1,0:T(8,128)(2,1)S(1)}, bf16[704,2048]{1,0:T(8,128)(2,1)S(...) custom-call(s32[2,3]{1,0:T(2,128)S(1)} %copy-done.2, ...), custom_call_target="tpu_custom_call" | custom-call | tf_op jit(solution)/shard_map/pallas_call | solution.py:263
  19.9 1.4 %shard_map.119 = (bf16[128,256]{1,0:T(8,128)(2,1)S(1)}, bf16[128,256]{1,0:T(8,128)(2,1)S(1)}) custom-call(s32[1,1024]{1,0:T(1,128)S(1)} %get-tuple-element.39.key_ref, bf16[128,256]{1,0:T(8,128)(2,1)S(1)} %get-tuple-element.78.own_ref, bf16[128,512]{1,0:T(8,128)(2,1)S(1)} %pad_maximum_fusion.1.refs_0_, bf16[128,768]{1,0:T(8,128)(2,1)S(1)} %collective-permute-done.refs_1_, ...), custom_call_target="tpu_custom_call" | custom-call | tf_op jit(solution)/shard_map/pallas_call | solution.py:275
  21.4 1.2 collective-permute-done.7.other_ref
  22.6 0.5 shard_map.120
  23.1 1.6 %collective-permute-start.8 = (bf16[32,2048]{1,0:T(8,128)(2,1)S(1)}, bf16[32,2048]{1,0:T(8,128)(2,1)S(1)}, u32[]{:S(2)}, u32[]{:S(2)}) collective-permute-start(bf16[32,2048]{1,0:T(8,128)(2,1)S(1)} %get-tuple-element.44), channel_id=1, source_target_pairs={{0,1},{1,0},{2,3},{3,2},{4,5},{5,4},{6,7},{7,6},{8,9},{9,8},{10,11... | collective-permute-start | bytes 393224 | tf_op jit(solution)/shard_map/ppermute | solution.py:237
  24.7 2.6 %collective-permute-start.9 = (bf16[32,2048]{1,0:T(8,128)(2,1)S(1)}, bf16[32,2048]{1,0:T(8,128)(2,1)S(1)}, u32[]{:S(2)}, u32[]{:S(2)}) collective-permute-start(bf16[32,2048]{1,0:T(8,128)(2,1)S(1)} %get-tuple-element.45), channel_id=1, source_target_pairs={{0,2},{1,3},{2,0},{3,1},{4,6},{5,7},{6,4},{7,5},{8,10},{9,11},{10,... | collective-permute-start | bytes 393224 | tf_op jit(solution)/shard_map/ppermute | solution.py:237
  27.3 0.2 collective-permute-start.10
  27.6 3.1 %collective-permute-done.8.refs_0_ = bf16[32,2048]{1,0:T(8,128)(2,1)S(1)} collective-permute-done((bf16[32,2048]{1,0:T(8,128)(2,1)S(1)}, bf16[32,2048]{1,0:T(8,128)(2,1)S(1)}, u32[]{:S(2)}, u32[]{:S(2)}) %collective-permute-start.8) | collective-permute-done | bytes 131104 | tf_op jit(solution)/shard_map/ppermute | solution.py:237
  30.7 6.9 %collective-permute-done.9.refs_1_ = bf16[32,2048]{1,0:T(8,128)(2,1)S(1)} collective-permute-done((bf16[32,2048]{1,0:T(8,128)(2,1)S(1)}, bf16[32,2048]{1,0:T(8,128)(2,1)S(1)}, u32[]{:S(2)}, u32[]{:S(2)}) %collective-permute-start.9) | collective-permute-done | bytes 131104 | tf_op jit(solution)/shard_map/ppermute | solution.py:237
  37.6 0.2 shard_map.121
  37.9 1.3 %collective-permute-done.19.b_ref = bf16[1,32,2176]{2,1,0:T(8,128)(2,1)S(1)} collective-permute-done((bf16[1,32,2176]{2,1,0:T(8,128)(2,1)S(1)}, bf16[1,32,2176]{2,1,0:T(8,128)(2,1)S(1)}, u32[]{:S(2)}, u32[]{:S(2)}) %collective-permute-start.19) | collective-permute-done | bytes 139296 | tf_op jit(solution)/shard_map/ppermute | solution.py:234
  39.2 2.4 %collective-permute-start.20 = (bf16[2,32,2176]{2,1,0:T(8,128)(2,1)S(1)}, bf16[2,32,2176]{2,1,0:T(8,128)(2,1)S(1)}, u32[]{:S(2)}, u32[]{:S(2)}) collective-permute-start(bf16[2,32,2176]{2,1,0:T(8,128)(2,1)S(1)} %shard_map.128), channel_id=1, source_target_pairs={{0,1},{1,0},{2,3},{3,2},{4,6},{5,7},{6,4},{7,5},{8,9},{9,8},{10,11... | collective-permute-start | bytes 835592 | tf_op jit(solution)/shard_map/ppermute | solution.py:315
  41.6 7.1 %collective-permute-done.20.a_ref = bf16[2,32,2176]{2,1,0:T(8,128)(2,1)S(1)} collective-permute-done((bf16[2,32,2176]{2,1,0:T(8,128)(2,1)S(1)}, bf16[2,32,2176]{2,1,0:T(8,128)(2,1)S(1)}, u32[]{:S(2)}, u32[]{:S(2)}) %collective-permute-start.20) | collective-permute-done | bytes 278560 | tf_op jit(solution)/shard_map/ppermute | solution.py:315
  48.7 0.9 collective-permute-start.21
  49.7 5.6 %collective-permute-done.21.b_ref = bf16[2,32,2176]{2,1,0:T(8,128)(2,1)S(1)} collective-permute-done((bf16[2,32,2176]{2,1,0:T(8,128)(2,1)S(1)}, bf16[2,32,2176]{2,1,0:T(8,128)(2,1)S(1)}, u32[]{:S(2)}, u32[]{:S(2)}) %collective-permute-start.21) | collective-permute-done | bytes 278560 | tf_op jit(solution)/shard_map/ppermute | solution.py:307
  55.3 1.0 collective-permute-start.22
  56.4 8.5 %collective-permute-done.22.refs_1_ = bf16[4,32,2176]{2,1,0:T(8,128)(2,1)S(1)} collective-permute-done((bf16[4,32,2176]{2,1,0:T(8,128)(2,1)S(1)}, bf16[4,32,2176]{2,1,0:T(8,128)(2,1)S(1)}, u32[]{:S(2)}, u32[]{:S(2)}) %collective-permute-start.22) | collective-permute-done | bytes 557088 | tf_op jit(solution)/shard_map/ppermute | solution.py:307
  64.9 2.0 %collective-permute-done.24.refs_1_ = bf16[4,32,2176]{2,1,0:T(8,128)(2,1)S(1)} collective-permute-done((bf16[4,32,2176]{2,1,0:T(8,128)(2,1)S(1)}, bf16[4,32,2176]{2,1,0:T(8,128)(2,1)S(1)}, u32[]{:S(2)}, u32[]{:S(2)}) %collective-permute-start.24) | collective-permute-done | bytes 557088 | tf_op jit(solution)/shard_map/ppermute | solution.py:234
  66.9 2.6 %shard_map.131 = (bf16[4,32,2048]{2,1,0:T(8,128)(2,1)S(1)}, bf16[4,32,2048]{2,1,0:T(8,128)(2,1)S(1)}) custom-call(bf16[4,32,2176]{2,1,0:T(8,128)(2,1)S(1)} %collective-permute-done.23.refs_0_, bf16[4,32,2176]{2,1,0:T(8,128)(2,1)S(1)} %collective-permute-done.24.refs_1_, bf16[704,2048]{1,0:T(8,128)(2,1)S(1)} %get-tuple-element.52.refs_4_.refs_2_, ...), custom_call_target="tpu_custom_call" | custom-call | tf_op jit(solution)/shard_map/pallas_call | solution.py:318
  69.5 0.2 collective-permute-start.26
  69.7 2.8 %collective-permute-start.31 = (bf16[1,32,2176]{2,1,0:T(8,128)(2,1)S(1)}, bf16[1,32,2176]{2,1,0:T(8,128)(2,1)S(1)}, u32[]{:S(2)}, u32[]{:S(2)}) collective-permute-start(bf16[1,32,2176]{2,1,0:T(8,128)(2,1)S(1)} %bitcast.22), channel_id=1, source_target_pairs={{0,3},{1,2},{2,1},{3,0},{4,7},{5,6},{6,5},{7,4},{8,11},{9,10},{10,... | collective-permute-start | bytes 417800 | tf_op jit(solution)/shard_map/ppermute | solution.py:315
  72.5 5.1 %collective-permute-done.31.a_ref = bf16[1,32,2176]{2,1,0:T(8,128)(2,1)S(1)} collective-permute-done((bf16[1,32,2176]{2,1,0:T(8,128)(2,1)S(1)}, bf16[1,32,2176]{2,1,0:T(8,128)(2,1)S(1)}, u32[]{:S(2)}, u32[]{:S(2)}) %collective-permute-start.31) | collective-permute-done | bytes 139296 | tf_op jit(solution)/shard_map/ppermute | solution.py:315
  77.6 1.0 collective-permute-start.32
  78.5 1.1 collective-permute-start.11
  79.6 3.0 %collective-permute-done.32.b_ref = bf16[1,32,2176]{2,1,0:T(8,128)(2,1)S(1)} collective-permute-done((bf16[1,32,2176]{2,1,0:T(8,128)(2,1)S(1)}, bf16[1,32,2176]{2,1,0:T(8,128)(2,1)S(1)}, u32[]{:S(2)}, u32[]{:S(2)}) %collective-permute-start.32) | collective-permute-done | bytes 139296 | tf_op jit(solution)/shard_map/ppermute | solution.py:307
  82.7 1.0 collective-permute-start.34
  83.7 0.9 collective-permute-done.11.b_ref
  84.6 1.0 collective-permute-start.13
  85.7 2.6 %shard_map.130 = (bf16[4,32,2048]{2,1,0:T(8,128)(2,1)S(1)}, bf16[4,32,2048]{2,1,0:T(8,128)(2,1)S(1)}) custom-call(bf16[4,32,2176]{2,1,0:T(8,128)(2,1)S(1)} %shard_map.129.refs_0_, bf16[4,32,2176]{2,1,0:T(8,128)(2,1)S(1)} %collective-permute-done.22.refs_1_, bf16[704,2048]{1,0:T(8,128)(2,1)S(1)} %get-tuple-element.52.refs_4_.refs_2_, ...), custom_call_target="tpu_custom_call" | custom-call | tf_op jit(solution)/shard_map/pallas_call | solution.py:318
  88.3 0.6 collective-permute-start.25
  88.9 0.1 shard_map.133
  89.0 1.1 collective-permute-start.27
  90.2 0.2 collective-permute-start.35
  90.3 1.9 %collective-permute-done.13.refs_3_ = bf16[2,32,2176]{2,1,0:T(8,128)(2,1)S(1)} collective-permute-done((bf16[2,32,2176]{2,1,0:T(8,128)(2,1)S(1)}, bf16[2,32,2176]{2,1,0:T(8,128)(2,1)S(1)}, u32[]{:S(2)}, u32[]{:S(2)}) %collective-permute-start.13) | collective-permute-done | bytes 278560 | tf_op jit(solution)/shard_map/ppermute | solution.py:307
  92.3 0.5 collective-permute-start.14
  92.8 2.6 %shard_map.137 = (bf16[2,32,2048]{2,1,0:T(8,128)(2,1)S(1)}, bf16[2,32,2048]{2,1,0:T(8,128)(2,1)S(1)}, bf16[2,32,2048]{2,1,0:T(8,128)(2,1)S(1)}, bf16[2,32,2048]{2,1,0:T(8,128)(2,1)S(1)}) custom-call(bf16[2,32,2176]{2,1,0:T(8,128)(2,1)S(1)} %collective-permute-done.33.refs_0_, bf16[2,32,2176]{2,1,0:T(8,128)(2,1)S(1)} %collective-permute-done.35.refs_1_, ...), custom_call_target="tpu_custom_call" | custom-call | tf_op jit(solution)/shard_map/pallas_call | solution.py:318
  95.5 2.8 %shard_map.123 = (bf16[2,32,2048]{2,1,0:T(8,128)(2,1)S(1)}, bf16[2,32,2048]{2,1,0:T(8,128)(2,1)S(1)}, bf16[2,32,2048]{2,1,0:T(8,128)(2,1)S(1)}, bf16[2,32,2048]{2,1,0:T(8,128)(2,1)S(1)}) custom-call(bf16[2,32,2176]{2,1,0:T(8,128)(2,1)S(1)} %collective-permute-done.12.refs_0_, bf16[2,32,2176]{2,1,0:T(8,128)(2,1)S(1)} %collective-permute-done.14.refs_1_, ...), custom_call_target="tpu_custom_call" | custom-call | tf_op jit(solution)/shard_map/pallas_call | solution.py:318
  98.4 0.5 collective-permute-start.16
  98.9 0.1 shard_map.132.a_ref
  99.1 0.1 shard_map.134
  99.2 1.0 collective-permute-start.28
  100.3 1.6 %collective-permute-start.38 = (bf16[2,32,2048]{2,1,0:T(8,128)(2,1)S(1)}, bf16[2,32,2048]{2,1,0:T(8,128)(2,1)S(1)}, u32[]{:S(2)}, u32[]{:S(2)}) collective-permute-start(bf16[2,32,2048]{2,1,0:T(8,128)(2,1)S(1)} %shard_map.139), channel_id=1, source_target_pairs={{0,16},{4,12},{8,24},{12,4},{16,0},{20,28},{24,8},{28,20},{1,17},{... | collective-permute-start | bytes 786440 | tf_op jit(solution)/shard_map/ppermute | solution.py:307
  101.9 0.8 collective-permute-start.17
  102.8 5.0 %collective-permute-done.28.b_ref = bf16[2,32,2048]{2,1,0:T(8,128)(2,1)S(1)} collective-permute-done((bf16[2,32,2048]{2,1,0:T(8,128)(2,1)S(1)}, bf16[2,32,2048]{2,1,0:T(8,128)(2,1)S(1)}, u32[]{:S(2)}, u32[]{:S(2)}) %collective-permute-start.28) | collective-permute-done | bytes 262176 | tf_op jit(solution)/shard_map/ppermute | solution.py:307
  107.9 3.4 %collective-permute-start.29 = (bf16[2,32,2048]{2,1,0:T(8,128)(2,1)S(1)}, bf16[2,32,2048]{2,1,0:T(8,128)(2,1)S(1)}, u32[]{:S(2)}, u32[]{:S(2)}) collective-permute-start(bf16[2,32,2048]{2,1,0:T(8,128)(2,1)S(1)} %shard_map.135), channel_id=1, source_target_pairs={{0,1},{1,0},{2,3},{3,2},{4,6},{5,7},{6,4},{7,5},{8,9},{9,8},{10,11... | collective-permute-start | bytes 786440 | tf_op jit(solution)/shard_map/ppermute | solution.py:315
  111.5 0.8 collective-permute-start.39
  112.4 1.3 %collective-permute-start.18 = (bf16[1,32,2048]{2,1,0:T(8,128)(2,1)S(1)}, bf16[1,32,2048]{2,1,0:T(8,128)(2,1)S(1)}, u32[]{:S(2)}, u32[]{:S(2)}) collective-permute-start(bf16[1,32,2048]{2,1,0:T(8,128)(2,1)S(1)} %get-tuple-element.60), channel_id=1, source_target_pairs={{0,8},{4,20},{8,0},{12,28},{16,24},{20,4},{24,16},{28,12},{1,9},{5... | collective-permute-start | bytes 393224 | tf_op jit(solution)/shard_map/ppermute | solution.py:307
  113.8 2.7 %collective-permute-done.39.b_ref = bf16[1,32,2048]{2,1,0:T(8,128)(2,1)S(1)} collective-permute-done((bf16[1,32,2048]{2,1,0:T(8,128)(2,1)S(1)}, bf16[1,32,2048]{2,1,0:T(8,128)(2,1)S(1)}, u32[]{:S(2)}, u32[]{:S(2)}) %collective-permute-start.39) | collective-permute-done | bytes 131104 | tf_op jit(solution)/shard_map/ppermute | solution.py:307
  116.5 1.8 %collective-permute-start.40 = (bf16[1,32,2048]{2,1,0:T(8,128)(2,1)S(1)}, bf16[1,32,2048]{2,1,0:T(8,128)(2,1)S(1)}, u32[]{:S(2)}, u32[]{:S(2)}) collective-permute-start(bf16[1,32,2048]{2,1,0:T(8,128)(2,1)S(1)} %shard_map.141), channel_id=1, source_target_pairs={{0,3},{1,2},{2,1},{3,0},{4,7},{5,6},{6,5},{7,4},{8,11},{9,10},{10,... | collective-permute-start | bytes 393224 | tf_op jit(solution)/shard_map/ppermute | solution.py:315
  118.4 0.1 collective-permute-start.30
  118.5 4.9 %collective-permute-done.40 = bf16[1,32,2048]{2,1,0:T(8,128)(2,1)S(1)} collective-permute-done((bf16[1,32,2048]{2,1,0:T(8,128)(2,1)S(1)}, bf16[1,32,2048]{2,1,0:T(8,128)(2,1)S(1)}, u32[]{:S(2)}, u32[]{:S(2)}) %collective-permute-start.40) | collective-permute-done | bytes 131104 | tf_op jit(solution)/shard_map/ppermute | solution.py:315
  123.5 0.7 fusion.1
  (55 shorter events, 1.0 us)
Async XLA Ops:
  1.0 7.0 %collective-permute-start.1 = (bf16[128,512]{1,0:T(8,128)(2,1)S(1)}, bf16[128,512]{1,0:T(8,128)(2,1)S(1)}, u32[]{:S(2)}, u32[]{:S(2)}) collective-permute-start(bf16[128,512]{1,0:T(8,128)(2,1)S(1)} %pad_maximum_fusion.1.refs_0_), channel_id=1, source_target_pairs={{0,8},{4,12},{8,0},{12,4},{16,24},{20,28},{24,16},{28,20},{1,9},{5... | collective-permute-start | bytes 393224 | tf_op jit(solution)/shard_map/ppermute | solution.py:234
  4.0 7.3 %collective-permute-start.2 = (bf16[128,512]{1,0:T(8,128)(2,1)S(1)}, bf16[128,512]{1,0:T(8,128)(2,1)S(1)}, u32[]{:S(2)}, u32[]{:S(2)}) collective-permute-start(bf16[128,512]{1,0:T(8,128)(2,1)S(1)} %pad_maximum_fusion.2), channel_id=1, source_target_pairs={{0,12},{4,8},{8,4},{12,0},{16,28},{20,24},{24,20},{28,16},{1,13},{... | collective-permute-start | bytes 393224 | tf_op jit(solution)/shard_map/ppermute | solution.py:234
  5.0 14.8 %collective-permute-start = (bf16[128,768]{1,0:T(8,128)(2,1)S(1)}, bf16[128,768]{1,0:T(8,128)(2,1)S(1)}, u32[]{:S(2)}, u32[]{:S(2)}) collective-permute-start(bf16[128,768]{1,0:T(8,128)(2,1)S(1)} %pad_maximum_fusion), channel_id=1, source_target_pairs={{0,4},{4,0},{8,12},{12,8},{16,20},{20,16},{24,28},{28,24},{1,5},{5... | collective-permute-start | bytes 589832 | tf_op jit(solution)/shard_map/ppermute | solution.py:234
  5.2 14.6 %collective-permute-start.3 = (bf16[128,512]{1,0:T(8,128)(2,1)S(1)}, bf16[128,512]{1,0:T(8,128)(2,1)S(1)}, u32[]{:S(2)}, u32[]{:S(2)}) collective-permute-start(bf16[128,512]{1,0:T(8,128)(2,1)S(1)} %pad_maximum_fusion.1.refs_0_), channel_id=1, source_target_pairs={{0,16},{4,20},{8,24},{12,28},{16,0},{20,4},{24,8},{28,12},{1,17},{... | collective-permute-start | bytes 393224 | tf_op jit(solution)/shard_map/ppermute | solution.py:234
  7.2 12.6 %collective-permute-start.4 = (bf16[128,512]{1,0:T(8,128)(2,1)S(1)}, bf16[128,512]{1,0:T(8,128)(2,1)S(1)}, u32[]{:S(2)}, u32[]{:S(2)}) collective-permute-start(bf16[128,512]{1,0:T(8,128)(2,1)S(1)} %pad_maximum_fusion.2), channel_id=1, source_target_pairs={{0,20},{4,16},{8,28},{12,24},{16,4},{20,0},{24,12},{28,8},{1,21},{... | collective-permute-start | bytes 393224 | tf_op jit(solution)/shard_map/ppermute | solution.py:234
  7.9 11.9 %collective-permute-start.5 = (bf16[128,512]{1,0:T(8,128)(2,1)S(1)}, bf16[128,512]{1,0:T(8,128)(2,1)S(1)}, u32[]{:S(2)}, u32[]{:S(2)}) collective-permute-start(bf16[128,512]{1,0:T(8,128)(2,1)S(1)} %pad_maximum_fusion.1.refs_0_), channel_id=1, source_target_pairs={{0,24},{4,28},{8,16},{12,20},{16,8},{20,12},{24,0},{28,4},{1,25},{... | collective-permute-start | bytes 393224 | tf_op jit(solution)/shard_map/ppermute | solution.py:234
  11.3 8.5 %collective-permute-start.6 = (bf16[128,512]{1,0:T(8,128)(2,1)S(1)}, bf16[128,512]{1,0:T(8,128)(2,1)S(1)}, u32[]{:S(2)}, u32[]{:S(2)}) collective-permute-start(bf16[128,512]{1,0:T(8,128)(2,1)S(1)} %pad_maximum_fusion.2), channel_id=1, source_target_pairs={{0,28},{4,24},{8,20},{12,16},{16,12},{20,8},{24,4},{28,0},{1,29},{... | collective-permute-start | bytes 393224 | tf_op jit(solution)/shard_map/ppermute | solution.py:234
  12.9 0.7 copy-start
  13.6 0.7 copy-start.1
  14.3 0.7 copy-start.2
  21.3 1.3 %collective-permute-start.7 = (bf16[128,256]{1,0:T(8,128)(2,1)S(1)}, bf16[128,256]{1,0:T(8,128)(2,1)S(1)}, u32[]{:S(2)}, u32[]{:S(2)}) collective-permute-start(bf16[128,256]{1,0:T(8,128)(2,1)S(1)} %get-tuple-element.41), channel_id=1, source_target_pairs={{0,4},{4,0},{8,12},{12,8},{16,20},{20,16},{24,28},{28,24},{1,5},{5... | collective-permute-start | bytes 196616 | tf_op jit(solution)/shard_map/ppermute | solution.py:234
  23.1 7.6 %collective-permute-start.8 = (bf16[32,2048]{1,0:T(8,128)(2,1)S(1)}, bf16[32,2048]{1,0:T(8,128)(2,1)S(1)}, u32[]{:S(2)}, u32[]{:S(2)}) collective-permute-start(bf16[32,2048]{1,0:T(8,128)(2,1)S(1)} %get-tuple-element.44), channel_id=1, source_target_pairs={{0,1},{1,0},{2,3},{3,2},{4,5},{5,4},{6,7},{7,6},{8,9},{9,8},{10,11... | collective-permute-start | bytes 393224 | tf_op jit(solution)/shard_map/ppermute | solution.py:237
  24.7 12.9 %collective-permute-start.9 = (bf16[32,2048]{1,0:T(8,128)(2,1)S(1)}, bf16[32,2048]{1,0:T(8,128)(2,1)S(1)}, u32[]{:S(2)}, u32[]{:S(2)}) collective-permute-start(bf16[32,2048]{1,0:T(8,128)(2,1)S(1)} %get-tuple-element.45), channel_id=1, source_target_pairs={{0,2},{1,3},{2,0},{3,1},{4,6},{5,7},{6,4},{7,5},{8,10},{9,11},{10,... | collective-permute-start | bytes 393224 | tf_op jit(solution)/shard_map/ppermute | solution.py:237
  27.3 10.3 %collective-permute-start.10 = (bf16[32,2048]{1,0:T(8,128)(2,1)S(1)}, bf16[32,2048]{1,0:T(8,128)(2,1)S(1)}, u32[]{:S(2)}, u32[]{:S(2)}) collective-permute-start(bf16[32,2048]{1,0:T(8,128)(2,1)S(1)} %get-tuple-element.46), channel_id=1, source_target_pairs={{0,3},{1,2},{2,1},{3,0},{4,7},{5,6},{6,5},{7,4},{8,11},{9,10},{10,... | collective-permute-start | bytes 393224 | tf_op jit(solution)/shard_map/ppermute | solution.py:237
  37.8 1.4 %collective-permute-start.19 = (bf16[1,32,2176]{2,1,0:T(8,128)(2,1)S(1)}, bf16[1,32,2176]{2,1,0:T(8,128)(2,1)S(1)}, u32[]{:S(2)}, u32[]{:S(2)}) collective-permute-start(bf16[1,32,2176]{2,1,0:T(8,128)(2,1)S(1)} %bitcast.20), channel_id=1, source_target_pairs={{0,4},{4,0},{8,12},{12,8},{16,20},{20,16},{24,28},{28,24},{1,5},{5... | collective-permute-start | bytes 417800 | tf_op jit(solution)/shard_map/ppermute | solution.py:234
  39.2 9.5 %collective-permute-start.20 = (bf16[2,32,2176]{2,1,0:T(8,128)(2,1)S(1)}, bf16[2,32,2176]{2,1,0:T(8,128)(2,1)S(1)}, u32[]{:S(2)}, u32[]{:S(2)}) collective-permute-start(bf16[2,32,2176]{2,1,0:T(8,128)(2,1)S(1)} %shard_map.128), channel_id=1, source_target_pairs={{0,1},{1,0},{2,3},{3,2},{4,6},{5,7},{6,4},{7,5},{8,9},{9,8},{10,11... | collective-permute-start | bytes 835592 | tf_op jit(solution)/shard_map/ppermute | solution.py:315
  48.7 6.5 %collective-permute-start.21 = (bf16[2,32,2176]{2,1,0:T(8,128)(2,1)S(1)}, bf16[2,32,2176]{2,1,0:T(8,128)(2,1)S(1)}, u32[]{:S(2)}, u32[]{:S(2)}) collective-permute-start(bf16[2,32,2176]{2,1,0:T(8,128)(2,1)S(1)} %collective-permute-done.20.a_ref), channel_id=1, source_target_pairs={{0,8},{4,20},{8,0},{12,28},{16,24},{20,4},{24,16},{28,12},{1,9},{5... | collective-permute-start | bytes 835592 | tf_op jit(solution)/shard_map/ppermute | solution.py:307
  55.3 9.6 %collective-permute-start.22 = (bf16[4,32,2176]{2,1,0:T(8,128)(2,1)S(1)}, bf16[4,32,2176]{2,1,0:T(8,128)(2,1)S(1)}, u32[]{:S(2)}, u32[]{:S(2)}) collective-permute-start(bf16[4,32,2176]{2,1,0:T(8,128)(2,1)S(1)} %shard_map.129.refs_0_), channel_id=1, source_target_pairs={{0,16},{4,12},{8,24},{12,4},{16,0},{20,28},{24,8},{28,20},{1,17},{... | collective-permute-start | bytes 1671176 | tf_op jit(solution)/shard_map/ppermute | solution.py:307
  56.4 8.6 %collective-permute-start.23 = (bf16[4,32,2176]{2,1,0:T(8,128)(2,1)S(1)}, bf16[4,32,2176]{2,1,0:T(8,128)(2,1)S(1)}, u32[]{:S(2)}, u32[]{:S(2)}) collective-permute-start(bf16[4,32,2176]{2,1,0:T(8,128)(2,1)S(1)} %shard_map.129.refs_0_), channel_id=1, source_target_pairs={{0,4},{4,0},{8,12},{12,8},{16,20},{20,16},{24,28},{28,24},{1,5},{5... | collective-permute-start | bytes 1671176 | tf_op jit(solution)/shard_map/ppermute | solution.py:234
  64.9 2.0 %collective-permute-start.24 = (bf16[4,32,2176]{2,1,0:T(8,128)(2,1)S(1)}, bf16[4,32,2176]{2,1,0:T(8,128)(2,1)S(1)}, u32[]{:S(2)}, u32[]{:S(2)}) collective-permute-start(bf16[4,32,2176]{2,1,0:T(8,128)(2,1)S(1)} %collective-permute-done.22.refs_1_), channel_id=1, source_target_pairs={{0,4},{4,0},{8,12},{12,8},{16,20},{20,16},{24,28},{28,24},{1,5},{5... | collective-permute-start | bytes 1671176 | tf_op jit(solution)/shard_map/ppermute | solution.py:234
  69.5 19.4 %collective-permute-start.26 = (bf16[4,32,2048]{2,1,0:T(8,128)(2,1)S(1)}, bf16[4,32,2048]{2,1,0:T(8,128)(2,1)S(1)}, u32[]{:S(2)}, u32[]{:S(2)}) collective-permute-start(bf16[4,32,2048]{2,1,0:T(8,128)(2,1)S(1)} %get-tuple-element.64), channel_id=1, source_target_pairs={{0,4},{4,0},{8,12},{12,8},{16,20},{20,16},{24,28},{28,24},{1,5},{5... | collective-permute-start | bytes 1572872 | tf_op jit(solution)/shard_map/ppermute | solution.py:234
  69.7 7.9 %collective-permute-start.31 = (bf16[1,32,2176]{2,1,0:T(8,128)(2,1)S(1)}, bf16[1,32,2176]{2,1,0:T(8,128)(2,1)S(1)}, u32[]{:S(2)}, u32[]{:S(2)}) collective-permute-start(bf16[1,32,2176]{2,1,0:T(8,128)(2,1)S(1)} %bitcast.22), channel_id=1, source_target_pairs={{0,3},{1,2},{2,1},{3,0},{4,7},{5,6},{6,5},{7,4},{8,11},{9,10},{10,... | collective-permute-start | bytes 417800 | tf_op jit(solution)/shard_map/ppermute | solution.py:315
  77.6 5.1 %collective-permute-start.32 = (bf16[1,32,2176]{2,1,0:T(8,128)(2,1)S(1)}, bf16[1,32,2176]{2,1,0:T(8,128)(2,1)S(1)}, u32[]{:S(2)}, u32[]{:S(2)}) collective-permute-start(bf16[1,32,2176]{2,1,0:T(8,128)(2,1)S(1)} %collective-permute-done.31.a_ref), channel_id=1, source_target_pairs={{0,8},{4,20},{8,0},{12,28},{16,24},{20,4},{24,16},{28,12},{1,9},{5... | collective-permute-start | bytes 417800 | tf_op jit(solution)/shard_map/ppermute | solution.py:307
  78.5 6.1 %collective-permute-start.11 = (bf16[1,32,2176]{2,1,0:T(8,128)(2,1)S(1)}, bf16[1,32,2176]{2,1,0:T(8,128)(2,1)S(1)}, u32[]{:S(2)}, u32[]{:S(2)}) collective-permute-start(bf16[1,32,2176]{2,1,0:T(8,128)(2,1)S(1)} %bitcast.23), channel_id=1, source_target_pairs={{0,8},{4,20},{8,0},{12,28},{16,24},{20,4},{24,16},{28,12},{1,9},{5... | collective-permute-start | bytes 417800 | tf_op jit(solution)/shard_map/ppermute | solution.py:307
  82.7 7.5 %collective-permute-start.34 = (bf16[2,32,2176]{2,1,0:T(8,128)(2,1)S(1)}, bf16[2,32,2176]{2,1,0:T(8,128)(2,1)S(1)}, u32[]{:S(2)}, u32[]{:S(2)}) collective-permute-start(bf16[2,32,2176]{2,1,0:T(8,128)(2,1)S(1)} %shard_map.136.refs_2_), channel_id=1, source_target_pairs={{0,16},{4,12},{8,24},{12,4},{16,0},{20,28},{24,8},{28,20},{1,17},{... | collective-permute-start | bytes 835592 | tf_op jit(solution)/shard_map/ppermute | solution.py:307
  84.6 7.6 %collective-permute-start.13 = (bf16[2,32,2176]{2,1,0:T(8,128)(2,1)S(1)}, bf16[2,32,2176]{2,1,0:T(8,128)(2,1)S(1)}, u32[]{:S(2)}, u32[]{:S(2)}) collective-permute-start(bf16[2,32,2176]{2,1,0:T(8,128)(2,1)S(1)} %shard_map.122.refs_2_), channel_id=1, source_target_pairs={{0,16},{4,12},{8,24},{12,4},{16,0},{20,28},{24,8},{28,20},{1,17},{... | collective-permute-start | bytes 835592 | tf_op jit(solution)/shard_map/ppermute | solution.py:307
  85.7 6.6 %collective-permute-start.33 = (bf16[2,32,2176]{2,1,0:T(8,128)(2,1)S(1)}, bf16[2,32,2176]{2,1,0:T(8,128)(2,1)S(1)}, u32[]{:S(2)}, u32[]{:S(2)}) collective-permute-start(bf16[2,32,2176]{2,1,0:T(8,128)(2,1)S(1)} %shard_map.136.refs_2_), channel_id=1, source_target_pairs={{0,4},{4,0},{8,12},{12,8},{16,20},{20,16},{24,28},{28,24},{1,5},{5... | collective-permute-start | bytes 835592 | tf_op jit(solution)/shard_map/ppermute | solution.py:234
  88.3 10.6 %collective-permute-start.25 = (bf16[4,32,2048]{2,1,0:T(8,128)(2,1)S(1)}, bf16[4,32,2048]{2,1,0:T(8,128)(2,1)S(1)}, u32[]{:S(2)}, u32[]{:S(2)}) collective-permute-start(bf16[4,32,2048]{2,1,0:T(8,128)(2,1)S(1)} %get-tuple-element.62), channel_id=1, source_target_pairs={{0,4},{4,0},{8,12},{12,8},{16,20},{20,16},{24,28},{28,24},{1,5},{5... | collective-permute-start | bytes 1572872 | tf_op jit(solution)/shard_map/ppermute | solution.py:234
  89.0 10.0 %collective-permute-start.27 = (bf16[4,32,2048]{2,1,0:T(8,128)(2,1)S(1)}, bf16[4,32,2048]{2,1,0:T(8,128)(2,1)S(1)}, u32[]{:S(2)}, u32[]{:S(2)}) collective-permute-start(bf16[4,32,2048]{2,1,0:T(8,128)(2,1)S(1)} %shard_map.133), channel_id=1, source_target_pairs={{0,16},{4,12},{8,24},{12,4},{16,0},{20,28},{24,8},{28,20},{1,17},{... | collective-permute-start | bytes 1572872 | tf_op jit(solution)/shard_map/ppermute | solution.py:307
  90.2 2.6 %collective-permute-start.35 = (bf16[2,32,2176]{2,1,0:T(8,128)(2,1)S(1)}, bf16[2,32,2176]{2,1,0:T(8,128)(2,1)S(1)}, u32[]{:S(2)}, u32[]{:S(2)}) collective-permute-start(bf16[2,32,2176]{2,1,0:T(8,128)(2,1)S(1)} %collective-permute-done.34.refs_3_), channel_id=1, source_target_pairs={{0,4},{4,0},{8,12},{12,8},{16,20},{20,16},{24,28},{28,24},{1,5},{5... | collective-permute-start | bytes 835592 | tf_op jit(solution)/shard_map/ppermute | solution.py:234
  92.2 3.3 %collective-permute-start.12 = (bf16[2,32,2176]{2,1,0:T(8,128)(2,1)S(1)}, bf16[2,32,2176]{2,1,0:T(8,128)(2,1)S(1)}, u32[]{:S(2)}, u32[]{:S(2)}) collective-permute-start(bf16[2,32,2176]{2,1,0:T(8,128)(2,1)S(1)} %shard_map.122.refs_2_), channel_id=1, source_target_pairs={{0,4},{4,0},{8,12},{12,8},{16,20},{20,16},{24,28},{28,24},{1,5},{5... | collective-permute-start | bytes 835592 | tf_op jit(solution)/shard_map/ppermute | solution.py:234
  92.3 3.3 %collective-permute-start.14 = (bf16[2,32,2176]{2,1,0:T(8,128)(2,1)S(1)}, bf16[2,32,2176]{2,1,0:T(8,128)(2,1)S(1)}, u32[]{:S(2)}, u32[]{:S(2)}) collective-permute-start(bf16[2,32,2176]{2,1,0:T(8,128)(2,1)S(1)} %collective-permute-done.13.refs_3_), channel_id=1, source_target_pairs={{0,4},{4,0},{8,12},{12,8},{16,20},{20,16},{24,28},{28,24},{1,5},{5... | collective-permute-start | bytes 835592 | tf_op jit(solution)/shard_map/ppermute | solution.py:234
  95.4 4.8 %collective-permute-start.37 = (bf16[2,32,2048]{2,1,0:T(8,128)(2,1)S(1)}, bf16[2,32,2048]{2,1,0:T(8,128)(2,1)S(1)}, u32[]{:S(2)}, u32[]{:S(2)}) collective-permute-start(bf16[2,32,2048]{2,1,0:T(8,128)(2,1)S(1)} %get-tuple-element.70), channel_id=1, source_target_pairs={{0,4},{4,0},{8,12},{12,8},{16,20},{20,16},{24,28},{28,24},{1,5},{5... | collective-permute-start | bytes 786440 | tf_op jit(solution)/shard_map/ppermute | solution.py:234
  98.4 3.5 %collective-permute-start.16 = (bf16[2,32,2048]{2,1,0:T(8,128)(2,1)S(1)}, bf16[2,32,2048]{2,1,0:T(8,128)(2,1)S(1)}, u32[]{:S(2)}, u32[]{:S(2)}) collective-permute-start(bf16[2,32,2048]{2,1,0:T(8,128)(2,1)S(1)} %get-tuple-element.58), channel_id=1, source_target_pairs={{0,4},{4,0},{8,12},{12,8},{16,20},{20,16},{24,28},{28,24},{1,5},{5... | collective-permute-start | bytes 786440 | tf_op jit(solution)/shard_map/ppermute | solution.py:234
  99.2 8.6 %collective-permute-start.28 = (bf16[2,32,2048]{2,1,0:T(8,128)(2,1)S(1)}, bf16[2,32,2048]{2,1,0:T(8,128)(2,1)S(1)}, u32[]{:S(2)}, u32[]{:S(2)}) collective-permute-start(bf16[2,32,2048]{2,1,0:T(8,128)(2,1)S(1)} %get-tuple-element.66), channel_id=1, source_target_pairs={{0,8},{4,20},{8,0},{12,28},{16,24},{20,4},{24,16},{28,12},{1,9},{5... | collective-permute-start | bytes 786440 | tf_op jit(solution)/shard_map/ppermute | solution.py:307
  100.2 11.1 %collective-permute-start.36 = (bf16[2,32,2048]{2,1,0:T(8,128)(2,1)S(1)}, bf16[2,32,2048]{2,1,0:T(8,128)(2,1)S(1)}, u32[]{:S(2)}, u32[]{:S(2)}) collective-permute-start(bf16[2,32,2048]{2,1,0:T(8,128)(2,1)S(1)} %get-tuple-element.68), channel_id=1, source_target_pairs={{0,4},{4,0},{8,12},{12,8},{16,20},{20,16},{24,28},{28,24},{1,5},{5... | collective-permute-start | bytes 786440 | tf_op jit(solution)/shard_map/ppermute | solution.py:234
  100.3 11.1 %collective-permute-start.38 = (bf16[2,32,2048]{2,1,0:T(8,128)(2,1)S(1)}, bf16[2,32,2048]{2,1,0:T(8,128)(2,1)S(1)}, u32[]{:S(2)}, u32[]{:S(2)}) collective-permute-start(bf16[2,32,2048]{2,1,0:T(8,128)(2,1)S(1)} %shard_map.139), channel_id=1, source_target_pairs={{0,16},{4,12},{8,24},{12,4},{16,0},{20,28},{24,8},{28,20},{1,17},{... | collective-permute-start | bytes 786440 | tf_op jit(solution)/shard_map/ppermute | solution.py:307
  101.9 10.4 %collective-permute-start.15 = (bf16[2,32,2048]{2,1,0:T(8,128)(2,1)S(1)}, bf16[2,32,2048]{2,1,0:T(8,128)(2,1)S(1)}, u32[]{:S(2)}, u32[]{:S(2)}) collective-permute-start(bf16[2,32,2048]{2,1,0:T(8,128)(2,1)S(1)} %get-tuple-element.56), channel_id=1, source_target_pairs={{0,4},{4,0},{8,12},{12,8},{16,20},{20,16},{24,28},{28,24},{1,5},{5... | collective-permute-start | bytes 786440 | tf_op jit(solution)/shard_map/ppermute | solution.py:234
  101.9 10.4 %collective-permute-start.17 = (bf16[2,32,2048]{2,1,0:T(8,128)(2,1)S(1)}, bf16[2,32,2048]{2,1,0:T(8,128)(2,1)S(1)}, u32[]{:S(2)}, u32[]{:S(2)}) collective-permute-start(bf16[2,32,2048]{2,1,0:T(8,128)(2,1)S(1)} %shard_map.125), channel_id=1, source_target_pairs={{0,16},{4,12},{8,24},{12,4},{16,0},{20,28},{24,8},{28,20},{1,17},{... | collective-permute-start | bytes 786440 | tf_op jit(solution)/shard_map/ppermute | solution.py:307
  107.9 10.5 %collective-permute-start.29 = (bf16[2,32,2048]{2,1,0:T(8,128)(2,1)S(1)}, bf16[2,32,2048]{2,1,0:T(8,128)(2,1)S(1)}, u32[]{:S(2)}, u32[]{:S(2)}) collective-permute-start(bf16[2,32,2048]{2,1,0:T(8,128)(2,1)S(1)} %shard_map.135), channel_id=1, source_target_pairs={{0,1},{1,0},{2,3},{3,2},{4,6},{5,7},{6,4},{7,5},{8,9},{9,8},{10,11... | collective-permute-start | bytes 786440 | tf_op jit(solution)/shard_map/ppermute | solution.py:315
  111.5 5.0 %collective-permute-start.39 = (bf16[1,32,2048]{2,1,0:T(8,128)(2,1)S(1)}, bf16[1,32,2048]{2,1,0:T(8,128)(2,1)S(1)}, u32[]{:S(2)}, u32[]{:S(2)}) collective-permute-start(bf16[1,32,2048]{2,1,0:T(8,128)(2,1)S(1)} %get-tuple-element.72), channel_id=1, source_target_pairs={{0,8},{4,20},{8,0},{12,28},{16,24},{20,4},{24,16},{28,12},{1,9},{5... | collective-permute-start | bytes 393224 | tf_op jit(solution)/shard_map/ppermute | solution.py:307
  112.4 6.0 %collective-permute-start.18 = (bf16[1,32,2048]{2,1,0:T(8,128)(2,1)S(1)}, bf16[1,32,2048]{2,1,0:T(8,128)(2,1)S(1)}, u32[]{:S(2)}, u32[]{:S(2)}) collective-permute-start(bf16[1,32,2048]{2,1,0:T(8,128)(2,1)S(1)} %get-tuple-element.60), channel_id=1, source_target_pairs={{0,8},{4,20},{8,0},{12,28},{16,24},{20,4},{24,16},{28,12},{1,9},{5... | collective-permute-start | bytes 393224 | tf_op jit(solution)/shard_map/ppermute | solution.py:307
  116.5 6.9 %collective-permute-start.40 = (bf16[1,32,2048]{2,1,0:T(8,128)(2,1)S(1)}, bf16[1,32,2048]{2,1,0:T(8,128)(2,1)S(1)}, u32[]{:S(2)}, u32[]{:S(2)}) collective-permute-start(bf16[1,32,2048]{2,1,0:T(8,128)(2,1)S(1)} %shard_map.141), channel_id=1, source_target_pairs={{0,3},{1,2},{2,1},{3,0},{4,7},{5,6},{6,5},{7,4},{8,11},{9,10},{10,... | collective-permute-start | bytes 393224 | tf_op jit(solution)/shard_map/ppermute | solution.py:315
  118.4 5.1 %collective-permute-start.30 = (bf16[32,2048]{1,0:T(8,128)(2,1)S(1)}, bf16[32,2048]{1,0:T(8,128)(2,1)S(1)}, u32[]{:S(2)}, u32[]{:S(2)}) collective-permute-start(bf16[32,2048]{1,0:T(8,128)(2,1)S(1)} %slice_bitcast_fusion), channel_id=1, source_target_pairs={{0,4},{4,0},{8,12},{12,8},{16,20},{20,16},{24,28},{28,24},{1,5},{5... | collective-permute-start | bytes 393224 | tf_op jit(solution)/shard_map/ppermute | solution.py:234

commit v2 on v1

--- a/solution.py
+++ b/solution.py
@@ -189,19 +189,28 @@
     return call(join_kernel, shape, [VMEM] * 2, 8)(a, b)
 
 
-def plus_kernel(a_ref, b_ref, *outs):
+def plus_kernel(parts, *refs):
+    more, outs = refs[parts:-parts], refs[-parts:]
     at = 0
-    for out in outs:
-        part = slice(at, at + out.shape[0])
-        at += out.shape[0]
-        out[...] = (a_ref[part].astype(jnp.float32) + b_ref[part].astype(jnp.float32)).astype(
-            out.dtype
-        )
-
-
-def plus(a, b, parts=1):
-    shape = jax.ShapeDtypeStruct((a.shape[0] // parts,) + a.shape[1:], a.dtype)
-    return call(plus_kernel, (shape,) * parts, [VMEM] * 2, 8)(a, b)
+    for own, out in zip(refs, outs):
+        value = own[...].astype(jnp.float32)
+        for whole in more:
+            value = value + whole[at : at + own.shape[0]].astype(jnp.float32)
+        out[...] = value.astype(out.dtype)
+        at += own.shape[0]
+
+
+def plus(owns, *more):
+    shapes = tuple(jax.ShapeDtypeStruct(a.shape, a.dtype) for a in owns)
+    kernel = functools.partial(plus_kernel, len(owns))
+    return call(kernel, shapes, [VMEM] * (len(owns) + len(more)), 8)(*owns, *more)
+
+
+def final_kernel(hidden_ref, *refs):
+    value = hidden_ref[...]
+    for r in refs[:-1]:
+        value = value + r[0].astype(jnp.float32)
+    refs[-1][...] = value.astype(refs[-1].dtype)
 
 
 def per_device(
@@ -306,65 +315,50 @@
         pairs = [(i, i ^ (turned[step] if i & 1 else far[step])) for i in range(seq_count)]
         return lax.ppermute(a, "seq", pairs)
 
-    def lane_exp_send(a, even, odd):
-        pairs = [
-            (i * exp_count + j, i * exp_count + (j ^ (odd if i & 1 else even)))
-            for i in range(seq_count)
-            for j in range(exp_count)
-        ]
-        return lax.ppermute(a, ("seq", "exp"), pairs)
-
-    def mlp(arrays):
+    def gather(own):
+        for step in range(len(far)):
+            own = join(own, lane_send(own, step))
+        return own
+
+    def mlp(mine):
+        other = seq_send(mine, 1)
+        units = mine.shape[0]
+        shapes = [(units,), (units // 2,), (units // 2,)]
         outs = call(
-            functools.partial(expert_kernel, expert_count, local, len(arrays)),
-            tuple(jax.ShapeDtypeStruct(a.shape[:2] + (width,), bf16) for a in arrays),
-            [VMEM] * (len(arrays) + 3),
+            functools.partial(expert_kernel, expert_count, local, 2),
+            tuple(jax.ShapeDtypeStruct(n + (share, width), bf16) for n in shapes),
+            [VMEM] * 5,
             32,
-        )(*arrays, gate_t, up_t, down)
-        return list(outs)
-
-    if exp_count == 4:
-        groups = [(0, 0), (1, 2), (3, 3)]
-    else:
-        groups = [(r, r) for r in range(exp_count)]
-    own_rows = own_rows[None]
-    bases = []
-    for even, odd in groups:
-        base = own_rows
-        if even != odd:
-            base = join(own_rows, seq_send(own_rows, 1))
-        bases.append(lane_exp_send(base, even, odd) if even or odd else base)
-    mixture = 0.0
-    for at, (even, odd) in enumerate(groups):
-        whole = bases[at]
-        for step in range(len(far)):
-            arrived = lane_send(whole, step)
-            if step + 1 < len(far):
-                whole = join(whole, arrived)
-        mine = [whole, arrived]
-        other = [seq_send(a, 1) for a in mine]
-        if even != odd:
-            sums = mlp(other)
-            parts = [seq_send(sums[i], 1) for i in (1, 0)][::-1]
-            sums = mlp(mine)
+        )(other, mine, gate_t, up_t, down)
+        return list(outs[1:]), seq_send(outs[0], 1)
+
+    bases, wholes, sums = {}, {}, {}
+    for r in range(exp_count):
+        if r == 1:
+            wholes[r] = exp_send(wholes[0], 1)
         else:
-            sums = mlp(other + mine)
-            parts = [seq_send(sums[i], 1) for i in (1, 0)][::-1]
-            sums = sums[2:]
-        (sent,) = plus(sums[1], parts[1])
-        (kept,) = plus(sums[0], parts[0])
+            if r == 0:
+                bases[r] = own_rows[None]
+            elif r & 1:
+                bases[r] = exp_send(bases[r - 1], 1)
+            else:
+                bases[r] = exp_send(bases[0], r)
+            wholes[r] = gather(bases[r])
+        sums[r] = mlp(wholes[r])
+    shares = []
+    for r in range(exp_count):
+        parts, arrived = sums[r]
+        kept, sent = plus(parts, arrived)
         for step in reversed(range(len(far))):
             arrived = lane_send(sent, step)
-            if step:
-                kept, sent = plus(kept, arrived, 2)
-            else:
-                (kept,) = plus(kept, arrived)
-        if even or odd:
-            kept = lane_exp_send(kept, even, odd)
-        mixture = mixture + kept[0].astype(f32)
-        if even != odd:
-            mixture = mixture + seq_send(kept[1], 1).astype(f32)
-    return (hidden + mixture).astype(bf16)
+            middle = kept.shape[0] // 2
+            halves = [kept[:middle], kept[middle:]] if step else [kept]
+            kept, *rest = plus(halves, arrived)
+            sent = rest[0] if rest else None
+        shares.append(exp_send(kept, r) if r else kept)
+    return call(
+        final_kernel, jax.ShapeDtypeStruct((share, width), bf16), [VMEM] * (1 + len(shares)), 8
+    )(hidden, *shares)
 
 
 def solution(mesh):

time: 124 us -> 119 us (0.960)
  waiting for transfers between devices: 60.2 us -> 53.8 us
    ppermute x4 -> x0, waiting for transfers between devices: 17.1 us -> none  [lane_exp_send(): return lax.ppermute(a, ('seq', 'exp'), pairs)]
    ppermute x3 -> x9, waiting for transfers between devices: 10.1 us -> 22.6 us  [exp_send(): return lax.ppermute(a, 'exp', xor_swap(exp_count, by))]
    ppermute x4 -> x0, starting transfers between devices: 10.5 us -> none  [lane_exp_send(): return lax.ppermute(a, ('seq', 'exp'), pairs)]
    ppermute x3 -> x9, starting transfers between devices: 4.45 us -> 13.4 us  [exp_send(): return lax.ppermute(a, 'exp', xor_swap(exp_count, by))]
    ppermute x22 -> x16, waiting for transfers between devices: 5.29 us -> 1.65 us  [seq_send(): return lax.ppermute(a, 'seq', xor_swap(seq_count, mask))]
    ppermute x12 -> x14, starting transfers between devices: 12.8 us -> 14.8 us  [lane_send(): return lax.ppermute(a, 'seq', pairs)]
    ppermute x12 -> x14, waiting for transfers between devices: 27.8 us -> 29.6 us  [lane_send(): return lax.ppermute(a, 'seq', pairs)]
    pallas_call x16 -> x17, Pallas kernels: 11.7 us -> 12.4 us  [the longest x4 10.8 us: mlp(): call(functools.partial(expert_kernel, expert_count, local, 2), tuple((jax...]
  transfers between devices with their start and end apart: 41 -> 39, of which waited for: 16 -> 17; matrix products, arithmetic and copies ran while one was open for 1% -> 1% of each run, Pallas kernels for 11% -> 14%
where the time goes in v2:
time: 119 us
  waiting for transfers between devices  53.8 us (45%)
  starting transfers between devices  41.2 us (35%)
  Pallas kernels  19.5 us (16%)
  local copies, waits for them, and re-layouts  3.96 us (3%)
    ppermute x14, waiting for transfers between devices, lane_send(): return lax.ppermute(a, 'seq', pairs)  29.6 us
    ppermute x9, waiting for transfers between devices, exp_send(): return lax.ppermute(a, 'exp', xor_swap(exp_count, by))  22.6 us
    ppermute x14, starting transfers between devices, lane_send(): return lax.ppermute(a, 'seq', pairs)  14.8 us
    ppermute x9, starting transfers between devices, exp_send(): return lax.ppermute(a, 'exp', xor_swap(exp_count, by))  13.4 us
    ppermute x16, starting transfers between devices, seq_send(): return lax.ppermute(a, 'seq', xor_swap(seq_count, mask))  12.9 us
    pallas_call x4, Pallas kernels, mlp(): call(functools.partial(expert_kernel, expert_count, local, 2), tuple((jax...  10.8 us
    pallas_call x1, Pallas kernels, per_device(): call(functools.partial(load_kernel, seq_count, exp_count, expert_count),...  4.85 us
  transfers between devices with their start and end apart: 39, of which 17 were waited for; matrix products, arithmetic and copies ran while one was open for 1% of the time, Pallas kernels for 14%

profile of v2, /device:TPU:0, one launch (start us, length us, event | category | flops | bytes accessed | tf_op | source)
XLA Modules:
  0.0 118.8 jit_solution(16278237136390631457)
XLA Ops:
  0.0 1.0 constant_dynamic-slice_fusion.1
  1.0 3.4 %collective-permute-start.6 = (bf16[128,512]{1,0:T(8,128)(2,1)S(1)}, bf16[128,512]{1,0:T(8,128)(2,1)S(1)}, u32[]{:S(2)}, u32[]{:S(2)}) collective-permute-start(bf16[128,512]{1,0:T(8,128)(2,1)S(1)} %pad_maximum_fusion.2), channel_id=1, source_target_pairs={{0,28},{4,24},{8,20},{12,16},{16,12},{20,8},{24,4},{28,0},{1,29},{... | collective-permute-start | bytes 393224 | tf_op jit(solution)/shard_map/ppermute | solution.py:243
  4.4 0.8 collective-permute-start.4
  5.3 0.9 constant_dynamic-slice_fusion
  6.3 3.0 %collective-permute-start.5 = (bf16[128,512]{1,0:T(8,128)(2,1)S(1)}, bf16[128,512]{1,0:T(8,128)(2,1)S(1)}, u32[]{:S(2)}, u32[]{:S(2)}) collective-permute-start(bf16[128,512]{1,0:T(8,128)(2,1)S(1)} %pad_maximum_fusion.1.refs_0_), channel_id=1, source_target_pairs={{0,24},{4,28},{8,16},{12,20},{16,8},{20,12},{24,0},{28,4},{1,25},{... | collective-permute-start | bytes 393224 | tf_op jit(solution)/shard_map/ppermute | solution.py:243
  9.3 1.5 %collective-permute-start.3 = (bf16[128,512]{1,0:T(8,128)(2,1)S(1)}, bf16[128,512]{1,0:T(8,128)(2,1)S(1)}, u32[]{:S(2)}, u32[]{:S(2)}) collective-permute-start(bf16[128,512]{1,0:T(8,128)(2,1)S(1)} %pad_maximum_fusion.1.refs_0_), channel_id=1, source_target_pairs={{0,16},{4,20},{8,24},{12,28},{16,0},{20,4},{24,8},{28,12},{1,17},{... | collective-permute-start | bytes 393224 | tf_op jit(solution)/shard_map/ppermute | solution.py:243
  10.8 0.4 collective-permute-done.4.refs_5_
  11.2 2.2 %collective-permute-start.1 = (bf16[128,512]{1,0:T(8,128)(2,1)S(1)}, bf16[128,512]{1,0:T(8,128)(2,1)S(1)}, u32[]{:S(2)}, u32[]{:S(2)}) collective-permute-start(bf16[128,512]{1,0:T(8,128)(2,1)S(1)} %pad_maximum_fusion.1.refs_0_), channel_id=1, source_target_pairs={{0,8},{4,12},{8,0},{12,4},{16,24},{20,28},{24,16},{28,20},{1,9},{5... | collective-permute-start | bytes 393224 | tf_op jit(solution)/shard_map/ppermute | solution.py:243
  13.4 0.7 copy-done
  14.1 0.7 copy-done.1
  14.8 0.7 copy-done.2
  15.5 4.9 %shard_map.118 = (bf16[32,2048]{1,0:T(8,128)(2,1)S(1)}, f32[1,2048]{1,0:T(1,128)S(1)}, bf16[512,2048]{1,0:T(8,128)(2,1)S(1)}, bf16[704,2048]{1,0:T(8,128)(2,1)S(...) custom-call(s32[2,3]{1,0:T(2,128)S(1)} %copy-done.2, ...), custom_call_target="tpu_custom_call" | custom-call | tf_op jit(solution)/shard_map/pallas_call | solution.py:272
  20.4 1.4 %shard_map.119 = (bf16[128,256]{1,0:T(8,128)(2,1)S(1)}, bf16[128,256]{1,0:T(8,128)(2,1)S(1)}) custom-call(s32[1,1024]{1,0:T(1,128)S(1)} %get-tuple-element.49.key_ref, bf16[128,256]{1,0:T(8,128)(2,1)S(1)} %get-tuple-element.106.own_ref, bf16[128,512]{1,0:T(8,128)(2,1)S(1)} %pad_maximum_fusion.1.refs_0_, bf16[128,768]{1,0:T(8,128)(2,1)S(1)} %collective-permute-done.refs_1_, ...), custom_call_target="tpu_custom_call" | custom-call | tf_op jit(solution)/shard_map/pallas_call | solution.py:284
  21.9 1.2 %collective-permute-done.7.other_ref = bf16[128,256]{1,0:T(8,128)(2,1)S(1)} collective-permute-done((bf16[128,256]{1,0:T(8,128)(2,1)S(1)}, bf16[128,256]{1,0:T(8,128)(2,1)S(1)}, u32[]{:S(2)}, u32[]{:S(2)}) %collective-permute-start.7) | collective-permute-done | bytes 65568 | tf_op jit(solution)/shard_map/ppermute | solution.py:243
  23.2 0.5 shard_map.120
  23.6 1.6 %collective-permute-start.8 = (bf16[32,2048]{1,0:T(8,128)(2,1)S(1)}, bf16[32,2048]{1,0:T(8,128)(2,1)S(1)}, u32[]{:S(2)}, u32[]{:S(2)}) collective-permute-start(bf16[32,2048]{1,0:T(8,128)(2,1)S(1)} %get-tuple-element.54), channel_id=1, source_target_pairs={{0,1},{1,0},{2,3},{3,2},{4,5},{5,4},{6,7},{7,6},{8,9},{9,8},{10,11... | collective-permute-start | bytes 393224 | tf_op jit(solution)/shard_map/ppermute | solution.py:246
  25.3 2.6 %collective-permute-start.9 = (bf16[32,2048]{1,0:T(8,128)(2,1)S(1)}, bf16[32,2048]{1,0:T(8,128)(2,1)S(1)}, u32[]{:S(2)}, u32[]{:S(2)}) collective-permute-start(bf16[32,2048]{1,0:T(8,128)(2,1)S(1)} %get-tuple-element.55), channel_id=1, source_target_pairs={{0,2},{1,3},{2,0},{3,1},{4,6},{5,7},{6,4},{7,5},{8,10},{9,11},{10,... | collective-permute-start | bytes 393224 | tf_op jit(solution)/shard_map/ppermute | solution.py:246
  27.8 0.2 collective-permute-start.10
  28.1 3.1 %collective-permute-done.8.refs_0_ = bf16[32,2048]{1,0:T(8,128)(2,1)S(1)} collective-permute-done((bf16[32,2048]{1,0:T(8,128)(2,1)S(1)}, bf16[32,2048]{1,0:T(8,128)(2,1)S(1)}, u32[]{:S(2)}, u32[]{:S(2)}) %collective-permute-start.8) | collective-permute-done | bytes 131104 | tf_op jit(solution)/shard_map/ppermute | solution.py:246
  31.2 6.9 %collective-permute-done.9.refs_1_ = bf16[32,2048]{1,0:T(8,128)(2,1)S(1)} collective-permute-done((bf16[32,2048]{1,0:T(8,128)(2,1)S(1)}, bf16[32,2048]{1,0:T(8,128)(2,1)S(1)}, u32[]{:S(2)}, u32[]{:S(2)}) %collective-permute-start.9) | collective-permute-done | bytes 131104 | tf_op jit(solution)/shard_map/ppermute | solution.py:246
  38.1 0.2 shard_map.121
  38.3 3.4 %collective-permute-start.23 = (bf16[1,32,2176]{2,1,0:T(8,128)(2,1)S(1)}, bf16[1,32,2176]{2,1,0:T(8,128)(2,1)S(1)}, u32[]{:S(2)}, u32[]{:S(2)}) collective-permute-start(bf16[1,32,2176]{2,1,0:T(8,128)(2,1)S(1)} %bitcast.11), channel_id=1, source_target_pairs={{0,2},{1,3},{2,0},{3,1},{4,6},{5,7},{6,4},{7,5},{8,10},{9,11},{10,... | collective-permute-start | bytes 417800 | tf_op jit(solution)/shard_map/ppermute | solution.py:246
  41.7 0.5 collective-permute-start.11
  42.3 5.4 %collective-permute-done.23.a_ref = bf16[1,32,2176]{2,1,0:T(8,128)(2,1)S(1)} collective-permute-done((bf16[1,32,2176]{2,1,0:T(8,128)(2,1)S(1)}, bf16[1,32,2176]{2,1,0:T(8,128)(2,1)S(1)}, u32[]{:S(2)}, u32[]{:S(2)}) %collective-permute-start.23) | collective-permute-done | bytes 139296 | tf_op jit(solution)/shard_map/ppermute | solution.py:246
  47.6 0.5 collective-permute-start.24
  48.2 1.6 %collective-permute-start.12 = (bf16[2,32,2176]{2,1,0:T(8,128)(2,1)S(1)}, bf16[2,32,2176]{2,1,0:T(8,128)(2,1)S(1)}, u32[]{:S(2)}, u32[]{:S(2)}) collective-permute-start(bf16[2,32,2176]{2,1,0:T(8,128)(2,1)S(1)} %shard_map.122.a_ref), channel_id=1, source_target_pairs={{0,16},{4,12},{8,24},{12,4},{16,0},{20,28},{24,8},{28,20},{1,17},{... | collective-permute-start | bytes 835592 | tf_op jit(solution)/shard_map/ppermute | solution.py:316
  49.8 4.4 %collective-permute-done.24.b_ref = bf16[1,32,2176]{2,1,0:T(8,128)(2,1)S(1)} collective-permute-done((bf16[1,32,2176]{2,1,0:T(8,128)(2,1)S(1)}, bf16[1,32,2176]{2,1,0:T(8,128)(2,1)S(1)}, u32[]{:S(2)}, u32[]{:S(2)}) %collective-permute-start.24) | collective-permute-done | bytes 139296 | tf_op jit(solution)/shard_map/ppermute | solution.py:316
  54.2 0.6 collective-permute-start.25
  54.9 2.1 %collective-permute-start.17 = (bf16[4,32,2176]{2,1,0:T(8,128)(2,1)S(1)}, bf16[4,32,2176]{2,1,0:T(8,128)(2,1)S(1)}, u32[]{:S(2)}, u32[]{:S(2)}) collective-permute-start(bf16[4,32,2176]{2,1,0:T(8,128)(2,1)S(1)} %shard_map.123.refs_1_), channel_id=1, source_target_pairs={{0,1},{1,0},{2,3},{3,2},{4,5},{5,4},{6,7},{7,6},{8,9},{9,8},{10,11... | collective-permute-start | bytes 1671176 | tf_op jit(solution)/shard_map/ppermute | solution.py:246
  56.9 3.9 %collective-permute-done.25.b_ref = bf16[2,32,2176]{2,1,0:T(8,128)(2,1)S(1)} collective-permute-done((bf16[2,32,2176]{2,1,0:T(8,128)(2,1)S(1)}, bf16[2,32,2176]{2,1,0:T(8,128)(2,1)S(1)}, u32[]{:S(2)}, u32[]{:S(2)}) %collective-permute-start.25) | collective-permute-done | bytes 278560 | tf_op jit(solution)/shard_map/ppermute | solution.py:316
  60.9 0.4 collective-permute-done.31.a_ref
  61.3 1.6 %collective-permute-start.32 = (bf16[1,32,2176]{2,1,0:T(8,128)(2,1)S(1)}, bf16[1,32,2176]{2,1,0:T(8,128)(2,1)S(1)}, u32[]{:S(2)}, u32[]{:S(2)}) collective-permute-start(bf16[1,32,2176]{2,1,0:T(8,128)(2,1)S(1)} %collective-permute-done.31.a_ref), channel_id=1, source_target_pairs={{0,8},{4,20},{8,0},{12,28},{16,24},{20,4},{24,16},{28,12},{1,9},{5... | collective-permute-start | bytes 417800 | tf_op jit(solution)/shard_map/ppermute | solution.py:316
  62.9 3.5 %collective-permute-done.32.b_ref = bf16[1,32,2176]{2,1,0:T(8,128)(2,1)S(1)} collective-permute-done((bf16[1,32,2176]{2,1,0:T(8,128)(2,1)S(1)}, bf16[1,32,2176]{2,1,0:T(8,128)(2,1)S(1)}, u32[]{:S(2)}, u32[]{:S(2)}) %collective-permute-start.32) | collective-permute-done | bytes 139296 | tf_op jit(solution)/shard_map/ppermute | solution.py:316
  66.4 1.6 %collective-permute-start.33 = (bf16[2,32,2176]{2,1,0:T(8,128)(2,1)S(1)}, bf16[2,32,2176]{2,1,0:T(8,128)(2,1)S(1)}, u32[]{:S(2)}, u32[]{:S(2)}) collective-permute-start(bf16[2,32,2176]{2,1,0:T(8,128)(2,1)S(1)} %shard_map.138.a_ref), channel_id=1, source_target_pairs={{0,16},{4,12},{8,24},{12,4},{16,0},{20,28},{24,8},{28,20},{1,17},{... | collective-permute-start | bytes 835592 | tf_op jit(solution)/shard_map/ppermute | solution.py:316
  68.0 5.0 %collective-permute-done.33.b_ref = bf16[2,32,2176]{2,1,0:T(8,128)(2,1)S(1)} collective-permute-done((bf16[2,32,2176]{2,1,0:T(8,128)(2,1)S(1)}, bf16[2,32,2176]{2,1,0:T(8,128)(2,1)S(1)}, u32[]{:S(2)}, u32[]{:S(2)}) %collective-permute-start.33) | collective-permute-done | bytes 278560 | tf_op jit(solution)/shard_map/ppermute | solution.py:316
  73.2 0.5 collective-permute-start.18
  73.7 2.6 %shard_map.124 = (bf16[4,32,2048]{2,1,0:T(8,128)(2,1)S(1)}, bf16[2,32,2048]{2,1,0:T(8,128)(2,1)S(1)}, bf16[2,32,2048]{2,1,0:T(8,128)(2,1)S(1)}) custom-call(bf16[4,32,2176]{2,1,0:T(8,128)(2,1)S(1)} %collective-permute-done.13.refs_0_, bf16[4,32,2176]{2,1,0:T(8,128)(2,1)S(1)} %shard_map.123.refs_1_, bf16[704,2048]{1,0:T(8,128)(2,1)S(1)} %get-tuple-element.62.refs_2_, ...), custom_call_target="tpu_custom_call" | custom-call | tf_op jit(solution)/shard_map/pallas_call | solution.py:327
  76.3 0.2 collective-permute-start.14
  76.5 2.6 %shard_map.134 = (bf16[4,32,2048]{2,1,0:T(8,128)(2,1)S(1)}, bf16[2,32,2048]{2,1,0:T(8,128)(2,1)S(1)}, bf16[2,32,2048]{2,1,0:T(8,128)(2,1)S(1)}) custom-call(bf16[4,32,2176]{2,1,0:T(8,128)(2,1)S(1)} %collective-permute-done.26.refs_0_, bf16[4,32,2176]{2,1,0:T(8,128)(2,1)S(1)} %shard_map.133.refs_1_, bf16[704,2048]{1,0:T(8,128)(2,1)S(1)} %get-tuple-element.62.refs_2_, ...), custom_call_target="tpu_custom_call" | custom-call | tf_op jit(solution)/shard_map/pallas_call | solution.py:327
  79.1 0.5 collective-permute-start.27
  79.6 2.6 %shard_map.140 = (bf16[4,32,2048]{2,1,0:T(8,128)(2,1)S(1)}, bf16[2,32,2048]{2,1,0:T(8,128)(2,1)S(1)}, bf16[2,32,2048]{2,1,0:T(8,128)(2,1)S(1)}) custom-call(bf16[4,32,2176]{2,1,0:T(8,128)(2,1)S(1)} %collective-permute-done.34.refs_0_, bf16[4,32,2176]{2,1,0:T(8,128)(2,1)S(1)} %shard_map.139.refs_1_, bf16[704,2048]{1,0:T(8,128)(2,1)S(1)} %get-tuple-element.62.refs_2_, ...), custom_call_target="tpu_custom_call" | custom-call | tf_op jit(solution)/shard_map/pallas_call | solution.py:327
  82.3 0.2 collective-permute-start.35
  82.5 1.6 %collective-permute-start.15 = (bf16[2,32,2048]{2,1,0:T(8,128)(2,1)S(1)}, bf16[2,32,2048]{2,1,0:T(8,128)(2,1)S(1)}, u32[]{:S(2)}, u32[]{:S(2)}) collective-permute-start(bf16[2,32,2048]{2,1,0:T(8,128)(2,1)S(1)} %get-tuple-element.69), channel_id=1, source_target_pairs={{0,16},{4,12},{8,24},{12,4},{16,0},{20,28},{24,8},{28,20},{1,17},{... | collective-permute-start | bytes 786440 | tf_op jit(solution)/shard_map/ppermute | solution.py:316
  84.1 2.8 %shard_map.128 = (bf16[4,32,2048]{2,1,0:T(8,128)(2,1)S(1)}, bf16[2,32,2048]{2,1,0:T(8,128)(2,1)S(1)}, bf16[2,32,2048]{2,1,0:T(8,128)(2,1)S(1)}) custom-call(bf16[4,32,2176]{2,1,0:T(8,128)(2,1)S(1)} %collective-permute-done.18.refs_0_, bf16[4,32,2176]{2,1,0:T(8,128)(2,1)S(1)} %collective-permute-done.17.refs_1_, ...), custom_call_target="tpu_custom_call" | custom-call | tf_op jit(solution)/shard_map/pallas_call | solution.py:327
  87.0 0.2 collective-permute-start.19
  87.4 0.6 collective-permute-start.28
  88.1 1.6 %collective-permute-start.36 = (bf16[2,32,2048]{2,1,0:T(8,128)(2,1)S(1)}, bf16[2,32,2048]{2,1,0:T(8,128)(2,1)S(1)}, u32[]{:S(2)}, u32[]{:S(2)}) collective-permute-start(bf16[2,32,2048]{2,1,0:T(8,128)(2,1)S(1)} %get-tuple-element.90), channel_id=1, source_target_pairs={{0,16},{4,12},{8,24},{12,4},{16,0},{20,28},{24,8},{28,20},{1,17},{... | collective-permute-start | bytes 786440 | tf_op jit(solution)/shard_map/ppermute | solution.py:316
  89.7 4.1 %collective-permute-done.28.refs_2_ = bf16[2,32,2048]{2,1,0:T(8,128)(2,1)S(1)} collective-permute-done((bf16[2,32,2048]{2,1,0:T(8,128)(2,1)S(1)}, bf16[2,32,2048]{2,1,0:T(8,128)(2,1)S(1)}, u32[]{:S(2)}, u32[]{:S(2)}) %collective-permute-start.28) | collective-permute-done | bytes 262176 | tf_op jit(solution)/shard_map/ppermute | solution.py:316
  93.9 0.5 collective-permute-start.29
  94.4 2.8 %collective-permute-done.36.refs_2_ = bf16[2,32,2048]{2,1,0:T(8,128)(2,1)S(1)} collective-permute-done((bf16[2,32,2048]{2,1,0:T(8,128)(2,1)S(1)}, bf16[2,32,2048]{2,1,0:T(8,128)(2,1)S(1)}, u32[]{:S(2)}, u32[]{:S(2)}) %collective-permute-start.36) | collective-permute-done | bytes 262176 | tf_op jit(solution)/shard_map/ppermute | solution.py:316
  97.3 0.5 collective-permute-start.37
  97.8 0.1 shard_map.129
  97.9 1.6 %collective-permute-start.20 = (bf16[2,32,2048]{2,1,0:T(8,128)(2,1)S(1)}, bf16[2,32,2048]{2,1,0:T(8,128)(2,1)S(1)}, u32[]{:S(2)}, u32[]{:S(2)}) collective-permute-start(bf16[2,32,2048]{2,1,0:T(8,128)(2,1)S(1)} %get-tuple-element.76), channel_id=1, source_target_pairs={{0,16},{4,12},{8,24},{12,4},{16,0},{20,28},{24,8},{28,20},{1,17},{... | collective-permute-start | bytes 786440 | tf_op jit(solution)/shard_map/ppermute | solution.py:316
  99.5 4.8 %collective-permute-done.20.refs_2_ = bf16[2,32,2048]{2,1,0:T(8,128)(2,1)S(1)} collective-permute-done((bf16[2,32,2048]{2,1,0:T(8,128)(2,1)S(1)}, bf16[2,32,2048]{2,1,0:T(8,128)(2,1)S(1)}, u32[]{:S(2)}, u32[]{:S(2)}) %collective-permute-start.20) | collective-permute-done | bytes 262176 | tf_op jit(solution)/shard_map/ppermute | solution.py:316
  104.4 1.7 %collective-permute-start.21 = (bf16[1,32,2048]{2,1,0:T(8,128)(2,1)S(1)}, bf16[1,32,2048]{2,1,0:T(8,128)(2,1)S(1)}, u32[]{:S(2)}, u32[]{:S(2)}) collective-permute-start(bf16[1,32,2048]{2,1,0:T(8,128)(2,1)S(1)} %get-tuple-element.78), channel_id=1, source_target_pairs={{0,8},{4,20},{8,0},{12,28},{16,24},{20,4},{24,16},{28,12},{1,9},{5... | collective-permute-start | bytes 393224 | tf_op jit(solution)/shard_map/ppermute | solution.py:316
  106.2 0.5 collective-permute-start.16
  106.7 0.5 collective-permute-start.30
  107.2 2.0 %collective-permute-start.38 = (bf16[1,32,2048]{2,1,0:T(8,128)(2,1)S(1)}, bf16[1,32,2048]{2,1,0:T(8,128)(2,1)S(1)}, u32[]{:S(2)}, u32[]{:S(2)}) collective-permute-start(bf16[1,32,2048]{2,1,0:T(8,128)(2,1)S(1)} %shard_map.143), channel_id=1, source_target_pairs={{0,3},{1,2},{2,1},{3,0},{4,7},{5,6},{6,5},{7,4},{8,11},{9,10},{10,... | collective-permute-start | bytes 393224 | tf_op jit(solution)/shard_map/ppermute | solution.py:246
  109.3 0.2 collective-permute-done.21.refs_1_
  109.5 1.0 collective-permute-start.22
  110.5 0.8 collective-permute-done.16.refs_1_
  111.3 5.8 %collective-permute-done.30.refs_2_ = bf16[1,32,2048]{2,1,0:T(8,128)(2,1)S(1)} collective-permute-done((bf16[1,32,2048]{2,1,0:T(8,128)(2,1)S(1)}, bf16[1,32,2048]{2,1,0:T(8,128)(2,1)S(1)}, u32[]{:S(2)}, u32[]{:S(2)}) %collective-permute-start.30) | collective-permute-done | bytes 131104 | tf_op jit(solution)/shard_map/ppermute | solution.py:246
  117.1 1.0 collective-permute-done.22.refs_1_
  118.0 0.7 shard_map.144
  (56 shorter events, 1.6 us)
Async XLA Ops:
  1.0 8.4 %collective-permute-start.6 = (bf16[128,512]{1,0:T(8,128)(2,1)S(1)}, bf16[128,512]{1,0:T(8,128)(2,1)S(1)}, u32[]{:S(2)}, u32[]{:S(2)}) collective-permute-start(bf16[128,512]{1,0:T(8,128)(2,1)S(1)} %pad_maximum_fusion.2), channel_id=1, source_target_pairs={{0,28},{4,24},{8,20},{12,16},{16,12},{20,8},{24,4},{28,0},{1,29},{... | collective-permute-start | bytes 393224 | tf_op jit(solution)/shard_map/ppermute | solution.py:243
  4.4 6.8 %collective-permute-start.4 = (bf16[128,512]{1,0:T(8,128)(2,1)S(1)}, bf16[128,512]{1,0:T(8,128)(2,1)S(1)}, u32[]{:S(2)}, u32[]{:S(2)}) collective-permute-start(bf16[128,512]{1,0:T(8,128)(2,1)S(1)} %pad_maximum_fusion.2), channel_id=1, source_target_pairs={{0,20},{4,16},{8,28},{12,24},{16,4},{20,0},{24,12},{28,8},{1,21},{... | collective-permute-start | bytes 393224 | tf_op jit(solution)/shard_map/ppermute | solution.py:243
  5.2 15.2 %collective-permute-start.2 = (bf16[128,512]{1,0:T(8,128)(2,1)S(1)}, bf16[128,512]{1,0:T(8,128)(2,1)S(1)}, u32[]{:S(2)}, u32[]{:S(2)}) collective-permute-start(bf16[128,512]{1,0:T(8,128)(2,1)S(1)} %pad_maximum_fusion.2), channel_id=1, source_target_pairs={{0,12},{4,8},{8,4},{12,0},{16,28},{20,24},{24,20},{28,16},{1,13},{... | collective-permute-start | bytes 393224 | tf_op jit(solution)/shard_map/ppermute | solution.py:243
  6.2 14.2 %collective-permute-start = (bf16[128,768]{1,0:T(8,128)(2,1)S(1)}, bf16[128,768]{1,0:T(8,128)(2,1)S(1)}, u32[]{:S(2)}, u32[]{:S(2)}) collective-permute-start(bf16[128,768]{1,0:T(8,128)(2,1)S(1)} %pad_maximum_fusion), channel_id=1, source_target_pairs={{0,4},{4,0},{8,12},{12,8},{16,20},{20,16},{24,28},{28,24},{1,5},{5... | collective-permute-start | bytes 589832 | tf_op jit(solution)/shard_map/ppermute | solution.py:243
  6.3 14.0 %collective-permute-start.5 = (bf16[128,512]{1,0:T(8,128)(2,1)S(1)}, bf16[128,512]{1,0:T(8,128)(2,1)S(1)}, u32[]{:S(2)}, u32[]{:S(2)}) collective-permute-start(bf16[128,512]{1,0:T(8,128)(2,1)S(1)} %pad_maximum_fusion.1.refs_0_), channel_id=1, source_target_pairs={{0,24},{4,28},{8,16},{12,20},{16,8},{20,12},{24,0},{28,4},{1,25},{... | collective-permute-start | bytes 393224 | tf_op jit(solution)/shard_map/ppermute | solution.py:243
  9.3 11.0 %collective-permute-start.3 = (bf16[128,512]{1,0:T(8,128)(2,1)S(1)}, bf16[128,512]{1,0:T(8,128)(2,1)S(1)}, u32[]{:S(2)}, u32[]{:S(2)}) collective-permute-start(bf16[128,512]{1,0:T(8,128)(2,1)S(1)} %pad_maximum_fusion.1.refs_0_), channel_id=1, source_target_pairs={{0,16},{4,20},{8,24},{12,28},{16,0},{20,4},{24,8},{28,12},{1,17},{... | collective-permute-start | bytes 393224 | tf_op jit(solution)/shard_map/ppermute | solution.py:243
  11.2 9.2 %collective-permute-start.1 = (bf16[128,512]{1,0:T(8,128)(2,1)S(1)}, bf16[128,512]{1,0:T(8,128)(2,1)S(1)}, u32[]{:S(2)}, u32[]{:S(2)}) collective-permute-start(bf16[128,512]{1,0:T(8,128)(2,1)S(1)} %pad_maximum_fusion.1.refs_0_), channel_id=1, source_target_pairs={{0,8},{4,12},{8,0},{12,4},{16,24},{20,28},{24,16},{28,20},{1,9},{5... | collective-permute-start | bytes 393224 | tf_op jit(solution)/shard_map/ppermute | solution.py:243
  13.4 0.7 copy-start
  14.1 0.7 copy-start.1
  14.8 0.7 copy-start.2
  21.8 1.3 %collective-permute-start.7 = (bf16[128,256]{1,0:T(8,128)(2,1)S(1)}, bf16[128,256]{1,0:T(8,128)(2,1)S(1)}, u32[]{:S(2)}, u32[]{:S(2)}) collective-permute-start(bf16[128,256]{1,0:T(8,128)(2,1)S(1)} %get-tuple-element.51), channel_id=1, source_target_pairs={{0,4},{4,0},{8,12},{12,8},{16,20},{20,16},{24,28},{28,24},{1,5},{5... | collective-permute-start | bytes 196616 | tf_op jit(solution)/shard_map/ppermute | solution.py:243
  23.6 7.6 %collective-permute-start.8 = (bf16[32,2048]{1,0:T(8,128)(2,1)S(1)}, bf16[32,2048]{1,0:T(8,128)(2,1)S(1)}, u32[]{:S(2)}, u32[]{:S(2)}) collective-permute-start(bf16[32,2048]{1,0:T(8,128)(2,1)S(1)} %get-tuple-element.54), channel_id=1, source_target_pairs={{0,1},{1,0},{2,3},{3,2},{4,5},{5,4},{6,7},{7,6},{8,9},{9,8},{10,11... | collective-permute-start | bytes 393224 | tf_op jit(solution)/shard_map/ppermute | solution.py:246
  25.3 12.9 %collective-permute-start.9 = (bf16[32,2048]{1,0:T(8,128)(2,1)S(1)}, bf16[32,2048]{1,0:T(8,128)(2,1)S(1)}, u32[]{:S(2)}, u32[]{:S(2)}) collective-permute-start(bf16[32,2048]{1,0:T(8,128)(2,1)S(1)} %get-tuple-element.55), channel_id=1, source_target_pairs={{0,2},{1,3},{2,0},{3,1},{4,6},{5,7},{6,4},{7,5},{8,10},{9,11},{10,... | collective-permute-start | bytes 393224 | tf_op jit(solution)/shard_map/ppermute | solution.py:246
  27.8 10.3 %collective-permute-start.10 = (bf16[32,2048]{1,0:T(8,128)(2,1)S(1)}, bf16[32,2048]{1,0:T(8,128)(2,1)S(1)}, u32[]{:S(2)}, u32[]{:S(2)}) collective-permute-start(bf16[32,2048]{1,0:T(8,128)(2,1)S(1)} %get-tuple-element.56), channel_id=1, source_target_pairs={{0,3},{1,2},{2,1},{3,0},{4,7},{5,6},{6,5},{7,4},{8,11},{9,10},{10,... | collective-permute-start | bytes 393224 | tf_op jit(solution)/shard_map/ppermute | solution.py:246
  38.3 9.3 %collective-permute-start.23 = (bf16[1,32,2176]{2,1,0:T(8,128)(2,1)S(1)}, bf16[1,32,2176]{2,1,0:T(8,128)(2,1)S(1)}, u32[]{:S(2)}, u32[]{:S(2)}) collective-permute-start(bf16[1,32,2176]{2,1,0:T(8,128)(2,1)S(1)} %bitcast.11), channel_id=1, source_target_pairs={{0,2},{1,3},{2,0},{3,1},{4,6},{5,7},{6,4},{7,5},{8,10},{9,11},{10,... | collective-permute-start | bytes 417800 | tf_op jit(solution)/shard_map/ppermute | solution.py:246
  41.7 6.4 %collective-permute-start.11 = (bf16[1,32,2176]{2,1,0:T(8,128)(2,1)S(1)}, bf16[1,32,2176]{2,1,0:T(8,128)(2,1)S(1)}, u32[]{:S(2)}, u32[]{:S(2)}) collective-permute-start(bf16[1,32,2176]{2,1,0:T(8,128)(2,1)S(1)} %bitcast.12), channel_id=1, source_target_pairs={{0,8},{4,20},{8,0},{12,28},{16,24},{20,4},{24,16},{28,12},{1,9},{5... | collective-permute-start | bytes 417800 | tf_op jit(solution)/shard_map/ppermute | solution.py:316
  47.6 6.5 %collective-permute-start.24 = (bf16[1,32,2176]{2,1,0:T(8,128)(2,1)S(1)}, bf16[1,32,2176]{2,1,0:T(8,128)(2,1)S(1)}, u32[]{:S(2)}, u32[]{:S(2)}) collective-permute-start(bf16[1,32,2176]{2,1,0:T(8,128)(2,1)S(1)} %collective-permute-done.23.a_ref), channel_id=1, source_target_pairs={{0,8},{4,20},{8,0},{12,28},{16,24},{20,4},{24,16},{28,12},{1,9},{5... | collective-permute-start | bytes 417800 | tf_op jit(solution)/shard_map/ppermute | solution.py:316
  48.2 6.6 %collective-permute-start.12 = (bf16[2,32,2176]{2,1,0:T(8,128)(2,1)S(1)}, bf16[2,32,2176]{2,1,0:T(8,128)(2,1)S(1)}, u32[]{:S(2)}, u32[]{:S(2)}) collective-permute-start(bf16[2,32,2176]{2,1,0:T(8,128)(2,1)S(1)} %shard_map.122.a_ref), channel_id=1, source_target_pairs={{0,16},{4,12},{8,24},{12,4},{16,0},{20,28},{24,8},{28,20},{1,17},{... | collective-permute-start | bytes 835592 | tf_op jit(solution)/shard_map/ppermute | solution.py:316
  54.2 6.6 %collective-permute-start.25 = (bf16[2,32,2176]{2,1,0:T(8,128)(2,1)S(1)}, bf16[2,32,2176]{2,1,0:T(8,128)(2,1)S(1)}, u32[]{:S(2)}, u32[]{:S(2)}) collective-permute-start(bf16[2,32,2176]{2,1,0:T(8,128)(2,1)S(1)} %shard_map.132.a_ref), channel_id=1, source_target_pairs={{0,16},{4,12},{8,24},{12,4},{16,0},{20,28},{24,8},{28,20},{1,17},{... | collective-permute-start | bytes 835592 | tf_op jit(solution)/shard_map/ppermute | solution.py:316
  54.8 6.5 %collective-permute-start.31 = (bf16[1,32,2176]{2,1,0:T(8,128)(2,1)S(1)}, bf16[1,32,2176]{2,1,0:T(8,128)(2,1)S(1)}, u32[]{:S(2)}, u32[]{:S(2)}) collective-permute-start(bf16[1,32,2176]{2,1,0:T(8,128)(2,1)S(1)} %collective-permute-done.23.a_ref), channel_id=1, source_target_pairs={{0,1},{1,0},{2,3},{3,2},{4,5},{5,4},{6,7},{7,6},{8,9},{9,8},{10,11... | collective-permute-start | bytes 417800 | tf_op jit(solution)/shard_map/ppermute | solution.py:246
  54.9 18.3 %collective-permute-start.17 = (bf16[4,32,2176]{2,1,0:T(8,128)(2,1)S(1)}, bf16[4,32,2176]{2,1,0:T(8,128)(2,1)S(1)}, u32[]{:S(2)}, u32[]{:S(2)}) collective-permute-start(bf16[4,32,2176]{2,1,0:T(8,128)(2,1)S(1)} %shard_map.123.refs_1_), channel_id=1, source_target_pairs={{0,1},{1,0},{2,3},{3,2},{4,5},{5,4},{6,7},{7,6},{8,9},{9,8},{10,11... | collective-permute-start | bytes 1671176 | tf_op jit(solution)/shard_map/ppermute | solution.py:246
  56.9 16.7 %collective-permute-start.13 = (bf16[4,32,2176]{2,1,0:T(8,128)(2,1)S(1)}, bf16[4,32,2176]{2,1,0:T(8,128)(2,1)S(1)}, u32[]{:S(2)}, u32[]{:S(2)}) collective-permute-start(bf16[4,32,2176]{2,1,0:T(8,128)(2,1)S(1)} %shard_map.123.refs_1_), channel_id=1, source_target_pairs={{0,4},{4,0},{8,12},{12,8},{16,20},{20,16},{24,28},{28,24},{1,5},{5... | collective-permute-start | bytes 1671176 | tf_op jit(solution)/shard_map/ppermute | solution.py:243
  60.9 15.6 %collective-permute-start.26 = (bf16[4,32,2176]{2,1,0:T(8,128)(2,1)S(1)}, bf16[4,32,2176]{2,1,0:T(8,128)(2,1)S(1)}, u32[]{:S(2)}, u32[]{:S(2)}) collective-permute-start(bf16[4,32,2176]{2,1,0:T(8,128)(2,1)S(1)} %shard_map.133.refs_1_), channel_id=1, source_target_pairs={{0,4},{4,0},{8,12},{12,8},{16,20},{20,16},{24,28},{28,24},{1,5},{5... | collective-permute-start | bytes 1671176 | tf_op jit(solution)/shard_map/ppermute | solution.py:243
  61.3 5.1 %collective-permute-start.32 = (bf16[1,32,2176]{2,1,0:T(8,128)(2,1)S(1)}, bf16[1,32,2176]{2,1,0:T(8,128)(2,1)S(1)}, u32[]{:S(2)}, u32[]{:S(2)}) collective-permute-start(bf16[1,32,2176]{2,1,0:T(8,128)(2,1)S(1)} %collective-permute-done.31.a_ref), channel_id=1, source_target_pairs={{0,8},{4,20},{8,0},{12,28},{16,24},{20,4},{24,16},{28,12},{1,9},{5... | collective-permute-start | bytes 417800 | tf_op jit(solution)/shard_map/ppermute | solution.py:316
  66.4 6.6 %collective-permute-start.33 = (bf16[2,32,2176]{2,1,0:T(8,128)(2,1)S(1)}, bf16[2,32,2176]{2,1,0:T(8,128)(2,1)S(1)}, u32[]{:S(2)}, u32[]{:S(2)}) collective-permute-start(bf16[2,32,2176]{2,1,0:T(8,128)(2,1)S(1)} %shard_map.138.a_ref), channel_id=1, source_target_pairs={{0,16},{4,12},{8,24},{12,4},{16,0},{20,28},{24,8},{28,20},{1,17},{... | collective-permute-start | bytes 835592 | tf_op jit(solution)/shard_map/ppermute | solution.py:316
  73.1 6.5 %collective-permute-start.34 = (bf16[4,32,2176]{2,1,0:T(8,128)(2,1)S(1)}, bf16[4,32,2176]{2,1,0:T(8,128)(2,1)S(1)}, u32[]{:S(2)}, u32[]{:S(2)}) collective-permute-start(bf16[4,32,2176]{2,1,0:T(8,128)(2,1)S(1)} %shard_map.139.refs_1_), channel_id=1, source_target_pairs={{0,4},{4,0},{8,12},{12,8},{16,20},{20,16},{24,28},{28,24},{1,5},{5... | collective-permute-start | bytes 1671176 | tf_op jit(solution)/shard_map/ppermute | solution.py:243
  73.2 11.0 %collective-permute-start.18 = (bf16[4,32,2176]{2,1,0:T(8,128)(2,1)S(1)}, bf16[4,32,2176]{2,1,0:T(8,128)(2,1)S(1)}, u32[]{:S(2)}, u32[]{:S(2)}) collective-permute-start(bf16[4,32,2176]{2,1,0:T(8,128)(2,1)S(1)} %collective-permute-done.17.refs_1_), channel_id=1, source_target_pairs={{0,4},{4,0},{8,12},{12,8},{16,20},{20,16},{24,28},{28,24},{1,5},{5... | collective-permute-start | bytes 1671176 | tf_op jit(solution)/shard_map/ppermute | solution.py:243
  76.3 6.1 %collective-permute-start.14 = (bf16[4,32,2048]{2,1,0:T(8,128)(2,1)S(1)}, bf16[4,32,2048]{2,1,0:T(8,128)(2,1)S(1)}, u32[]{:S(2)}, u32[]{:S(2)}) collective-permute-start(bf16[4,32,2048]{2,1,0:T(8,128)(2,1)S(1)} %get-tuple-element.67), channel_id=1, source_target_pairs={{0,4},{4,0},{8,12},{12,8},{16,20},{20,16},{24,28},{28,24},{1,5},{5... | collective-permute-start | bytes 1572872 | tf_op jit(solution)/shard_map/ppermute | solution.py:243
  79.1 8.1 %collective-permute-start.27 = (bf16[4,32,2048]{2,1,0:T(8,128)(2,1)S(1)}, bf16[4,32,2048]{2,1,0:T(8,128)(2,1)S(1)}, u32[]{:S(2)}, u32[]{:S(2)}) collective-permute-start(bf16[4,32,2048]{2,1,0:T(8,128)(2,1)S(1)} %get-tuple-element.81), channel_id=1, source_target_pairs={{0,4},{4,0},{8,12},{12,8},{16,20},{20,16},{24,28},{28,24},{1,5},{5... | collective-permute-start | bytes 1572872 | tf_op jit(solution)/shard_map/ppermute | solution.py:243
  82.3 5.7 %collective-permute-start.35 = (bf16[4,32,2048]{2,1,0:T(8,128)(2,1)S(1)}, bf16[4,32,2048]{2,1,0:T(8,128)(2,1)S(1)}, u32[]{:S(2)}, u32[]{:S(2)}) collective-permute-start(bf16[4,32,2048]{2,1,0:T(8,128)(2,1)S(1)} %get-tuple-element.88), channel_id=1, source_target_pairs={{0,4},{4,0},{8,12},{12,8},{16,20},{20,16},{24,28},{28,24},{1,5},{5... | collective-permute-start | bytes 1572872 | tf_op jit(solution)/shard_map/ppermute | solution.py:243
  82.5 23.6 %collective-permute-start.15 = (bf16[2,32,2048]{2,1,0:T(8,128)(2,1)S(1)}, bf16[2,32,2048]{2,1,0:T(8,128)(2,1)S(1)}, u32[]{:S(2)}, u32[]{:S(2)}) collective-permute-start(bf16[2,32,2048]{2,1,0:T(8,128)(2,1)S(1)} %get-tuple-element.69), channel_id=1, source_target_pairs={{0,16},{4,12},{8,24},{12,4},{16,0},{20,28},{24,8},{28,20},{1,17},{... | collective-permute-start | bytes 786440 | tf_op jit(solution)/shard_map/ppermute | solution.py:316
  87.0 10.8 %collective-permute-start.19 = (bf16[4,32,2048]{2,1,0:T(8,128)(2,1)S(1)}, bf16[4,32,2048]{2,1,0:T(8,128)(2,1)S(1)}, u32[]{:S(2)}, u32[]{:S(2)}) collective-permute-start(bf16[4,32,2048]{2,1,0:T(8,128)(2,1)S(1)} %get-tuple-element.74), channel_id=1, source_target_pairs={{0,4},{4,0},{8,12},{12,8},{16,20},{20,16},{24,28},{28,24},{1,5},{5... | collective-permute-start | bytes 1572872 | tf_op jit(solution)/shard_map/ppermute | solution.py:243
  87.4 6.4 %collective-permute-start.28 = (bf16[2,32,2048]{2,1,0:T(8,128)(2,1)S(1)}, bf16[2,32,2048]{2,1,0:T(8,128)(2,1)S(1)}, u32[]{:S(2)}, u32[]{:S(2)}) collective-permute-start(bf16[2,32,2048]{2,1,0:T(8,128)(2,1)S(1)} %get-tuple-element.83), channel_id=1, source_target_pairs={{0,16},{4,12},{8,24},{12,4},{16,0},{20,28},{24,8},{28,20},{1,17},{... | collective-permute-start | bytes 786440 | tf_op jit(solution)/shard_map/ppermute | solution.py:316
  88.1 9.2 %collective-permute-start.36 = (bf16[2,32,2048]{2,1,0:T(8,128)(2,1)S(1)}, bf16[2,32,2048]{2,1,0:T(8,128)(2,1)S(1)}, u32[]{:S(2)}, u32[]{:S(2)}) collective-permute-start(bf16[2,32,2048]{2,1,0:T(8,128)(2,1)S(1)} %get-tuple-element.90), channel_id=1, source_target_pairs={{0,16},{4,12},{8,24},{12,4},{16,0},{20,28},{24,8},{28,20},{1,17},{... | collective-permute-start | bytes 786440 | tf_op jit(solution)/shard_map/ppermute | solution.py:316
  93.9 12.8 %collective-permute-start.29 = (bf16[1,32,2048]{2,1,0:T(8,128)(2,1)S(1)}, bf16[1,32,2048]{2,1,0:T(8,128)(2,1)S(1)}, u32[]{:S(2)}, u32[]{:S(2)}) collective-permute-start(bf16[1,32,2048]{2,1,0:T(8,128)(2,1)S(1)} %get-tuple-element.85), channel_id=1, source_target_pairs={{0,8},{4,20},{8,0},{12,28},{16,24},{20,4},{24,16},{28,12},{1,9},{5... | collective-permute-start | bytes 393224 | tf_op jit(solution)/shard_map/ppermute | solution.py:316
  97.3 9.9 %collective-permute-start.37 = (bf16[1,32,2048]{2,1,0:T(8,128)(2,1)S(1)}, bf16[1,32,2048]{2,1,0:T(8,128)(2,1)S(1)}, u32[]{:S(2)}, u32[]{:S(2)}) collective-permute-start(bf16[1,32,2048]{2,1,0:T(8,128)(2,1)S(1)} %get-tuple-element.92), channel_id=1, source_target_pairs={{0,8},{4,20},{8,0},{12,28},{16,24},{20,4},{24,16},{28,12},{1,9},{5... | collective-permute-start | bytes 393224 | tf_op jit(solution)/shard_map/ppermute | solution.py:316
  97.9 6.4 %collective-permute-start.20 = (bf16[2,32,2048]{2,1,0:T(8,128)(2,1)S(1)}, bf16[2,32,2048]{2,1,0:T(8,128)(2,1)S(1)}, u32[]{:S(2)}, u32[]{:S(2)}) collective-permute-start(bf16[2,32,2048]{2,1,0:T(8,128)(2,1)S(1)} %get-tuple-element.76), channel_id=1, source_target_pairs={{0,16},{4,12},{8,24},{12,4},{16,0},{20,28},{24,8},{28,20},{1,17},{... | collective-permute-start | bytes 786440 | tf_op jit(solution)/shard_map/ppermute | solution.py:316
  104.4 5.0 %collective-permute-start.21 = (bf16[1,32,2048]{2,1,0:T(8,128)(2,1)S(1)}, bf16[1,32,2048]{2,1,0:T(8,128)(2,1)S(1)}, u32[]{:S(2)}, u32[]{:S(2)}) collective-permute-start(bf16[1,32,2048]{2,1,0:T(8,128)(2,1)S(1)} %get-tuple-element.78), channel_id=1, source_target_pairs={{0,8},{4,20},{8,0},{12,28},{16,24},{20,4},{24,16},{28,12},{1,9},{5... | collective-permute-start | bytes 393224 | tf_op jit(solution)/shard_map/ppermute | solution.py:316
  106.2 5.0 %collective-permute-start.16 = (bf16[1,32,2048]{2,1,0:T(8,128)(2,1)S(1)}, bf16[1,32,2048]{2,1,0:T(8,128)(2,1)S(1)}, u32[]{:S(2)}, u32[]{:S(2)}) collective-permute-start(bf16[1,32,2048]{2,1,0:T(8,128)(2,1)S(1)} %get-tuple-element.71), channel_id=1, source_target_pairs={{0,8},{4,20},{8,0},{12,28},{16,24},{20,4},{24,16},{28,12},{1,9},{5... | collective-permute-start | bytes 393224 | tf_op jit(solution)/shard_map/ppermute | solution.py:316
  106.7 10.3 %collective-permute-start.30 = (bf16[1,32,2048]{2,1,0:T(8,128)(2,1)S(1)}, bf16[1,32,2048]{2,1,0:T(8,128)(2,1)S(1)}, u32[]{:S(2)}, u32[]{:S(2)}) collective-permute-start(bf16[1,32,2048]{2,1,0:T(8,128)(2,1)S(1)} %shard_map.137), channel_id=1, source_target_pairs={{0,2},{1,3},{2,0},{3,1},{4,6},{5,7},{6,4},{7,5},{8,10},{9,11},{10,... | collective-permute-start | bytes 393224 | tf_op jit(solution)/shard_map/ppermute | solution.py:246
  107.2 9.8 %collective-permute-start.38 = (bf16[1,32,2048]{2,1,0:T(8,128)(2,1)S(1)}, bf16[1,32,2048]{2,1,0:T(8,128)(2,1)S(1)}, u32[]{:S(2)}, u32[]{:S(2)}) collective-permute-start(bf16[1,32,2048]{2,1,0:T(8,128)(2,1)S(1)} %shard_map.143), channel_id=1, source_target_pairs={{0,3},{1,2},{2,1},{3,0},{4,7},{5,6},{6,5},{7,4},{8,11},{9,10},{10,... | collective-permute-start | bytes 393224 | tf_op jit(solution)/shard_map/ppermute | solution.py:246
  109.5 8.5 %collective-permute-start.22 = (bf16[1,32,2048]{2,1,0:T(8,128)(2,1)S(1)}, bf16[1,32,2048]{2,1,0:T(8,128)(2,1)S(1)}, u32[]{:S(2)}, u32[]{:S(2)}) collective-permute-start(bf16[1,32,2048]{2,1,0:T(8,128)(2,1)S(1)} %shard_map.131), channel_id=1, source_target_pairs={{0,1},{1,0},{2,3},{3,2},{4,5},{5,4},{6,7},{7,6},{8,9},{9,8},{10,11... | collective-permute-start | bytes 393224 | tf_op jit(solution)/shard_map/ppermute | solution.py:246

commit v3 on v2

--- a/solution.py
+++ b/solution.py
@@ -31,6 +31,16 @@
 
 def xor_swap(count, mask):
     return [(i, i ^ mask) for i in range(count)]
+
+
+def fetch_kernel(*refs):
+    count = len(refs) // 2
+    sems = refs[2 * count]
+    copies = [pltpu.make_async_copy(refs[i], refs[count + i], sems.at[i]) for i in range(count)]
+    for copy in copies:
+        copy.start()
+    for copy in copies:
+        copy.wait()
 
 
 def load_kernel(seq_count, exp_count, expert_count, picks_ref, routes_ref, gates_ref, *refs):
@@ -265,20 +275,29 @@
         up_weight.transpose(0, 2, 1).reshape(local * hidden_units, width),
         down_weight.reshape(local * hidden_units, width),
     ]
-    shapes = [jax.ShapeDtypeStruct(a.shape, a.dtype) for a in loaded]
+    near = loaded[:3]
+    shapes = [jax.ShapeDtypeStruct(a.shape, a.dtype) for a in near]
     shapes[0] = jax.ShapeDtypeStruct((share, width), residual.dtype)
     shapes.append(jax.ShapeDtypeStruct((1, seq_count * tok_rows), jnp.int32))
     shapes.append(jax.ShapeDtypeStruct((share, gate_columns), bf16))
-    residual_rows, gain, out_proj, gate_t, up_t, down, key_pos, gates = call(
+    weights = [pltpu.with_memory_space_constraint(a, HBM) for a in loaded[3:]]
+    gate_t, up_t, down = call(
+        fetch_kernel,
+        tuple(jax.ShapeDtypeStruct(a.shape, a.dtype) for a in weights),
+        [HBM] * len(weights),
+        24,
+        [pltpu.SemaphoreType.DMA((len(weights),))],
+    )(*weights)
+    residual_rows, gain, out_proj, key_pos, gates = call(
         functools.partial(load_kernel, seq_count, exp_count, expert_count),
         tuple(shapes),
-        [SMEM, VMEM, VMEM] + [HBM] * len(loaded),
+        [SMEM, VMEM, VMEM] + [HBM] * len(near),
         24,
         [
             pltpu.VMEM((tok_rows, gate_columns), f32),
-            pltpu.SemaphoreType.DMA((len(loaded),)),
+            pltpu.SemaphoreType.DMA((len(near),)),
         ],
-    )(block_picks, routes.T, route_gates.T, *[pltpu.with_memory_space_constraint(a, HBM) for a in loaded])
+    )(block_picks, routes.T, route_gates.T, *[pltpu.with_memory_space_constraint(a, HBM) for a in near])
 
     half_shape = jax.ShapeDtypeStruct((tok_rows, half_width), bf16)
     attended, partner_attended = call(

time: 119 us -> 122 us (1.025)
    pallas_call x0 -> x1, Pallas kernels: none -> 3.57 us  [per_device(): call(fetch_kernel, tuple((jax.ShapeDtypeStruct(a.shape, a.dtype) for a in...]
    pallas_call x1, Pallas kernels: 4.85 us -> 2.28 us  [per_device(): call(functools.partial(load_kernel, seq_count, exp_count, expert_count),...]
    ppermute x16, waiting for transfers between devices: 1.65 us -> 3.22 us  [seq_send(): return lax.ppermute(a, 'seq', xor_swap(seq_count, mask))]
  transfers between devices with their start and end apart: 39 -> 39, of which waited for: 17 -> 18; matrix products, arithmetic and copies ran while one was open for 1% -> 1% of each run, Pallas kernels for 14% -> 15%
where the time goes in v3:
time: 122 us
  waiting for transfers between devices  55 us (45%)
  starting transfers between devices  42.3 us (35%)
  Pallas kernels  20.5 us (17%)
  local copies, waits for them, and re-layouts  3.97 us (3%)
    ppermute x14, waiting for transfers between devices, lane_send(): return lax.ppermute(a, 'seq', pairs)  29.4 us
    ppermute x9, waiting for transfers between devices, exp_send(): return lax.ppermute(a, 'exp', xor_swap(exp_count, by))  22.4 us
    ppermute x14, starting transfers between devices, lane_send(): return lax.ppermute(a, 'seq', pairs)  15.3 us
    ppermute x9, starting transfers between devices, exp_send(): return lax.ppermute(a, 'exp', xor_swap(exp_count, by))  13.6 us
    ppermute x16, starting transfers between devices, seq_send(): return lax.ppermute(a, 'seq', xor_swap(seq_count, mask))  13.4 us
    pallas_call x4, Pallas kernels, mlp(): call(functools.partial(expert_kernel, expert_count, local, 2), tuple((jax...  10.8 us
    pallas_call x1, Pallas kernels, per_device(): call(fetch_kernel, tuple((jax.ShapeDtypeStruct(a.shape, a.dtype) for a in...  3.57 us
    ppermute x16, waiting for transfers between devices, seq_send(): return lax.ppermute(a, 'seq', xor_swap(seq_count, mask))  3.22 us
  transfers between devices with their start and end apart: 39, of which 18 were waited for; matrix products, arithmetic and copies ran while one was open for 1% of the time, Pallas kernels for 15%

profile of v3, /device:TPU:0, one launch (start us, length us, event | category | flops | bytes accessed | tf_op | source)
XLA Modules:
  0.0 122.0 jit_solution(2785207707347154768)
XLA Ops:
  0.0 1.0 constant_dynamic-slice_fusion.1
  1.0 3.0 %collective-permute-start.1 = (bf16[128,512]{1,0:T(8,128)(2,1)S(1)}, bf16[128,512]{1,0:T(8,128)(2,1)S(1)}, u32[]{:S(2)}, u32[]{:S(2)}) collective-permute-start(bf16[128,512]{1,0:T(8,128)(2,1)S(1)} %pad_maximum_fusion.1.refs_0_), channel_id=1, source_target_pairs={{0,8},{4,12},{8,0},{12,4},{16,24},{20,28},{24,16},{28,20},{1,9},{5... | collective-permute-start | bytes 393224 | tf_op jit(solution)/shard_map/ppermute | solution.py:253
  4.1 0.9 constant_dynamic-slice_fusion
  5.0 0.2 collective-permute-start
  5.2 2.0 %collective-permute-start.3 = (bf16[128,512]{1,0:T(8,128)(2,1)S(1)}, bf16[128,512]{1,0:T(8,128)(2,1)S(1)}, u32[]{:S(2)}, u32[]{:S(2)}) collective-permute-start(bf16[128,512]{1,0:T(8,128)(2,1)S(1)} %pad_maximum_fusion.1.refs_0_), channel_id=1, source_target_pairs={{0,16},{4,20},{8,24},{12,28},{16,0},{20,4},{24,8},{28,12},{1,17},{... | collective-permute-start | bytes 393224 | tf_op jit(solution)/shard_map/ppermute | solution.py:253
  7.2 0.7 collective-permute-done.1.refs_2_
  7.9 3.4 %collective-permute-start.5 = (bf16[128,512]{1,0:T(8,128)(2,1)S(1)}, bf16[128,512]{1,0:T(8,128)(2,1)S(1)}, u32[]{:S(2)}, u32[]{:S(2)}) collective-permute-start(bf16[128,512]{1,0:T(8,128)(2,1)S(1)} %pad_maximum_fusion.1.refs_0_), channel_id=1, source_target_pairs={{0,24},{4,28},{8,16},{12,20},{16,8},{20,12},{24,0},{28,4},{1,25},{... | collective-permute-start | bytes 393224 | tf_op jit(solution)/shard_map/ppermute | solution.py:253
  11.3 1.6 %collective-permute-start.6 = (bf16[128,512]{1,0:T(8,128)(2,1)S(1)}, bf16[128,512]{1,0:T(8,128)(2,1)S(1)}, u32[]{:S(2)}, u32[]{:S(2)}) collective-permute-start(bf16[128,512]{1,0:T(8,128)(2,1)S(1)} %pad_maximum_fusion.2), channel_id=1, source_target_pairs={{0,28},{4,24},{8,20},{12,16},{16,12},{20,8},{24,4},{28,0},{1,29},{... | collective-permute-start | bytes 393224 | tf_op jit(solution)/shard_map/ppermute | solution.py:253
  12.9 0.7 copy-done
  13.6 0.7 copy-done.1
  14.3 0.7 copy-done.2
  15.0 2.3 %shard_map.118 = (bf16[32,2048]{1,0:T(8,128)(2,1)S(1)}, f32[1,2048]{1,0:T(1,128)S(1)}, bf16[512,2048]{1,0:T(8,128)(2,1)S(1)}, s32[1,1024]{1,0:T(1,128)S(1)}, bf16[32,128]{1,0:T(8,128)(2,1)S(1)}) custom-call(s32[2,3]{1,0:T(2,128)S(1)} %copy-done.2, s32[6,128]{1,0:T(8,128)S(1)} %bitcast.14, f32[6,128]{1,0:T(8,128)S(1)} %bitcast.15, bf16[128,2048]{1,0:T(8,128)(2,1)} %refs_0_.1, ...), custom_call_target="tpu_custom_call" | custom-call | tf_op jit(solution)/shard_map/pallas_call | solution.py:291
  17.3 1.6 %collective-permute-done.4.refs_5_ = bf16[128,512]{1,0:T(8,128)(2,1)S(1)} collective-permute-done((bf16[128,512]{1,0:T(8,128)(2,1)S(1)}, bf16[128,512]{1,0:T(8,128)(2,1)S(1)}, u32[]{:S(2)}, u32[]{:S(2)}) %collective-permute-start.4) | collective-permute-done | bytes 131104 | tf_op jit(solution)/shard_map/ppermute | solution.py:253
  18.8 1.4 %shard_map.119 = (bf16[128,256]{1,0:T(8,128)(2,1)S(1)}, bf16[128,256]{1,0:T(8,128)(2,1)S(1)}) custom-call(s32[1,1024]{1,0:T(1,128)S(1)} %get-tuple-element.49.key_ref, bf16[128,256]{1,0:T(8,128)(2,1)S(1)} %get-tuple-element.106.own_ref, bf16[128,512]{1,0:T(8,128)(2,1)S(1)} %pad_maximum_fusion.1.refs_0_, bf16[128,768]{1,0:T(8,128)(2,1)S(1)} %collective-permute-done.refs_1_, ...), custom_call_target="tpu_custom_call" | custom-call | tf_op jit(solution)/shard_map/pallas_call | solution.py:303
  20.3 0.5 collective-permute-start.7
  20.8 0.9 collective-permute-done.7.other_ref
  21.7 0.4 shard_map.120
  22.1 1.8 %collective-permute-start.8 = (bf16[32,2048]{1,0:T(8,128)(2,1)S(1)}, bf16[32,2048]{1,0:T(8,128)(2,1)S(1)}, u32[]{:S(2)}, u32[]{:S(2)}) collective-permute-start(bf16[32,2048]{1,0:T(8,128)(2,1)S(1)} %get-tuple-element.54), channel_id=1, source_target_pairs={{0,1},{1,0},{2,3},{3,2},{4,5},{5,4},{6,7},{7,6},{8,9},{9,8},{10,11... | collective-permute-start | bytes 393224 | tf_op jit(solution)/shard_map/ppermute | solution.py:256
  24.0 2.6 %collective-permute-start.9 = (bf16[32,2048]{1,0:T(8,128)(2,1)S(1)}, bf16[32,2048]{1,0:T(8,128)(2,1)S(1)}, u32[]{:S(2)}, u32[]{:S(2)}) collective-permute-start(bf16[32,2048]{1,0:T(8,128)(2,1)S(1)} %get-tuple-element.55), channel_id=1, source_target_pairs={{0,2},{1,3},{2,0},{3,1},{4,6},{5,7},{6,4},{7,5},{8,10},{9,11},{10,... | collective-permute-start | bytes 393224 | tf_op jit(solution)/shard_map/ppermute | solution.py:256
  26.6 3.5 %collective-permute-done.8.refs_0_ = bf16[32,2048]{1,0:T(8,128)(2,1)S(1)} collective-permute-done((bf16[32,2048]{1,0:T(8,128)(2,1)S(1)}, bf16[32,2048]{1,0:T(8,128)(2,1)S(1)}, u32[]{:S(2)}, u32[]{:S(2)}) %collective-permute-start.8) | collective-permute-done | bytes 131104 | tf_op jit(solution)/shard_map/ppermute | solution.py:256
  30.0 6.9 %collective-permute-done.9.refs_1_ = bf16[32,2048]{1,0:T(8,128)(2,1)S(1)} collective-permute-done((bf16[32,2048]{1,0:T(8,128)(2,1)S(1)}, bf16[32,2048]{1,0:T(8,128)(2,1)S(1)}, u32[]{:S(2)}, u32[]{:S(2)}) %collective-permute-start.9) | collective-permute-done | bytes 131104 | tf_op jit(solution)/shard_map/ppermute | solution.py:256
  36.9 0.2 shard_map.121
  37.1 3.6 %collective-permute-start.23 = (bf16[1,32,2176]{2,1,0:T(8,128)(2,1)S(1)}, bf16[1,32,2176]{2,1,0:T(8,128)(2,1)S(1)}, u32[]{:S(2)}, u32[]{:S(2)}) collective-permute-start(bf16[1,32,2176]{2,1,0:T(8,128)(2,1)S(1)} %bitcast.11), channel_id=1, source_target_pairs={{0,2},{1,3},{2,0},{3,1},{4,6},{5,7},{6,4},{7,5},{8,10},{9,11},{10,... | collective-permute-start | bytes 417800 | tf_op jit(solution)/shard_map/ppermute | solution.py:256
  40.6 1.5 %collective-permute-start.11 = (bf16[1,32,2176]{2,1,0:T(8,128)(2,1)S(1)}, bf16[1,32,2176]{2,1,0:T(8,128)(2,1)S(1)}, u32[]{:S(2)}, u32[]{:S(2)}) collective-permute-start(bf16[1,32,2176]{2,1,0:T(8,128)(2,1)S(1)} %bitcast.12), channel_id=1, source_target_pairs={{0,8},{4,20},{8,0},{12,28},{16,24},{20,4},{24,16},{28,12},{1,9},{5... | collective-permute-start | bytes 417800 | tf_op jit(solution)/shard_map/ppermute | solution.py:335
  42.1 4.6 %collective-permute-done.23.a_ref = bf16[1,32,2176]{2,1,0:T(8,128)(2,1)S(1)} collective-permute-done((bf16[1,32,2176]{2,1,0:T(8,128)(2,1)S(1)}, bf16[1,32,2176]{2,1,0:T(8,128)(2,1)S(1)}, u32[]{:S(2)}, u32[]{:S(2)}) %collective-permute-start.23) | collective-permute-done | bytes 139296 | tf_op jit(solution)/shard_map/ppermute | solution.py:256
  46.7 1.5 %collective-permute-start.24 = (bf16[1,32,2176]{2,1,0:T(8,128)(2,1)S(1)}, bf16[1,32,2176]{2,1,0:T(8,128)(2,1)S(1)}, u32[]{:S(2)}, u32[]{:S(2)}) collective-permute-start(bf16[1,32,2176]{2,1,0:T(8,128)(2,1)S(1)} %collective-permute-done.23.a_ref), channel_id=1, source_target_pairs={{0,8},{4,20},{8,0},{12,28},{16,24},{20,4},{24,16},{28,12},{1,9},{5... | collective-permute-start | bytes 417800 | tf_op jit(solution)/shard_map/ppermute | solution.py:335
  48.2 1.6 %collective-permute-start.12 = (bf16[2,32,2176]{2,1,0:T(8,128)(2,1)S(1)}, bf16[2,32,2176]{2,1,0:T(8,128)(2,1)S(1)}, u32[]{:S(2)}, u32[]{:S(2)}) collective-permute-start(bf16[2,32,2176]{2,1,0:T(8,128)(2,1)S(1)} %shard_map.122.a_ref), channel_id=1, source_target_pairs={{0,16},{4,12},{8,24},{12,4},{16,0},{20,28},{24,8},{28,20},{1,17},{... | collective-permute-start | bytes 835592 | tf_op jit(solution)/shard_map/ppermute | solution.py:335
  49.8 3.4 %collective-permute-done.24.b_ref = bf16[1,32,2176]{2,1,0:T(8,128)(2,1)S(1)} collective-permute-done((bf16[1,32,2176]{2,1,0:T(8,128)(2,1)S(1)}, bf16[1,32,2176]{2,1,0:T(8,128)(2,1)S(1)}, u32[]{:S(2)}, u32[]{:S(2)}) %collective-permute-start.24) | collective-permute-done | bytes 139296 | tf_op jit(solution)/shard_map/ppermute | solution.py:335
  53.3 1.6 %collective-permute-start.25 = (bf16[2,32,2176]{2,1,0:T(8,128)(2,1)S(1)}, bf16[2,32,2176]{2,1,0:T(8,128)(2,1)S(1)}, u32[]{:S(2)}, u32[]{:S(2)}) collective-permute-start(bf16[2,32,2176]{2,1,0:T(8,128)(2,1)S(1)} %shard_map.133.a_ref), channel_id=1, source_target_pairs={{0,16},{4,12},{8,24},{12,4},{16,0},{20,28},{24,8},{28,20},{1,17},{... | collective-permute-start | bytes 835592 | tf_op jit(solution)/shard_map/ppermute | solution.py:335
  54.9 2.1 %collective-permute-start.17 = (bf16[4,32,2176]{2,1,0:T(8,128)(2,1)S(1)}, bf16[4,32,2176]{2,1,0:T(8,128)(2,1)S(1)}, u32[]{:S(2)}, u32[]{:S(2)}) collective-permute-start(bf16[4,32,2176]{2,1,0:T(8,128)(2,1)S(1)} %shard_map.123.refs_1_), channel_id=1, source_target_pairs={{0,1},{1,0},{2,3},{3,2},{4,5},{5,4},{6,7},{7,6},{8,9},{9,8},{10,11... | collective-permute-start | bytes 1671176 | tf_op jit(solution)/shard_map/ppermute | solution.py:256
  57.0 2.9 %collective-permute-done.25.b_ref = bf16[2,32,2176]{2,1,0:T(8,128)(2,1)S(1)} collective-permute-done((bf16[2,32,2176]{2,1,0:T(8,128)(2,1)S(1)}, bf16[2,32,2176]{2,1,0:T(8,128)(2,1)S(1)}, u32[]{:S(2)}, u32[]{:S(2)}) %collective-permute-start.25) | collective-permute-done | bytes 278560 | tf_op jit(solution)/shard_map/ppermute | solution.py:335
  60.0 1.4 %collective-permute-done.31.a_ref = bf16[1,32,2176]{2,1,0:T(8,128)(2,1)S(1)} collective-permute-done((bf16[1,32,2176]{2,1,0:T(8,128)(2,1)S(1)}, bf16[1,32,2176]{2,1,0:T(8,128)(2,1)S(1)}, u32[]{:S(2)}, u32[]{:S(2)}) %collective-permute-start.31) | collective-permute-done | bytes 139296 | tf_op jit(solution)/shard_map/ppermute | solution.py:256
  61.4 1.5 %collective-permute-start.32 = (bf16[1,32,2176]{2,1,0:T(8,128)(2,1)S(1)}, bf16[1,32,2176]{2,1,0:T(8,128)(2,1)S(1)}, u32[]{:S(2)}, u32[]{:S(2)}) collective-permute-start(bf16[1,32,2176]{2,1,0:T(8,128)(2,1)S(1)} %collective-permute-done.31.a_ref), channel_id=1, source_target_pairs={{0,8},{4,20},{8,0},{12,28},{16,24},{20,4},{24,16},{28,12},{1,9},{5... | collective-permute-start | bytes 417800 | tf_op jit(solution)/shard_map/ppermute | solution.py:335
  62.9 3.5 %collective-permute-done.32.b_ref = bf16[1,32,2176]{2,1,0:T(8,128)(2,1)S(1)} collective-permute-done((bf16[1,32,2176]{2,1,0:T(8,128)(2,1)S(1)}, bf16[1,32,2176]{2,1,0:T(8,128)(2,1)S(1)}, u32[]{:S(2)}, u32[]{:S(2)}) %collective-permute-start.32) | collective-permute-done | bytes 139296 | tf_op jit(solution)/shard_map/ppermute | solution.py:335
  66.4 0.6 collective-permute-start.33
  67.0 6.0 %collective-permute-done.33.b_ref = bf16[2,32,2176]{2,1,0:T(8,128)(2,1)S(1)} collective-permute-done((bf16[2,32,2176]{2,1,0:T(8,128)(2,1)S(1)}, bf16[2,32,2176]{2,1,0:T(8,128)(2,1)S(1)}, u32[]{:S(2)}, u32[]{:S(2)}) %collective-permute-start.33) | collective-permute-done | bytes 278560 | tf_op jit(solution)/shard_map/ppermute | solution.py:335
  73.2 0.5 collective-permute-start.18
  73.7 3.6 %shard_map.124 = (bf16[704,2048]{1,0:T(8,128)(2,1)S(1)}, bf16[704,2048]{1,0:T(8,128)(2,1)S(1)}, bf16[704,2048]{1,0:T(8,128)(2,1)S(1)}) custom-call(bf16[704,2048]{1,0:T(8,128)(2,1)} %bitcast.16, bf16[704,2048]{1,0:T(8,128)(2,1)} %bitcast.17, bf16[704,2048]{1,0:T(8,128)(2,1)} %bitcast.18), custom_call_target="tpu_custom_call" | custom-call | tf_op jit(solution)/shard_map/pallas_call | solution.py:284
  77.3 2.7 %shard_map.125 = (bf16[4,32,2048]{2,1,0:T(8,128)(2,1)S(1)}, bf16[2,32,2048]{2,1,0:T(8,128)(2,1)S(1)}, bf16[2,32,2048]{2,1,0:T(8,128)(2,1)S(1)}) custom-call(bf16[4,32,2176]{2,1,0:T(8,128)(2,1)S(1)} %collective-permute-done.13.refs_0_, bf16[4,32,2176]{2,1,0:T(8,128)(2,1)S(1)} %shard_map.123.refs_1_, bf16[704,2048]{1,0:T(8,128)(2,1)S(1)} %get-tuple-element.62.refs_2_, ...), custom_call_target="tpu_custom_call" | custom-call | tf_op jit(solution)/shard_map/pallas_call | solution.py:346
  80.1 2.6 %shard_map.135 = (bf16[4,32,2048]{2,1,0:T(8,128)(2,1)S(1)}, bf16[2,32,2048]{2,1,0:T(8,128)(2,1)S(1)}, bf16[2,32,2048]{2,1,0:T(8,128)(2,1)S(1)}) custom-call(bf16[4,32,2176]{2,1,0:T(8,128)(2,1)S(1)} %collective-permute-done.26.refs_0_, bf16[4,32,2176]{2,1,0:T(8,128)(2,1)S(1)} %shard_map.134.refs_1_, bf16[704,2048]{1,0:T(8,128)(2,1)S(1)} %get-tuple-element.62.refs_2_, ...), custom_call_target="tpu_custom_call" | custom-call | tf_op jit(solution)/shard_map/pallas_call | solution.py:346
  82.7 0.5 collective-permute-start.27
  83.2 2.6 %shard_map.141 = (bf16[4,32,2048]{2,1,0:T(8,128)(2,1)S(1)}, bf16[2,32,2048]{2,1,0:T(8,128)(2,1)S(1)}, bf16[2,32,2048]{2,1,0:T(8,128)(2,1)S(1)}) custom-call(bf16[4,32,2176]{2,1,0:T(8,128)(2,1)S(1)} %collective-permute-done.34.refs_0_, bf16[4,32,2176]{2,1,0:T(8,128)(2,1)S(1)} %shard_map.140.refs_1_, bf16[704,2048]{1,0:T(8,128)(2,1)S(1)} %get-tuple-element.62.refs_2_, ...), custom_call_target="tpu_custom_call" | custom-call | tf_op jit(solution)/shard_map/pallas_call | solution.py:346
  85.9 0.1 collective-permute-start.35
  86.1 0.6 collective-permute-start.15
  86.8 2.8 %shard_map.129 = (bf16[4,32,2048]{2,1,0:T(8,128)(2,1)S(1)}, bf16[2,32,2048]{2,1,0:T(8,128)(2,1)S(1)}, bf16[2,32,2048]{2,1,0:T(8,128)(2,1)S(1)}) custom-call(bf16[4,32,2176]{2,1,0:T(8,128)(2,1)S(1)} %collective-permute-done.18.refs_0_, bf16[4,32,2176]{2,1,0:T(8,128)(2,1)S(1)} %collective-permute-done.17.refs_1_, ...), custom_call_target="tpu_custom_call" | custom-call | tf_op jit(solution)/shard_map/pallas_call | solution.py:346
  89.6 1.2 collective-permute-start.19
  91.0 0.5 collective-permute-start.28
  91.6 1.6 %collective-permute-start.36 = (bf16[2,32,2048]{2,1,0:T(8,128)(2,1)S(1)}, bf16[2,32,2048]{2,1,0:T(8,128)(2,1)S(1)}, u32[]{:S(2)}, u32[]{:S(2)}) collective-permute-start(bf16[2,32,2048]{2,1,0:T(8,128)(2,1)S(1)} %get-tuple-element.90), channel_id=1, source_target_pairs={{0,16},{4,12},{8,24},{12,4},{16,0},{20,28},{24,8},{28,20},{1,17},{... | collective-permute-start | bytes 786440 | tf_op jit(solution)/shard_map/ppermute | solution.py:335
  93.3 4.1 %collective-permute-done.28.refs_2_ = bf16[2,32,2048]{2,1,0:T(8,128)(2,1)S(1)} collective-permute-done((bf16[2,32,2048]{2,1,0:T(8,128)(2,1)S(1)}, bf16[2,32,2048]{2,1,0:T(8,128)(2,1)S(1)}, u32[]{:S(2)}, u32[]{:S(2)}) %collective-permute-start.28) | collective-permute-done | bytes 262176 | tf_op jit(solution)/shard_map/ppermute | solution.py:335
  97.5 0.6 collective-permute-start.29
  98.0 3.1 %collective-permute-done.36.refs_2_ = bf16[2,32,2048]{2,1,0:T(8,128)(2,1)S(1)} collective-permute-done((bf16[2,32,2048]{2,1,0:T(8,128)(2,1)S(1)}, bf16[2,32,2048]{2,1,0:T(8,128)(2,1)S(1)}, u32[]{:S(2)}, u32[]{:S(2)}) %collective-permute-start.36) | collective-permute-done | bytes 262176 | tf_op jit(solution)/shard_map/ppermute | solution.py:335
  101.2 0.3 collective-permute-start.37
  101.6 1.3 %collective-permute-start.20 = (bf16[2,32,2048]{2,1,0:T(8,128)(2,1)S(1)}, bf16[2,32,2048]{2,1,0:T(8,128)(2,1)S(1)}, u32[]{:S(2)}, u32[]{:S(2)}) collective-permute-start(bf16[2,32,2048]{2,1,0:T(8,128)(2,1)S(1)} %get-tuple-element.76), channel_id=1, source_target_pairs={{0,16},{4,12},{8,24},{12,4},{16,0},{20,28},{24,8},{28,20},{1,17},{... | collective-permute-start | bytes 786440 | tf_op jit(solution)/shard_map/ppermute | solution.py:335
  102.9 5.1 %collective-permute-done.20.refs_2_ = bf16[2,32,2048]{2,1,0:T(8,128)(2,1)S(1)} collective-permute-done((bf16[2,32,2048]{2,1,0:T(8,128)(2,1)S(1)}, bf16[2,32,2048]{2,1,0:T(8,128)(2,1)S(1)}, u32[]{:S(2)}, u32[]{:S(2)}) %collective-permute-start.20) | collective-permute-done | bytes 262176 | tf_op jit(solution)/shard_map/ppermute | solution.py:335
  108.1 1.9 %collective-permute-start.21 = (bf16[1,32,2048]{2,1,0:T(8,128)(2,1)S(1)}, bf16[1,32,2048]{2,1,0:T(8,128)(2,1)S(1)}, u32[]{:S(2)}, u32[]{:S(2)}) collective-permute-start(bf16[1,32,2048]{2,1,0:T(8,128)(2,1)S(1)} %get-tuple-element.78), channel_id=1, source_target_pairs={{0,8},{4,20},{8,0},{12,28},{16,24},{20,4},{24,16},{28,12},{1,9},{5... | collective-permute-start | bytes 393224 | tf_op jit(solution)/shard_map/ppermute | solution.py:335
  110.1 0.3 collective-permute-start.16
  110.4 0.5 collective-permute-start.30
  110.9 2.0 %collective-permute-start.38 = (bf16[1,32,2048]{2,1,0:T(8,128)(2,1)S(1)}, bf16[1,32,2048]{2,1,0:T(8,128)(2,1)S(1)}, u32[]{:S(2)}, u32[]{:S(2)}) collective-permute-start(bf16[1,32,2048]{2,1,0:T(8,128)(2,1)S(1)} %shard_map.144), channel_id=1, source_target_pairs={{0,3},{1,2},{2,1},{3,0},{4,7},{5,6},{6,5},{7,4},{8,11},{9,10},{10,... | collective-permute-start | bytes 393224 | tf_op jit(solution)/shard_map/ppermute | solution.py:256
  112.9 0.2 collective-permute-done.21.refs_1_
  113.1 1.0 collective-permute-start.22
  114.1 1.0 collective-permute-done.16.refs_1_
  115.2 5.1 %collective-permute-done.30.refs_2_ = bf16[1,32,2048]{2,1,0:T(8,128)(2,1)S(1)} collective-permute-done((bf16[1,32,2048]{2,1,0:T(8,128)(2,1)S(1)}, bf16[1,32,2048]{2,1,0:T(8,128)(2,1)S(1)}, u32[]{:S(2)}, u32[]{:S(2)}) %collective-permute-start.30) | collective-permute-done | bytes 131104 | tf_op jit(solution)/shard_map/ppermute | solution.py:256
  120.3 1.1 collective-permute-done.22.refs_1_
  121.3 0.7 shard_map.145
  (57 shorter events, 1.6 us)
Async XLA Ops:
  1.0 7.0 %collective-permute-start.1 = (bf16[128,512]{1,0:T(8,128)(2,1)S(1)}, bf16[128,512]{1,0:T(8,128)(2,1)S(1)}, u32[]{:S(2)}, u32[]{:S(2)}) collective-permute-start(bf16[128,512]{1,0:T(8,128)(2,1)S(1)} %pad_maximum_fusion.1.refs_0_), channel_id=1, source_target_pairs={{0,8},{4,12},{8,0},{12,4},{16,24},{20,28},{24,16},{28,20},{1,9},{5... | collective-permute-start | bytes 393224 | tf_op jit(solution)/shard_map/ppermute | solution.py:253
  4.0 7.3 %collective-permute-start.2 = (bf16[128,512]{1,0:T(8,128)(2,1)S(1)}, bf16[128,512]{1,0:T(8,128)(2,1)S(1)}, u32[]{:S(2)}, u32[]{:S(2)}) collective-permute-start(bf16[128,512]{1,0:T(8,128)(2,1)S(1)} %pad_maximum_fusion.2), channel_id=1, source_target_pairs={{0,12},{4,8},{8,4},{12,0},{16,28},{20,24},{24,20},{28,16},{1,13},{... | collective-permute-start | bytes 393224 | tf_op jit(solution)/shard_map/ppermute | solution.py:253
  5.0 13.8 %collective-permute-start = (bf16[128,768]{1,0:T(8,128)(2,1)S(1)}, bf16[128,768]{1,0:T(8,128)(2,1)S(1)}, u32[]{:S(2)}, u32[]{:S(2)}) collective-permute-start(bf16[128,768]{1,0:T(8,128)(2,1)S(1)} %pad_maximum_fusion), channel_id=1, source_target_pairs={{0,4},{4,0},{8,12},{12,8},{16,20},{20,16},{24,28},{28,24},{1,5},{5... | collective-permute-start | bytes 589832 | tf_op jit(solution)/shard_map/ppermute | solution.py:253
  5.2 12.1 %collective-permute-start.3 = (bf16[128,512]{1,0:T(8,128)(2,1)S(1)}, bf16[128,512]{1,0:T(8,128)(2,1)S(1)}, u32[]{:S(2)}, u32[]{:S(2)}) collective-permute-start(bf16[128,512]{1,0:T(8,128)(2,1)S(1)} %pad_maximum_fusion.1.refs_0_), channel_id=1, source_target_pairs={{0,16},{4,20},{8,24},{12,28},{16,0},{20,4},{24,8},{28,12},{1,17},{... | collective-permute-start | bytes 393224 | tf_op jit(solution)/shard_map/ppermute | solution.py:253
  7.2 11.6 %collective-permute-start.4 = (bf16[128,512]{1,0:T(8,128)(2,1)S(1)}, bf16[128,512]{1,0:T(8,128)(2,1)S(1)}, u32[]{:S(2)}, u32[]{:S(2)}) collective-permute-start(bf16[128,512]{1,0:T(8,128)(2,1)S(1)} %pad_maximum_fusion.2), channel_id=1, source_target_pairs={{0,20},{4,16},{8,28},{12,24},{16,4},{20,0},{24,12},{28,8},{1,21},{... | collective-permute-start | bytes 393224 | tf_op jit(solution)/shard_map/ppermute | solution.py:253
  7.9 10.9 %collective-permute-start.5 = (bf16[128,512]{1,0:T(8,128)(2,1)S(1)}, bf16[128,512]{1,0:T(8,128)(2,1)S(1)}, u32[]{:S(2)}, u32[]{:S(2)}) collective-permute-start(bf16[128,512]{1,0:T(8,128)(2,1)S(1)} %pad_maximum_fusion.1.refs_0_), channel_id=1, source_target_pairs={{0,24},{4,28},{8,16},{12,20},{16,8},{20,12},{24,0},{28,4},{1,25},{... | collective-permute-start | bytes 393224 | tf_op jit(solution)/shard_map/ppermute | solution.py:253
  11.3 7.5 %collective-permute-start.6 = (bf16[128,512]{1,0:T(8,128)(2,1)S(1)}, bf16[128,512]{1,0:T(8,128)(2,1)S(1)}, u32[]{:S(2)}, u32[]{:S(2)}) collective-permute-start(bf16[128,512]{1,0:T(8,128)(2,1)S(1)} %pad_maximum_fusion.2), channel_id=1, source_target_pairs={{0,28},{4,24},{8,20},{12,16},{16,12},{20,8},{24,4},{28,0},{1,29},{... | collective-permute-start | bytes 393224 | tf_op jit(solution)/shard_map/ppermute | solution.py:253
  12.9 0.7 copy-start
  13.6 0.7 copy-start.1
  14.3 0.7 copy-start.2
  20.3 1.4 %collective-permute-start.7 = (bf16[128,256]{1,0:T(8,128)(2,1)S(1)}, bf16[128,256]{1,0:T(8,128)(2,1)S(1)}, u32[]{:S(2)}, u32[]{:S(2)}) collective-permute-start(bf16[128,256]{1,0:T(8,128)(2,1)S(1)} %get-tuple-element.51), channel_id=1, source_target_pairs={{0,4},{4,0},{8,12},{12,8},{16,20},{20,16},{24,28},{28,24},{1,5},{5... | collective-permute-start | bytes 196616 | tf_op jit(solution)/shard_map/ppermute | solution.py:253
  22.1 7.9 %collective-permute-start.8 = (bf16[32,2048]{1,0:T(8,128)(2,1)S(1)}, bf16[32,2048]{1,0:T(8,128)(2,1)S(1)}, u32[]{:S(2)}, u32[]{:S(2)}) collective-permute-start(bf16[32,2048]{1,0:T(8,128)(2,1)S(1)} %get-tuple-element.54), channel_id=1, source_target_pairs={{0,1},{1,0},{2,3},{3,2},{4,5},{5,4},{6,7},{7,6},{8,9},{9,8},{10,11... | collective-permute-start | bytes 393224 | tf_op jit(solution)/shard_map/ppermute | solution.py:256
  24.0 12.9 %collective-permute-start.9 = (bf16[32,2048]{1,0:T(8,128)(2,1)S(1)}, bf16[32,2048]{1,0:T(8,128)(2,1)S(1)}, u32[]{:S(2)}, u32[]{:S(2)}) collective-permute-start(bf16[32,2048]{1,0:T(8,128)(2,1)S(1)} %get-tuple-element.55), channel_id=1, source_target_pairs={{0,2},{1,3},{2,0},{3,1},{4,6},{5,7},{6,4},{7,5},{8,10},{9,11},{10,... | collective-permute-start | bytes 393224 | tf_op jit(solution)/shard_map/ppermute | solution.py:256
  26.5 10.3 %collective-permute-start.10 = (bf16[32,2048]{1,0:T(8,128)(2,1)S(1)}, bf16[32,2048]{1,0:T(8,128)(2,1)S(1)}, u32[]{:S(2)}, u32[]{:S(2)}) collective-permute-start(bf16[32,2048]{1,0:T(8,128)(2,1)S(1)} %get-tuple-element.56), channel_id=1, source_target_pairs={{0,3},{1,2},{2,1},{3,0},{4,7},{5,6},{6,5},{7,4},{8,11},{9,10},{10,... | collective-permute-start | bytes 393224 | tf_op jit(solution)/shard_map/ppermute | solution.py:256
  37.1 9.6 %collective-permute-start.23 = (bf16[1,32,2176]{2,1,0:T(8,128)(2,1)S(1)}, bf16[1,32,2176]{2,1,0:T(8,128)(2,1)S(1)}, u32[]{:S(2)}, u32[]{:S(2)}) collective-permute-start(bf16[1,32,2176]{2,1,0:T(8,128)(2,1)S(1)} %bitcast.11), channel_id=1, source_target_pairs={{0,2},{1,3},{2,0},{3,1},{4,6},{5,7},{6,4},{7,5},{8,10},{9,11},{10,... | collective-permute-start | bytes 417800 | tf_op jit(solution)/shard_map/ppermute | solution.py:256
  40.6 7.5 %collective-permute-start.11 = (bf16[1,32,2176]{2,1,0:T(8,128)(2,1)S(1)}, bf16[1,32,2176]{2,1,0:T(8,128)(2,1)S(1)}, u32[]{:S(2)}, u32[]{:S(2)}) collective-permute-start(bf16[1,32,2176]{2,1,0:T(8,128)(2,1)S(1)} %bitcast.12), channel_id=1, source_target_pairs={{0,8},{4,20},{8,0},{12,28},{16,24},{20,4},{24,16},{28,12},{1,9},{5... | collective-permute-start | bytes 417800 | tf_op jit(solution)/shard_map/ppermute | solution.py:335
  46.7 6.5 %collective-permute-start.24 = (bf16[1,32,2176]{2,1,0:T(8,128)(2,1)S(1)}, bf16[1,32,2176]{2,1,0:T(8,128)(2,1)S(1)}, u32[]{:S(2)}, u32[]{:S(2)}) collective-permute-start(bf16[1,32,2176]{2,1,0:T(8,128)(2,1)S(1)} %collective-permute-done.23.a_ref), channel_id=1, source_target_pairs={{0,8},{4,20},{8,0},{12,28},{16,24},{20,4},{24,16},{28,12},{1,9},{5... | collective-permute-start | bytes 417800 | tf_op jit(solution)/shard_map/ppermute | solution.py:335
  48.2 6.6 %collective-permute-start.12 = (bf16[2,32,2176]{2,1,0:T(8,128)(2,1)S(1)}, bf16[2,32,2176]{2,1,0:T(8,128)(2,1)S(1)}, u32[]{:S(2)}, u32[]{:S(2)}) collective-permute-start(bf16[2,32,2176]{2,1,0:T(8,128)(2,1)S(1)} %shard_map.122.a_ref), channel_id=1, source_target_pairs={{0,16},{4,12},{8,24},{12,4},{16,0},{20,28},{24,8},{28,20},{1,17},{... | collective-permute-start | bytes 835592 | tf_op jit(solution)/shard_map/ppermute | solution.py:335
  53.3 6.6 %collective-permute-start.25 = (bf16[2,32,2176]{2,1,0:T(8,128)(2,1)S(1)}, bf16[2,32,2176]{2,1,0:T(8,128)(2,1)S(1)}, u32[]{:S(2)}, u32[]{:S(2)}) collective-permute-start(bf16[2,32,2176]{2,1,0:T(8,128)(2,1)S(1)} %shard_map.133.a_ref), channel_id=1, source_target_pairs={{0,16},{4,12},{8,24},{12,4},{16,0},{20,28},{24,8},{28,20},{1,17},{... | collective-permute-start | bytes 835592 | tf_op jit(solution)/shard_map/ppermute | solution.py:335
  54.8 6.5 %collective-permute-start.31 = (bf16[1,32,2176]{2,1,0:T(8,128)(2,1)S(1)}, bf16[1,32,2176]{2,1,0:T(8,128)(2,1)S(1)}, u32[]{:S(2)}, u32[]{:S(2)}) collective-permute-start(bf16[1,32,2176]{2,1,0:T(8,128)(2,1)S(1)} %collective-permute-done.23.a_ref), channel_id=1, source_target_pairs={{0,1},{1,0},{2,3},{3,2},{4,5},{5,4},{6,7},{7,6},{8,9},{9,8},{10,11... | collective-permute-start | bytes 417800 | tf_op jit(solution)/shard_map/ppermute | solution.py:256
  54.9 18.3 %collective-permute-start.17 = (bf16[4,32,2176]{2,1,0:T(8,128)(2,1)S(1)}, bf16[4,32,2176]{2,1,0:T(8,128)(2,1)S(1)}, u32[]{:S(2)}, u32[]{:S(2)}) collective-permute-start(bf16[4,32,2176]{2,1,0:T(8,128)(2,1)S(1)} %shard_map.123.refs_1_), channel_id=1, source_target_pairs={{0,1},{1,0},{2,3},{3,2},{4,5},{5,4},{6,7},{7,6},{8,9},{9,8},{10,11... | collective-permute-start | bytes 1671176 | tf_op jit(solution)/shard_map/ppermute | solution.py:256
  57.0 20.3 %collective-permute-start.13 = (bf16[4,32,2176]{2,1,0:T(8,128)(2,1)S(1)}, bf16[4,32,2176]{2,1,0:T(8,128)(2,1)S(1)}, u32[]{:S(2)}, u32[]{:S(2)}) collective-permute-start(bf16[4,32,2176]{2,1,0:T(8,128)(2,1)S(1)} %shard_map.123.refs_1_), channel_id=1, source_target_pairs={{0,4},{4,0},{8,12},{12,8},{16,20},{20,16},{24,28},{28,24},{1,5},{5... | collective-permute-start | bytes 1671176 | tf_op jit(solution)/shard_map/ppermute | solution.py:253
  59.9 20.2 %collective-permute-start.26 = (bf16[4,32,2176]{2,1,0:T(8,128)(2,1)S(1)}, bf16[4,32,2176]{2,1,0:T(8,128)(2,1)S(1)}, u32[]{:S(2)}, u32[]{:S(2)}) collective-permute-start(bf16[4,32,2176]{2,1,0:T(8,128)(2,1)S(1)} %shard_map.134.refs_1_), channel_id=1, source_target_pairs={{0,4},{4,0},{8,12},{12,8},{16,20},{20,16},{24,28},{28,24},{1,5},{5... | collective-permute-start | bytes 1671176 | tf_op jit(solution)/shard_map/ppermute | solution.py:253
  61.4 5.1 %collective-permute-start.32 = (bf16[1,32,2176]{2,1,0:T(8,128)(2,1)S(1)}, bf16[1,32,2176]{2,1,0:T(8,128)(2,1)S(1)}, u32[]{:S(2)}, u32[]{:S(2)}) collective-permute-start(bf16[1,32,2176]{2,1,0:T(8,128)(2,1)S(1)} %collective-permute-done.31.a_ref), channel_id=1, source_target_pairs={{0,8},{4,20},{8,0},{12,28},{16,24},{20,4},{24,16},{28,12},{1,9},{5... | collective-permute-start | bytes 417800 | tf_op jit(solution)/shard_map/ppermute | solution.py:335
  66.4 6.6 %collective-permute-start.33 = (bf16[2,32,2176]{2,1,0:T(8,128)(2,1)S(1)}, bf16[2,32,2176]{2,1,0:T(8,128)(2,1)S(1)}, u32[]{:S(2)}, u32[]{:S(2)}) collective-permute-start(bf16[2,32,2176]{2,1,0:T(8,128)(2,1)S(1)} %shard_map.139.a_ref), channel_id=1, source_target_pairs={{0,16},{4,12},{8,24},{12,4},{16,0},{20,28},{24,8},{28,20},{1,17},{... | collective-permute-start | bytes 835592 | tf_op jit(solution)/shard_map/ppermute | solution.py:335
  73.1 10.1 %collective-permute-start.34 = (bf16[4,32,2176]{2,1,0:T(8,128)(2,1)S(1)}, bf16[4,32,2176]{2,1,0:T(8,128)(2,1)S(1)}, u32[]{:S(2)}, u32[]{:S(2)}) collective-permute-start(bf16[4,32,2176]{2,1,0:T(8,128)(2,1)S(1)} %shard_map.140.refs_1_), channel_id=1, source_target_pairs={{0,4},{4,0},{8,12},{12,8},{16,20},{20,16},{24,28},{28,24},{1,5},{5... | collective-permute-start | bytes 1671176 | tf_op jit(solution)/shard_map/ppermute | solution.py:253
  73.2 13.6 %collective-permute-start.18 = (bf16[4,32,2176]{2,1,0:T(8,128)(2,1)S(1)}, bf16[4,32,2176]{2,1,0:T(8,128)(2,1)S(1)}, u32[]{:S(2)}, u32[]{:S(2)}) collective-permute-start(bf16[4,32,2176]{2,1,0:T(8,128)(2,1)S(1)} %collective-permute-done.17.refs_1_), channel_id=1, source_target_pairs={{0,4},{4,0},{8,12},{12,8},{16,20},{20,16},{24,28},{28,24},{1,5},{5... | collective-permute-start | bytes 1671176 | tf_op jit(solution)/shard_map/ppermute | solution.py:253
  79.9 6.1 %collective-permute-start.14 = (bf16[4,32,2048]{2,1,0:T(8,128)(2,1)S(1)}, bf16[4,32,2048]{2,1,0:T(8,128)(2,1)S(1)}, u32[]{:S(2)}, u32[]{:S(2)}) collective-permute-start(bf16[4,32,2048]{2,1,0:T(8,128)(2,1)S(1)} %get-tuple-element.67), channel_id=1, source_target_pairs={{0,4},{4,0},{8,12},{12,8},{16,20},{20,16},{24,28},{28,24},{1,5},{5... | collective-permute-start | bytes 1572872 | tf_op jit(solution)/shard_map/ppermute | solution.py:253
  82.7 8.1 %collective-permute-start.27 = (bf16[4,32,2048]{2,1,0:T(8,128)(2,1)S(1)}, bf16[4,32,2048]{2,1,0:T(8,128)(2,1)S(1)}, u32[]{:S(2)}, u32[]{:S(2)}) collective-permute-start(bf16[4,32,2048]{2,1,0:T(8,128)(2,1)S(1)} %get-tuple-element.81), channel_id=1, source_target_pairs={{0,4},{4,0},{8,12},{12,8},{16,20},{20,16},{24,28},{28,24},{1,5},{5... | collective-permute-start | bytes 1572872 | tf_op jit(solution)/shard_map/ppermute | solution.py:253
  85.9 5.6 %collective-permute-start.35 = (bf16[4,32,2048]{2,1,0:T(8,128)(2,1)S(1)}, bf16[4,32,2048]{2,1,0:T(8,128)(2,1)S(1)}, u32[]{:S(2)}, u32[]{:S(2)}) collective-permute-start(bf16[4,32,2048]{2,1,0:T(8,128)(2,1)S(1)} %get-tuple-element.88), channel_id=1, source_target_pairs={{0,4},{4,0},{8,12},{12,8},{16,20},{20,16},{24,28},{28,24},{1,5},{5... | collective-permute-start | bytes 1572872 | tf_op jit(solution)/shard_map/ppermute | solution.py:253
  86.1 23.9 %collective-permute-start.15 = (bf16[2,32,2048]{2,1,0:T(8,128)(2,1)S(1)}, bf16[2,32,2048]{2,1,0:T(8,128)(2,1)S(1)}, u32[]{:S(2)}, u32[]{:S(2)}) collective-permute-start(bf16[2,32,2048]{2,1,0:T(8,128)(2,1)S(1)} %get-tuple-element.69), channel_id=1, source_target_pairs={{0,16},{4,12},{8,24},{12,4},{16,0},{20,28},{24,8},{28,20},{1,17},{... | collective-permute-start | bytes 786440 | tf_op jit(solution)/shard_map/ppermute | solution.py:335
  89.6 11.8 %collective-permute-start.19 = (bf16[4,32,2048]{2,1,0:T(8,128)(2,1)S(1)}, bf16[4,32,2048]{2,1,0:T(8,128)(2,1)S(1)}, u32[]{:S(2)}, u32[]{:S(2)}) collective-permute-start(bf16[4,32,2048]{2,1,0:T(8,128)(2,1)S(1)} %get-tuple-element.74), channel_id=1, source_target_pairs={{0,4},{4,0},{8,12},{12,8},{16,20},{20,16},{24,28},{28,24},{1,5},{5... | collective-permute-start | bytes 1572872 | tf_op jit(solution)/shard_map/ppermute | solution.py:253
  91.0 6.4 %collective-permute-start.28 = (bf16[2,32,2048]{2,1,0:T(8,128)(2,1)S(1)}, bf16[2,32,2048]{2,1,0:T(8,128)(2,1)S(1)}, u32[]{:S(2)}, u32[]{:S(2)}) collective-permute-start(bf16[2,32,2048]{2,1,0:T(8,128)(2,1)S(1)} %get-tuple-element.83), channel_id=1, source_target_pairs={{0,16},{4,12},{8,24},{12,4},{16,0},{20,28},{24,8},{28,20},{1,17},{... | collective-permute-start | bytes 786440 | tf_op jit(solution)/shard_map/ppermute | solution.py:335
  91.6 9.5 %collective-permute-start.36 = (bf16[2,32,2048]{2,1,0:T(8,128)(2,1)S(1)}, bf16[2,32,2048]{2,1,0:T(8,128)(2,1)S(1)}, u32[]{:S(2)}, u32[]{:S(2)}) collective-permute-start(bf16[2,32,2048]{2,1,0:T(8,128)(2,1)S(1)} %get-tuple-element.90), channel_id=1, source_target_pairs={{0,16},{4,12},{8,24},{12,4},{16,0},{20,28},{24,8},{28,20},{1,17},{... | collective-permute-start | bytes 786440 | tf_op jit(solution)/shard_map/ppermute | solution.py:335
  97.5 12.9 %collective-permute-start.29 = (bf16[1,32,2048]{2,1,0:T(8,128)(2,1)S(1)}, bf16[1,32,2048]{2,1,0:T(8,128)(2,1)S(1)}, u32[]{:S(2)}, u32[]{:S(2)}) collective-permute-start(bf16[1,32,2048]{2,1,0:T(8,128)(2,1)S(1)} %get-tuple-element.85), channel_id=1, source_target_pairs={{0,8},{4,20},{8,0},{12,28},{16,24},{20,4},{24,16},{28,12},{1,9},{5... | collective-permute-start | bytes 393224 | tf_op jit(solution)/shard_map/ppermute | solution.py:335
  101.2 9.7 %collective-permute-start.37 = (bf16[1,32,2048]{2,1,0:T(8,128)(2,1)S(1)}, bf16[1,32,2048]{2,1,0:T(8,128)(2,1)S(1)}, u32[]{:S(2)}, u32[]{:S(2)}) collective-permute-start(bf16[1,32,2048]{2,1,0:T(8,128)(2,1)S(1)} %get-tuple-element.92), channel_id=1, source_target_pairs={{0,8},{4,20},{8,0},{12,28},{16,24},{20,4},{24,16},{28,12},{1,9},{5... | collective-permute-start | bytes 393224 | tf_op jit(solution)/shard_map/ppermute | solution.py:335
  101.6 6.4 %collective-permute-start.20 = (bf16[2,32,2048]{2,1,0:T(8,128)(2,1)S(1)}, bf16[2,32,2048]{2,1,0:T(8,128)(2,1)S(1)}, u32[]{:S(2)}, u32[]{:S(2)}) collective-permute-start(bf16[2,32,2048]{2,1,0:T(8,128)(2,1)S(1)} %get-tuple-element.76), channel_id=1, source_target_pairs={{0,16},{4,12},{8,24},{12,4},{16,0},{20,28},{24,8},{28,20},{1,17},{... | collective-permute-start | bytes 786440 | tf_op jit(solution)/shard_map/ppermute | solution.py:335
  108.1 5.0 %collective-permute-start.21 = (bf16[1,32,2048]{2,1,0:T(8,128)(2,1)S(1)}, bf16[1,32,2048]{2,1,0:T(8,128)(2,1)S(1)}, u32[]{:S(2)}, u32[]{:S(2)}) collective-permute-start(bf16[1,32,2048]{2,1,0:T(8,128)(2,1)S(1)} %get-tuple-element.78), channel_id=1, source_target_pairs={{0,8},{4,20},{8,0},{12,28},{16,24},{20,4},{24,16},{28,12},{1,9},{5... | collective-permute-start | bytes 393224 | tf_op jit(solution)/shard_map/ppermute | solution.py:335
  110.1 5.0 %collective-permute-start.16 = (bf16[1,32,2048]{2,1,0:T(8,128)(2,1)S(1)}, bf16[1,32,2048]{2,1,0:T(8,128)(2,1)S(1)}, u32[]{:S(2)}, u32[]{:S(2)}) collective-permute-start(bf16[1,32,2048]{2,1,0:T(8,128)(2,1)S(1)} %get-tuple-element.71), channel_id=1, source_target_pairs={{0,8},{4,20},{8,0},{12,28},{16,24},{20,4},{24,16},{28,12},{1,9},{5... | collective-permute-start | bytes 393224 | tf_op jit(solution)/shard_map/ppermute | solution.py:335
  110.4 9.9 %collective-permute-start.30 = (bf16[1,32,2048]{2,1,0:T(8,128)(2,1)S(1)}, bf16[1,32,2048]{2,1,0:T(8,128)(2,1)S(1)}, u32[]{:S(2)}, u32[]{:S(2)}) collective-permute-start(bf16[1,32,2048]{2,1,0:T(8,128)(2,1)S(1)} %shard_map.138), channel_id=1, source_target_pairs={{0,2},{1,3},{2,0},{3,1},{4,6},{5,7},{6,4},{7,5},{8,10},{9,11},{10,... | collective-permute-start | bytes 393224 | tf_op jit(solution)/shard_map/ppermute | solution.py:256
  110.9 9.3 %collective-permute-start.38 = (bf16[1,32,2048]{2,1,0:T(8,128)(2,1)S(1)}, bf16[1,32,2048]{2,1,0:T(8,128)(2,1)S(1)}, u32[]{:S(2)}, u32[]{:S(2)}) collective-permute-start(bf16[1,32,2048]{2,1,0:T(8,128)(2,1)S(1)} %shard_map.144), channel_id=1, source_target_pairs={{0,3},{1,2},{2,1},{3,0},{4,7},{5,6},{6,5},{7,4},{8,11},{9,10},{10,... | collective-permute-start | bytes 393224 | tf_op jit(solution)/shard_map/ppermute | solution.py:256
  113.1 8.2 %collective-permute-start.22 = (bf16[1,32,2048]{2,1,0:T(8,128)(2,1)S(1)}, bf16[1,32,2048]{2,1,0:T(8,128)(2,1)S(1)}, u32[]{:S(2)}, u32[]{:S(2)}) collective-permute-start(bf16[1,32,2048]{2,1,0:T(8,128)(2,1)S(1)} %shard_map.132), channel_id=1, source_target_pairs={{0,1},{1,0},{2,3},{3,2},{4,5},{5,4},{6,7},{7,6},{8,9},{9,8},{10,11... | collective-permute-start | bytes 393224 | tf_op jit(solution)/shard_map/ppermute | solution.py:256
